TPU v7x, 128 devices: a whole 4x4x4 slice. The times are simulated.
128 devices in a mesh: seq: 8 (over z, y_hi), chan: 16 (over y_lo, x, core).
Axes of the slice: x: 4, y: 4 (y_hi: 2, y_lo: 2; y = y_hi * 2 + y_lo), z: 4, core: 2. Of those that a mesh axis runs over, the one named last changes fastest.
Arguments:
- tokens: bfloat16 [4096, 4096], P('seq', 'chan'), may hold values from -6 to 6
- gate_proj: bfloat16 [4096, 8192], P(None, 'chan'), may hold values from -0.09375 to 0.09375
- value_proj: bfloat16 [4096, 8192], P(None, 'chan'), may hold values from -0.09375 to 0.09375
- state_proj: bfloat16 [4096, 256], replicated, may hold values from -0.0078125 to 0.0078125
- step_proj: bfloat16 [4096, 64], P(None, 'chan'), may hold values from -0.09375 to 0.09375
- step_bias: float32 [64], P('chan'), may hold values from -1 to 1
- decay_rate: float32 [64], P('chan'), may hold values from 0.0001 to 0.05
- skip_gain: float32 [64], P('chan'), may hold values from 0.5 to 4
- conv_kernel: float32 [4, 8192], P(None, 'chan'), may hold values from -3 to 3
- norm_gain: float32 [8192], P('chan'), may hold values from 0.1 to 1.9
- out_proj: bfloat16 [8192, 4096], P('chan'), may hold values from -0.046875 to 0.046875
- complement: int32 [4096], replicated, may hold values from 0 to 4095, as said below
- keep_mask: int32 [4096, 4096], P('seq', 'chan'), may hold values 0 or 1
Outputs:
- mixed: bfloat16 [4096, 4096], P('seq', 'chan')
Inputs may be any that keep to these rules, and one draw needn't show every extreme that they name: complement pairs the features: complement[complement[j]] = j and complement[j] != j for every j.
All inputs are finite; a program needn't handle non-finite values. No bound on the sum of `keep_mask` on one device may be relied on, other than what follows from the above.
Results may differ from a plain program's by a relative error of at most 0.025.
Values may be sent and summed in bfloat16 or wider, within the bound.
No kernel may reach another device: no remote copies, remote signals or barrier semaphores. Data moves between devices by JAX's collectives and lax.ppermute only.
A program may use at most 128 MiB of HBM per device.

v0:
```python
import jax
import jax.numpy as jnp
from jax import lax
from jax.sharding import PartitionSpec as P

KW = 4
BLOCK = 256


def from_partner(block, axis, stride):
    count = lax.axis_size(axis)
    route = []
    for low in range(count):
        high = low | 1 << stride
        if high != low and high < count:
            route += [(low, high), (high, low)]
    return lax.ppermute(block, axis, route)


def from_behind(block, axis, distance):
    devices = range(lax.axis_size(axis))
    route = [(i - distance, i) for i in devices if i - distance in devices]
    return lax.ppermute(block, axis, route)


def entering_2(value, axis, join, neutral):
    place = lax.axis_index(axis)
    gathered = jax.tree.map(
        lambda a, kind: lax.all_gather(a.astype(kind), axis), value, (jnp.bfloat16, jnp.bfloat16)
    )
    state = jax.tree.map(lambda a, e: jnp.zeros_like(a) + jnp.asarray(e, a.dtype), value, neutral)

    def one(hop, state):
        return join(
            state,
            jax.tree.map(
                lambda a, own: lax.dynamic_index_in_dim(a, hop, 0, False).astype(own.dtype),
                gathered,
                value,
            ),
        )

    return lax.fori_loop(0, place, one, state)


def block_step(state, items):
    x_heads, b_part, c_part, step, log_decay = items
    cumulative = jnp.cumsum(log_decay, axis=1)
    gaps = cumulative[:, :, None, :] - cumulative[:, None, :, :]
    length = cumulative.shape[1]
    lower_mask = (jnp.arange(length)[:, None] >= jnp.arange(length)[None, :])[None, :, :, None]
    weights = jnp.where(lower_mask, jnp.exp(jnp.where(lower_mask, gaps, 0.0)), 0.0)
    x_float = x_heads.astype(jnp.float32)
    b_float = b_part.astype(jnp.float32)
    c_float = c_part.astype(jnp.float32)
    highest = lax.Precision.HIGHEST
    scores = jnp.einsum("btn,bsn->bts", c_float, b_float, precision=highest)
    mixing = weights * scores[..., None] * step[:, None, :, :]
    inner_y = jnp.einsum("btsh,bshp->bthp", mixing, x_float, precision=highest)
    carried = jnp.exp(cumulative)[..., None] * jnp.einsum(
        "btn,bhpn->bthp", c_float, state, precision=highest
    )
    total_decay = cumulative[:, -1, :]
    towards = jnp.exp(total_decay[:, None, :] - cumulative) * step
    fresh = jnp.einsum("bsh,bshp,bsn->bhpn", towards, x_float, b_float, precision=highest)
    new_state = jnp.exp(total_decay)[:, :, None, None] * state + fresh
    return (new_state, inner_y + carried)


def ssd_blocks(x_heads, b_part, c_part, step, log_decay):
    branches, length, heads, head_dim = x_heads.shape
    nblocks = length // BLOCK

    def blocked(arr):
        return jnp.moveaxis(arr.reshape((branches, nblocks, BLOCK) + arr.shape[2:]), 1, 0)

    start_state = jnp.zeros((branches, heads, head_dim, b_part.shape[-1]), jnp.float32)
    end_state, outputs = lax.scan(
        block_step,
        start_state,
        (blocked(x_heads), blocked(b_part), blocked(c_part), blocked(step), blocked(log_decay)),
    )
    return (jnp.moveaxis(outputs, 0, 1).reshape(x_heads.shape), end_state)


def combine_states(earlier, later):
    return (earlier[0] * later[0], later[0][..., None, None] * earlier[1] + later[1])


def mirror_rows(rows_block):
    nbits = lax.axis_size("seq").bit_length() - 1
    for bit_index in range(nbits):
        rows_block = from_partner(rows_block, "seq", bit_index)
    return rows_block[::-1]


def from_lower(tail):
    return from_behind(tail, "seq", 1)


def from_earlier(decays, states):
    identity = (jnp.ones_like(decays), jnp.zeros_like(states))
    return entering_2((decays, states), "seq", combine_states, identity)[1]


def shards(
    tokens,
    gate_proj,
    value_proj,
    state_proj,
    step_proj,
    step_bias,
    decay_rate,
    skip_gain,
    conv_kernel,
    norm_gain,
    out_proj,
    complement,
    keep_mask,
):
    rows = tokens.shape[0]
    inner = gate_proj.shape[1]
    heads = step_proj.shape[1]
    head_dim = inner // heads
    nstate = state_proj.shape[1] // 2
    width = gate_proj.shape[0]
    w_forward = jnp.concatenate([gate_proj, value_proj, state_proj, step_proj], axis=1)
    positions = jnp.arange(width, dtype=jnp.int32)
    inverse = jnp.zeros((width,), jnp.int32).at[complement].set(positions)
    w_reverse = jnp.take(w_forward, inverse, axis=0)
    mirrored = mirror_rows(tokens)
    first = jnp.dot(
        lax.all_gather(tokens, "chan", axis=1, tiled=True),
        w_forward,
        preferred_element_type=jnp.float32,
    )
    second = jnp.dot(
        lax.all_gather(mirrored, "chan", axis=1, tiled=True),
        w_reverse,
        preferred_element_type=jnp.float32,
    )
    proj = jnp.stack([first, second])
    gate_part = proj[..., :inner].astype(jnp.bfloat16)
    value_part = proj[..., inner : 2 * inner].astype(jnp.bfloat16)
    b_part = proj[..., 2 * inner : 2 * inner + nstate].astype(jnp.bfloat16)
    c_part = proj[..., 2 * inner + nstate : 2 * inner + 2 * nstate].astype(jnp.bfloat16)
    step_raw = proj[..., 2 * inner + 2 * nstate :]
    tail = value_part[:, rows - (KW - 1) :, :]
    before = from_lower(tail)
    padded = jnp.concatenate([before, value_part], axis=1).astype(jnp.float32)
    conv = conv_kernel[0] * padded[:, 0:rows, :]
    for tap in range(1, KW):
        conv = conv + conv_kernel[tap] * padded[:, tap : tap + rows, :]
    x_ssm = jax.nn.silu(conv).astype(jnp.bfloat16)
    step = jax.nn.softplus(step_raw + step_bias)
    log_decay = -step * decay_rate
    x_heads = x_ssm.reshape(2, rows, heads, head_dim)
    local_y, end_state = ssd_blocks(x_heads, b_part, c_part, step, log_decay)
    running = jnp.cumsum(log_decay, axis=1)
    shard_decay = jnp.exp(running[:, -1, :])
    incoming = from_earlier(shard_decay, end_state)
    entering = jnp.einsum(
        "btn,bhpn->bthp", c_part.astype(jnp.float32), incoming, precision=lax.Precision.HIGHEST
    )
    full_y = (
        local_y
        + jnp.exp(running)[..., None] * entering
        + skip_gain[:, None] * x_heads.astype(jnp.float32)
    )
    gated = full_y * jax.nn.silu(gate_part.astype(jnp.float32).reshape(2, rows, heads, head_dim))
    scale = lax.rsqrt(jnp.mean(gated * gated, axis=-1, keepdims=True) + 1e-05)
    normed = (
        (gated * scale * norm_gain.reshape(heads, head_dim))
        .reshape(2, rows, inner)
        .astype(jnp.bfloat16)
    )
    back_rows = mirror_rows(normed[1])
    stacked = jnp.concatenate([normed[0], back_rows], axis=1)
    out_table = jnp.concatenate([out_proj, jnp.take(out_proj, complement, axis=1)], axis=0)
    partial_total = jnp.dot(stacked, out_table, preferred_element_type=jnp.float32)
    summed = lax.psum_scatter(
        partial_total.astype(jnp.bfloat16), "chan", scatter_dimension=1, tiled=True
    ).astype(jnp.float32)
    return (summed * keep_mask.astype(jnp.float32) * (1.0 / 0.9)).astype(jnp.bfloat16)


def solution(mesh):
    return jax.shard_map(
        shards,
        mesh=mesh,
        in_specs=(
            P("seq", "chan"),
            P(None, "chan"),
            P(None, "chan"),
            P(),
            P(None, "chan"),
            P("chan"),
            P("chan"),
            P("chan"),
            P(None, "chan"),
            P("chan"),
            P("chan", None),
            P(),
            P("seq", "chan"),
        ),
        out_specs=P("seq", "chan"),
        check_vma=False,
    )
```

profile of v0, /device:TPU:0, one launch (start us, length us, event | category | flops | bytes accessed | tf_op | source)
XLA Modules:
  0.0 375.6 jit_solution(16991684730666367663)
XLA Ops:
  7.3 3.4 collective-permute-start
  10.7 6.5 %collective-permute-done = bf16[512,256]{1,0:T(8,128)(2,1)S(1)} collective-permute-done((bf16[512,256]{1,0:T(8,128)(2,1)}, bf16[512,256]{1,0:T(8,128)(2,1)S(1)}, u32[]{:S(2)}, u32[]{:S(2)}) %collective-permute-start) | collective-permute-done | bytes 262176 | tf_op jit(solution)/shard_map/ppermute | solution.py:17
  17.2 2.0 collective-permute-start.1
  19.1 5.4 %collective-permute-done.1 = bf16[512,256]{1,0:T(8,128)(2,1)S(1)} collective-permute-done((bf16[512,256]{1,0:T(8,128)(2,1)S(1)}, bf16[512,256]{1,0:T(8,128)(2,1)S(1)}, u32[]{:S(2)}, u32[]{:S(2)}) %collective-permute-start.1) | collective-permute-done | bytes 262176 | tf_op jit(solution)/shard_map/ppermute | solution.py:17
  24.6 3.7 collective-permute-start.2
  28.3 5.2 %collective-permute-done.2 = bf16[512,256]{1,0:T(8,128)(2,1)S(1)} collective-permute-done((bf16[512,256]{1,0:T(8,128)(2,1)S(1)}, bf16[512,256]{1,0:T(8,128)(2,1)S(1)}, u32[]{:S(2)}, u32[]{:S(2)}) %collective-permute-start.2) | collective-permute-done | bytes 262176 | tf_op jit(solution)/shard_map/ppermute | solution.py:17
  33.5 2.6 rev.6
  36.2 1.3 copy.115
  37.5 15.5 %scatter_custom_fusion = s32[4096]{0:T(1024)S(1)} fusion(s32[4096]{0:T(1024)S(1)} %get-tuple-element.161, s32[4096]{0:T(1024)S(1)} %iota.19, s32[]{:T(128)} %constant.83.clone.1), kind=kCustom, calls=%fused_computation.113 | custom fusion | bytes 16388 | tf_op jit(solution)/shard_map/scatter | solution.py:129
  53.0 9.6 %pad_maximum_fusion = bf16[4096,1284]{1,0:T(8,128)(2,1)} fusion(bf16[4096,4]{1,0:T(8,128)(2,1)S(1)} %copy.115, bf16[4096,256]{1,0:T(8,128)(2,1)} %param.20, bf16[4096,512]{1,0:T(8,128)(2,1)} %param.19, bf16[4096,512]{1,0:T(8,128)(2,1)} %param.18), kind=kLoop, calls=%fused_computation.56 | loop fusion | flops 42074112 | bytes 21037056 | tf_op jit(solution)/shard_map/concatenate | solution.py:127
  62.7 29.6 %gather_fusion = bf16[4096,1284]{1,0:T(8,128)(2,1)} fusion(bf16[4096,1284]{1,0:T(8,128)(2,1)} %pad_maximum_fusion, s32[4096]{0:T(1024)S(1)} %fusion.73), kind=kCustom, calls=%fused_computation | custom fusion | bytes 21053440 | tf_op jit(solution)/shard_map/jit(_take)/gather | solution.py:130
  92.3 12.5 %convolution_bitcast_fusion = f32[1,512,1284]{1,2,0:T(8,128)} fusion(bf16[4096,1284]{1,0:T(8,128)(2,1)} %pad_maximum_fusion, bf16[512,4096]{1,0:T(8,128)(2,1)} %all-gather.6.cloned.1.call-done), kind=kOutput, calls=%fused_computation.72 | convolution fusion | flops 5385486336 | bytes 17342464 | tf_op jit(solution)/shard_map/dot_general | solution.py:132
  104.8 12.7 %fusion.56 = f32[1,512,1284]{1,2,0:T(8,128)S(1)} fusion(bf16[512,4096]{1,0:T(8,128)(2,1)} %all-gather.8.cloned.1.call-done, bf16[4096,1284]{1,0:T(8,128)(2,1)} %gather_fusion, pred[4096]{0:T(1024)(128)(4,1)S(1)} %compare_and_fusion.1), kind=kOutput, calls=%fused_computation.71 | convolution fusion | flops 5390745600 | bytes 17346560 | tf_op jit(solution)/shard_map/dot_general | solution.py:137
  118.0 1.6 fusion.82
  120.2 5.1 %collective-permute-start.3 = (bf16[2,3,512]{1,2,0:T(8,128)(2,1)S(1)}, bf16[2,3,512]{1,2,0:T(8,128)(2,1)S(1)}, u32[]{:S(2)}, u32[]{:S(2)}) collective-permute-start(bf16[2,3,512]{1,2,0:T(8,128)(2,1)S(1)} %slice.104), channel_id=1, source_target_pairs={{0,16},{16,32},{32,48},{48,64},{64,80},{80,96},{96,112},{1,17},{17... | collective-permute-start | bytes 18440 | tf_op jit(solution)/shard_map/ppermute | solution.py:23
  126.7 2.5 collective-permute-done.3
  130.0 1.8 maximum_convert_fusion
  131.8 3.1 multiply_convert_fusion.1
  134.9 2.1 reshape_reshape.3
  137.0 2.4 copy.139
  139.4 24.1 %while.26 = (s32[]{:T(128)}, f32[2,4,128,128]{3,2,1,0:T(8,128)S(1)}, f32[2,2,256,4,128]{2,4,3,1,0:T(8,128)}, f32[2,2,256,4]{2,3,1,0:T(4,128)S(1)}, f32[2,2,256,4...) while((s32[]{:T(128)}, ...), condition=%wide.region_4.5_spmd.clone, body=%wide.region_1.4_spmd.clone.sunk | while | flops 1648693248 | bytes 11834916 | solution.py:78
  139.4 2.4 reduce-window.26
  142.5 1.1 fusion.108
  143.7 3.9 %fusion.109 = f32[2,256,4,128]{1,3,2,0:T(8,128)} fusion(f32[2,256,4]{1,2,0:T(4,128)S(1)} %get-tuple-element.254, f32[2,256,256]{2,1,0:T(8,128)S(1)} %fusion.108, f32[2,256,4]{1,2,0:T(4,128)S(1)} %bitcast.142, pred[256,256]{1,0:T(8,128)(4,1)S(1)} %iota_compare_fusion.2, bf16[2,2,256,4,128]{2,4,3,1,0:T(8,128)(2,1)} %get-tuple-element.283, ...), kind=kOutput, calls=%fused_computation.12.clone.1 | convolution fusion | flops 807927808 | bytes 2187776 | tf_op jit(solution)/shard_map/while/body/eval_jaxpr/btsh,bshp->bthp/dot_general | solution.py:59
  147.6 2.9 fusion.110
  151.5 2.4 reduce-window.26
  154.6 1.1 fusion.108
  155.8 3.9 %fusion.109 = f32[2,256,4,128]{1,3,2,0:T(8,128)} fusion(f32[2,256,4]{1,2,0:T(4,128)S(1)} %get-tuple-element.254, f32[2,256,256]{2,1,0:T(8,128)S(1)} %fusion.108, f32[2,256,4]{1,2,0:T(4,128)S(1)} %bitcast.142, pred[256,256]{1,0:T(8,128)(4,1)S(1)} %iota_compare_fusion.2, bf16[2,2,256,4,128]{2,4,3,1,0:T(8,128)(2,1)} %get-tuple-element.283, ...), kind=kOutput, calls=%fused_computation.12.clone.1 | convolution fusion | flops 807927808 | bytes 2187776 | tf_op jit(solution)/shard_map/while/body/eval_jaxpr/btsh,bshp->bthp/dot_general | solution.py:59
  159.7 2.9 fusion.110
  162.6 0.9 convolution_add_fusion.2
  164.4 2.4 reduce-window.16
  167.7 24.8 %all-gather = bf16[16,1,4]{2,1,0:T(2,128)(2,1)S(1)} all-gather(bf16[2,1,4]{2,1,0:T(2,128)(2,1)S(1)} %copy.122), channel_id=2, replica_groups=mesh['seq'=8,'chan'=16] {'seq'}, dimensions={0}, use_global_device_ids=true | all-gather | bytes 144 | tf_op jit(solution)/shard_map/all_gather | solution.py:29
  192.5 3.2 copy.135
  195.7 25.5 %all-gather.10.cloned.1.call-done = bf16[16,4,128,128]{3,2,1,0:T(8,128)(2,1)} async-done(((bf16[2,4,128,128]{3,2,1,0:T(8,128)(2,1)}), bf16[16,4,128,128]{3,2,1,0:T(8,128)(2,1)}) %all-gather.10.cloned.1.call-update) | async-done | bytes 2097168 | tf_op jit(solution)/shard_map/all_gather | solution.py:29
  221.3 2.1 fusion.70
  223.4 3.4 multiply_reduce_fusion
  227.2 1.8 collective-permute-start.4
  229.0 13.1 %collective-permute-done.4 = bf16[512,512]{0,1:T(8,128)(2,1)S(1)} collective-permute-done((bf16[512,512]{0,1:T(8,128)(2,1)S(1)}, bf16[512,512]{0,1:T(8,128)(2,1)S(1)}, u32[]{:S(2)}, u32[]{:S(2)}) %collective-permute-start.4) | collective-permute-done | bytes 524320 | tf_op jit(solution)/shard_map/ppermute | solution.py:17
  242.1 2.5 collective-permute-start.5
  244.6 6.5 %copy.125 = bf16[512,4096]{0,1:T(8,128)(2,1)} copy(bf16[512,4096]{1,0:T(8,128)(2,1)} %param.27) | data formatting | bytes 8388608 | tf_op args[10]
  251.0 20.2 %gather_fusion.1 = bf16[4096,512]{1,0:T(8,128)(2,1)} fusion(bf16[512,4096]{0,1:T(8,128)(2,1)} %copy.125, s32[4096]{0:T(1024)S(1)} %get-tuple-element.162), kind=kCustom, calls=%fused_computation.1 | custom fusion | bytes 8404992 | tf_op jit(solution)/shard_map/jit(_take)/gather | solution.py:179
  271.2 6.8 %collective-permute-start.6 = (bf16[512,512]{0,1:T(8,128)(2,1)S(1)}, bf16[512,512]{0,1:T(8,128)(2,1)S(1)}, u32[]{:S(2)}, u32[]{:S(2)}) collective-permute-start(bf16[512,512]{0,1:T(8,128)(2,1)S(1)} %collective-permute-done.5), channel_id=1, source_target_pairs={{0,64},{64,0},{16,80},{80,16},{32,96},{96,32},{48,112},{112,48},{1... | collective-permute-start | bytes 1572872 | tf_op jit(solution)/shard_map/ppermute | solution.py:17
  278.0 3.9 %select_bitcast_fusion = bf16[512,4096]{0,1:T(8,128)(2,1)} fusion(bf16[4096,512]{1,0:T(8,128)(2,1)} %gather_fusion.1, pred[4096]{0:T(1024)(128)(4,1)S(1)} %compare_and_fusion), kind=kLoop, calls=%fused_computation.70 | loop fusion | flops 2097152 | bytes 8392704 | tf_op jit(solution)/shard_map/jit(_take)/select_n | solution.py:179
  281.9 6.0 %collective-permute-done.6 = bf16[512,512]{0,1:T(8,128)(2,1)S(1)} collective-permute-done((bf16[512,512]{0,1:T(8,128)(2,1)S(1)}, bf16[512,512]{0,1:T(8,128)(2,1)S(1)}, u32[]{:S(2)}, u32[]{:S(2)}) %collective-permute-start.6) | collective-permute-done | bytes 524320 | tf_op jit(solution)/shard_map/ppermute | solution.py:17
  287.9 1.6 rev.7
  289.6 10.0 %fusion.51 = bf16[512,4096]{1,0:T(8,128)(2,1)} fusion(bf16[512,4096]{0,1:T(8,128)(2,1)} %select_bitcast_fusion, bf16[512,4096]{0,1:T(8,128)(2,1)} %copy.125, bf16[512,512]{0,1:T(8,128)(2,1)S(1)} %rev.7, bf16[512,512]{0,1:T(8,128)(2,1)S(1)} %bitcast.144), kind=kOutput, calls=%fused_computation.67 | convolution fusion | flops 4315938816 | bytes 13631488 | tf_op jit(solution)/shard_map/dot_general | solution.py:180
  299.6 67.7 %reduce-scatter.2.cloned.1.call-done = bf16[512,256]{1,0:T(8,128)(2,1)} async-done(((bf16[512,4096]{1,0:T(8,128)(2,1)}), bf16[512,256]{1,0:T(8,128)(2,1)}) %reduce-scatter.2.cloned.1.call-update) | async-done | bytes 262160 | tf_op jit(solution)/shard_map/reduce_scatter | solution.py:181
  367.3 1.7 multiply_convert_fusion.2
  (96 shorter events, 8.5 us)
Async XLA Ops:
  6.5 30.9 %copy-start.6 = (s32[4096]{0:T(1024)S(1)}, s32[4096]{0:T(1024)}, u32[]{:S(2)}) copy-start(s32[4096]{0:T(1024)} %param.28) | copy-start | bytes 49156
  6.5 85.8 %all-gather.6.cloned.1.call-start = ((), (), s32[]{:S(2)}) async-start(), calls=%async_computation.1 | async-start | bytes 4456448 | tf_op jit(solution)/shard_map/all_gather | solution.py:133
  7.3 97.6 %all-gather.8.cloned.1.call-start = ((), (), s32[]{:S(2)}) async-start(), calls=%async_computation.2 | async-start | bytes 4456448 | tf_op jit(solution)/shard_map/all_gather | solution.py:138
  7.3 9.9 %collective-permute-start = (bf16[512,256]{1,0:T(8,128)(2,1)}, bf16[512,256]{1,0:T(8,128)(2,1)S(1)}, u32[]{:S(2)}, u32[]{:S(2)}) collective-permute-start(bf16[512,256]{1,0:T(8,128)(2,1)} %param.17), channel_id=1, source_target_pairs={{0,16},{16,0},{32,48},{48,32},{64,80},{80,64},{96,112},{112,96},{1... | collective-permute-start | bytes 786440 | tf_op jit(solution)/shard_map/ppermute | solution.py:17
  17.2 7.4 %collective-permute-start.1 = (bf16[512,256]{1,0:T(8,128)(2,1)S(1)}, bf16[512,256]{1,0:T(8,128)(2,1)S(1)}, u32[]{:S(2)}, u32[]{:S(2)}) collective-permute-start(bf16[512,256]{1,0:T(8,128)(2,1)S(1)} %collective-permute-done), channel_id=1, source_target_pairs={{0,32},{32,0},{16,48},{48,16},{64,96},{96,64},{80,112},{112,80},{1... | collective-permute-start | bytes 786440 | tf_op jit(solution)/shard_map/ppermute | solution.py:17
  24.6 8.9 %collective-permute-start.2 = (bf16[512,256]{1,0:T(8,128)(2,1)S(1)}, bf16[512,256]{1,0:T(8,128)(2,1)S(1)}, u32[]{:S(2)}, u32[]{:S(2)}) collective-permute-start(bf16[512,256]{1,0:T(8,128)(2,1)S(1)} %collective-permute-done.1), channel_id=1, source_target_pairs={{0,64},{64,0},{16,80},{80,16},{32,96},{96,32},{48,112},{112,48},{1... | collective-permute-start | bytes 786440 | tf_op jit(solution)/shard_map/ppermute | solution.py:17
  36.1 185.1 %all-gather.10.cloned.1.call-start = ((), (), s32[]{:S(2)}) async-start(), calls=%async_computation.4 | async-start | bytes 2359296 | tf_op jit(solution)/shard_map/all_gather | solution.py:29
  62.7 29.6 %copy-start.7 = (f32[4,512]{1,0:T(4,128)S(1)}, f32[4,512]{1,0:T(4,128)}, u32[]{:S(2)}) copy-start(f32[4,512]{1,0:T(4,128)} %param.25) | copy-start | bytes 24580
  104.8 12.7 %copy-start.2 = (f32[1,512,1284]{1,2,0:T(8,128)S(1)}, f32[1,512,1284]{1,2,0:T(8,128)}, u32[]{:S(2)}) copy-start(f32[1,512,1284]{1,2,0:T(8,128)} %convolution_bitcast_fusion) | copy-start | bytes 7888900
  118.0 2.2 copy-start.1
  118.0 7.3 %copy-start.9 = (f32[4]{0:T(128)S(1)}, f32[4]{0:T(128)}, u32[]{:S(2)}) copy-start(f32[4]{0:T(128)} %param.23) | copy-start | bytes 52
  118.0 7.3 %copy-start.10 = (f32[4]{0:T(128)S(1)}, f32[4]{0:T(128)}, u32[]{:S(2)}) copy-start(f32[4]{0:T(128)} %param.22) | copy-start | bytes 52
  120.2 9.0 %collective-permute-start.3 = (bf16[2,3,512]{1,2,0:T(8,128)(2,1)S(1)}, bf16[2,3,512]{1,2,0:T(8,128)(2,1)S(1)}, u32[]{:S(2)}, u32[]{:S(2)}) collective-permute-start(bf16[2,3,512]{1,2,0:T(8,128)(2,1)S(1)} %slice.104), channel_id=1, source_target_pairs={{0,16},{16,32},{32,48},{48,64},{64,80},{80,96},{96,112},{1,17},{17... | collective-permute-start | bytes 18440 | tf_op jit(solution)/shard_map/ppermute | solution.py:23
  129.3 0.7 copy-start.5
  147.6 3.0 copy-start
  159.7 2.9 copy-start
  164.3 203.0 %reduce-scatter.2.cloned.1.call-start = ((), (), s32[]{:S(2)}) async-start(), calls=%async_computation.3 | async-start | bytes 4456448 | tf_op jit(solution)/shard_map/reduce_scatter | solution.py:181
  221.3 2.1 copy-start.3
  221.3 2.1 copy-start.11
  223.4 3.5 copy-start.8
  227.2 14.8 %collective-permute-start.4 = (bf16[512,512]{0,1:T(8,128)(2,1)S(1)}, bf16[512,512]{0,1:T(8,128)(2,1)S(1)}, u32[]{:S(2)}, u32[]{:S(2)}) collective-permute-start(bf16[512,512]{0,1:T(8,128)(2,1)S(1)} %bitcast.145), channel_id=1, source_target_pairs={{0,16},{16,0},{32,48},{48,32},{64,80},{80,64},{96,112},{112,96},{1... | collective-permute-start | bytes 1572872 | tf_op jit(solution)/shard_map/ppermute | solution.py:17
  242.1 29.1 %collective-permute-start.5 = (bf16[512,512]{0,1:T(8,128)(2,1)S(1)}, bf16[512,512]{0,1:T(8,128)(2,1)S(1)}, u32[]{:S(2)}, u32[]{:S(2)}) collective-permute-start(bf16[512,512]{0,1:T(8,128)(2,1)S(1)} %collective-permute-done.4), channel_id=1, source_target_pairs={{0,32},{32,0},{16,48},{48,16},{64,96},{96,64},{80,112},{112,80},{1... | collective-permute-start | bytes 1572872 | tf_op jit(solution)/shard_map/ppermute | solution.py:17
  271.2 16.7 %collective-permute-start.6 = (bf16[512,512]{0,1:T(8,128)(2,1)S(1)}, bf16[512,512]{0,1:T(8,128)(2,1)S(1)}, u32[]{:S(2)}, u32[]{:S(2)}) collective-permute-start(bf16[512,512]{0,1:T(8,128)(2,1)S(1)} %collective-permute-done.5), channel_id=1, source_target_pairs={{0,64},{64,0},{16,80},{80,16},{32,96},{96,32},{48,112},{112,48},{1... | collective-permute-start | bytes 1572872 | tf_op jit(solution)/shard_map/ppermute | solution.py:17
  299.6 67.7 %copy-start.4 = (s32[512,256]{1,0:T(8,128)S(1)}, s32[512,256]{1,0:T(8,128)}, u32[]{:S(2)}) copy-start(s32[512,256]{1,0:T(8,128)} %param.29) | copy-start | bytes 1572868
Sparse Core Ops, SparseCore 0:
  9.0 47.3 all-gather.5
  58.0 45.1 all-gather.7
  164.4 56.7 all-gather.9
  299.7 67.5 reduce-scatter.1
where the time goes:
time: 377 us; the launch traced here: 376 us
  waiting for transfers between devices  133 us (35%)
  local copies, waits for them, and re-layouts  90.6 us (24%)
  matrix products  54.9 us (15%)
  other arithmetic  33.6 us (9%)
  starting transfers between devices  25.2 us (7%)
  blocking collectives  24.8 us (7%)
  between operations  13.5 us (4%)
    reduce_scatter x1, waiting for transfers between devices, shards(): lax.psum_scatter(partial_total.astype(jnp.bfloat16), 'chan', scatter_dime...  67.7 us
    ppermute x6, waiting for transfers between devices, from_partner(): return lax.ppermute(block, axis, route)  36.3 us
    gather x1, local copies, waits for them, and re-layouts, shards(): w_reverse = jnp.take(w_forward, inverse, axis=0)  29.6 us
    all_gather x1, waiting for transfers between devices, entering_2(): lax.all_gather(a.astype(kind), axis)  25.5 us
    all_gather x1, blocking collectives, entering_2(): lax.all_gather(a.astype(kind), axis)  24.8 us
    gather x1, local copies, waits for them, and re-layouts, shards(): jnp.take(out_proj, complement, axis=1)  20.2 us
    ppermute x6, starting transfers between devices, from_partner(): return lax.ppermute(block, axis, route)  20 us
    scatter x1, local copies, waits for them, and re-layouts, shards(): inverse = jnp.zeros((width,), jnp.int32).at[complement].set(positions)  15.5 us
  transfers between devices with their start and end apart: 11, of which 8 were waited for; matrix products, arithmetic and copies ran while one was open for 29% of the time, Pallas kernels for 0%

commit v1 on v0

v1 whole, which is shorter than its diff:
```python
import jax
import jax.numpy as jnp
from jax import lax
from jax.experimental import pallas as pl
from jax.experimental.pallas import tpu as pltpu
from jax.sharding import PartitionSpec as P

BF = jnp.bfloat16
F32 = jnp.float32
KW = 4
VMEM_LIMIT = 48 * 2**20


def chip_route(dy, dx):
    return [
        ((y * 4 + x) * 2 + c, ((y + dy) % 2 * 4 + (x + dx) % 4) * 2 + c)
        for y in range(2)
        for x in range(4)
        for c in range(2)
    ]


def to_chip(a, dy, dx):
    return lax.ppermute(a, "chan", chip_route(dy, dx))


def to_sibling(a):
    return lax.ppermute(a, "chan", [(i, i ^ 1) for i in range(16)])


def dot(a, b, dims=((1,), (0,)), precision=None):
    return lax.dot_general(
        a, b, (dims, ((), ())), preferred_element_type=F32, precision=precision
    )


def params():
    return pltpu.CompilerParams(vmem_limit_bytes=VMEM_LIMIT)


def cost(flops, nbytes):
    return pl.CostEstimate(flops=int(flops), bytes_accessed=int(nbytes), transcendentals=0)


def gather_stage(blocks, chans, comp, before, gate_proj, value_proj, small_proj):
    nb = len(blocks)
    rows, width = blocks[0].shape
    d = comp.shape[1]
    tile = 512
    ntiles = d // tile
    ws = small_proj.shape[1]
    first = before is None

    def kernel(chan, *refs):
        tok = refs[:nb]
        comp_ref, gate_hbm, value_hbm, small_hbm = refs[nb : nb + 4]
        pos = nb + 4
        if not first:
            tp_in, av_in, ag_in, as_in = refs[pos : pos + 4]
            pos += 4
        tp_out, av, ag, asm = refs[pos : pos + 4]
        wg, wv, wsm, sem = refs[pos + 4 :]
        n = pl.program_id(0)

        def copies():
            out = []
            for j in range(nb):
                src = pl.ds(pl.multiple_of(chan[j] * width, width), width)
                dst = pl.ds(j * width, width)
                out.append(pltpu.make_async_copy(gate_hbm.at[src, :], wg.at[dst, :], sem.at[0, j]))
                out.append(pltpu.make_async_copy(value_hbm.at[src, :], wv.at[dst, :], sem.at[1, j]))
                out.append(pltpu.make_async_copy(small_hbm.at[src, :], wsm.at[dst, :], sem.at[2, j]))
            return out

        @pl.when(n == 0)
        def _():
            for c in copies():
                c.start()

        @pl.when(n < ntiles)
        def _():
            target = comp_ref[...]
            total = None
            for j in range(nb):
                local = target - chan[j] * width
                pick = lax.broadcasted_iota(jnp.int32, (width, tile), 0) == local
                part = dot(tok[j][...], jnp.where(pick, 1.0, 0.0).astype(BF))
                total = part if total is None else total + part
            if not first:
                total = total + tp_in[...].astype(F32)
            tp_out[...] = total.astype(BF)

        @pl.when(n == ntiles)
        def _():
            for c in copies():
                c.wait()
            x = jnp.concatenate([tok[j][...] for j in range(nb)], axis=1)
            if first:
                av[...] = dot(x, wv[...])
                ag[...] = dot(x, wg[...])
                asm[...] = dot(x, wsm[...])
            else:
                av[...] = dot(x, wv[...]) + av_in[...]
                ag[...] = dot(x, wg[...]) + ag_in[...]
                asm[...] = dot(x, wsm[...]) + as_in[...]

    inner = gate_proj.shape[1]
    whole = lambda shape: pl.BlockSpec(shape, lambda n, s: (0,) * len(shape))
    tp_spec = pl.BlockSpec((rows, tile), lambda n, s: (0, jnp.minimum(n, ntiles - 1)))
    any_spec = pl.BlockSpec(memory_space=pl.ANY)
    acc_specs = [tp_spec, whole((rows, inner)), whole((rows, inner)), whole((rows, ws))]
    shapes = [
        jax.ShapeDtypeStruct((rows, d), BF),
        jax.ShapeDtypeStruct((rows, inner), F32),
        jax.ShapeDtypeStruct((rows, inner), F32),
        jax.ShapeDtypeStruct((rows, ws), F32),
    ]
    args = [chans, *blocks, comp, gate_proj, value_proj, small_proj]
    in_specs = [whole((rows, width))] * nb
    in_specs += [pl.BlockSpec((1, tile), lambda n, s: (0, jnp.minimum(n, ntiles - 1)))]
    in_specs += [any_spec] * 3
    aliases = {}
    if not first:
        aliases = {len(args) + i: i for i in range(4)}
        args += before
        in_specs += acc_specs
    return pl.pallas_call(
        kernel,
        grid_spec=pltpu.PrefetchScalarGridSpec(
            num_scalar_prefetch=1,
            grid=(ntiles + 1,),
            in_specs=in_specs,
            out_specs=acc_specs,
            scratch_shapes=[
                pltpu.VMEM((nb * width, inner), BF),
                pltpu.VMEM((nb * width, inner), BF),
                pltpu.VMEM((nb * width, ws), BF),
                pltpu.SemaphoreType.DMA((3, nb)),
            ],
        ),
        out_shape=shapes,
        input_output_aliases=aliases,
        compiler_params=params(),
        cost_estimate=cost(2 * rows * nb * width * (d + 2 * inner + ws), 8 * 2**20),
        name="gather_stage",
    )(*args)


def reverse_small(tp, value_proj, small_proj, acc_value, acc_small):
    rows, d = tp.shape
    inner, ws = value_proj.shape[1], small_proj.shape[1]
    kb = 512

    def kernel(t, wv, wsm, av, asm, v_out, bc_out, st_out, accv, accs):
        i = pl.program_id(0)

        @pl.when(i == 0)
        def _():
            accv[...] = jnp.zeros_like(accv)
            accs[...] = jnp.zeros_like(accs)

        accv[...] += dot(t[...], wv[...])
        accs[...] += dot(t[...], wsm[...])

        @pl.when(i == d // kb - 1)
        def _():
            v_out[0] = av[...].astype(BF)
            v_out[1] = accv[...].astype(BF)
            bc_out[0] = asm[:, :256].astype(BF)
            bc_out[1] = accs[:, :256].astype(BF)
            st_out[0] = asm[:, 256:]
            st_out[1] = accs[:, 256:]

    whole = lambda shape: pl.BlockSpec(shape, lambda i: (0,) * len(shape))
    return pl.pallas_call(
        kernel,
        grid=(d // kb,),
        in_specs=[
            pl.BlockSpec((rows, kb), lambda i: (0, i)),
            pl.BlockSpec((kb, inner), lambda i: (i, 0)),
            pl.BlockSpec((kb, ws), lambda i: (i, 0)),
            whole((rows, inner)),
            whole((rows, ws)),
        ],
        out_specs=[whole((2, rows, inner)), whole((2, rows, 256)), whole((2, rows, 128))],
        out_shape=[
            jax.ShapeDtypeStruct((2, rows, inner), BF),
            jax.ShapeDtypeStruct((2, rows, 256), BF),
            jax.ShapeDtypeStruct((2, rows, 128), F32),
        ],
        scratch_shapes=[pltpu.VMEM((rows, inner), F32), pltpu.VMEM((rows, ws), F32)],
        compiler_params=params(),
        cost_estimate=cost(2 * rows * d * (inner + ws), 12 * 2**20),
        name="reverse_small",
    )(tp, value_proj, small_proj, acc_value, acc_small)


def reverse_gate(tp, gate_proj, acc_gate):
    rows, d = tp.shape
    inner = gate_proj.shape[1]
    kb = 512

    def kernel(t, wg, ag, g_out, acc):
        i = pl.program_id(0)

        @pl.when(i == 0)
        def _():
            acc[...] = jnp.zeros_like(acc)
            g_out[0] = ag[...].astype(BF)

        acc[...] += dot(t[...], wg[...])

        @pl.when(i == d // kb - 1)
        def _():
            g_out[1] = acc[...].astype(BF)

    whole = lambda shape: pl.BlockSpec(shape, lambda i: (0,) * len(shape))
    return pl.pallas_call(
        kernel,
        grid=(d // kb,),
        in_specs=[
            pl.BlockSpec((rows, kb), lambda i: (0, i)),
            pl.BlockSpec((kb, inner), lambda i: (i, 0)),
            whole((rows, inner)),
        ],
        out_specs=whole((2, rows, inner)),
        out_shape=jax.ShapeDtypeStruct((2, rows, inner), BF),
        scratch_shapes=[pltpu.VMEM((rows, inner), F32)],
        compiler_params=params(),
        cost_estimate=cost(2 * rows * d * inner, 10 * 2**20),
        name="reverse_gate",
    )(tp, gate_proj, acc_gate)


def steps(raw, bias, rate):
    _, rows, lanes = raw.shape

    def kernel(raw_ref, bias_ref, rate_ref, step_o, cum_o, step_t, cum_t, decay_o):
        r = lax.broadcasted_iota(jnp.int32, (rows, rows), 0)
        c = lax.broadcasted_iota(jnp.int32, (rows, rows), 1)
        for b in range(2):
            step = jax.nn.softplus(raw_ref[b] + bias_ref[...])
            logdec = -step * rate_ref[...]
            tri = jnp.where((r >= c) if b == 0 else (r <= c), 1.0, 0.0)
            cum = dot(tri, logdec, precision=lax.Precision.HIGHEST)
            step_o[b] = step
            cum_o[b] = cum
            step_t[b] = step.T[:8]
            cum_t[b] = cum.T[:8]
            last = cum[rows - 1 : rows] if b == 0 else cum[0:1]
            decay_o[b : b + 1] = jnp.exp(last)

    vm = pl.BlockSpec(memory_space=pltpu.VMEM)
    return pl.pallas_call(
        kernel,
        in_specs=[vm] * 3,
        out_specs=[vm] * 5,
        out_shape=[
            jax.ShapeDtypeStruct((2, rows, lanes), F32),
            jax.ShapeDtypeStruct((2, rows, lanes), F32),
            jax.ShapeDtypeStruct((2, 8, rows), F32),
            jax.ShapeDtypeStruct((2, 8, rows), F32),
            jax.ShapeDtypeStruct((2, lanes), F32),
        ],
        compiler_params=params(),
        cost_estimate=cost(10**9, 2**20),
        name="steps",
    )(raw, bias, rate)


def conv_states(value, halo, taps, bc, step, cum):
    _, rows, inner = value.shape
    heads = inner // 128

    def kernel(v_ref, halo_ref, taps_ref, bc_ref, step_ref, cum_ref, xs_o, end_o):
        def branch(b):
            v = v_ref[0].astype(F32)
            hal = halo_ref[0].astype(F32)
            if b == 0:
                padded = jnp.concatenate([hal, v], axis=0)
                shift = lambda k: padded[5 + k : 5 + k + rows]
            else:
                padded = jnp.concatenate([v, hal], axis=0)
                shift = lambda k: padded[3 - k : 3 - k + rows]
            conv = taps_ref[0:1] * shift(0)
            for k in range(1, KW):
                conv = conv + taps_ref[k : k + 1] * shift(k)
            xs = (conv * jax.nn.sigmoid(conv)).astype(BF)
            xs_o[0] = xs
            cums = cum_ref[0]
            last = cums[rows - 1 : rows] if b == 0 else cums[0:1]
            towards = jnp.exp(last - cums) * step_ref[0]
            bm = bc_ref[0].astype(F32)
            for h in range(heads):
                weighted = (bm * towards[:, h : h + 1]).astype(BF)
                end_o[0, h] = dot(weighted, xs[:, h * 128 : h * 128 + 128], ((0,), (0,)))

        for b in range(2):
            pl.when(pl.program_id(0) == b)(lambda b=b: branch(b))

    by = lambda *shape: pl.BlockSpec((1, *shape), lambda b: (b,) + (0,) * len(shape))
    return pl.pallas_call(
        kernel,
        grid=(2,),
        in_specs=[
            by(rows, inner),
            by(8, inner),
            pl.BlockSpec(taps.shape, lambda b: (0, 0)),
            by(rows, 128),
            by(rows, 128),
            by(rows, 128),
        ],
        out_specs=[by(rows, inner), by(heads, 128, 128)],
        out_shape=[
            jax.ShapeDtypeStruct((2, rows, inner), BF),
            jax.ShapeDtypeStruct((2, heads, 128, 128), F32),
        ],
        compiler_params=params(),
        cost_estimate=cost(10**9, 3 * 2**20),
        name="conv_states",
    )(value, halo, taps, bc, step, cum)


def within_shard(xs, bc, step_t, cum_t, cum, skip):
    _, rows, inner = xs.shape
    heads = inner // 128
    half = rows // 2

    def kernel(x_ref, bc_ref, st_ref, ct_ref, cum_ref, skip_ref, y_ref):
        h = pl.program_id(1)
        lane = lax.broadcasted_iota(jnp.int32, (1, 128), 1)
        pick = lane == h
        cum_col = jnp.sum(jnp.where(pick, cum_ref[0], 0.0), axis=1, keepdims=True)
        gain = jnp.sum(jnp.where(pick, skip_ref[...], 0.0), axis=1, keepdims=True)
        cum_row = ct_ref[0, pl.ds(h, 1), :]
        step_row = st_ref[0, pl.ds(h, 1), :]
        lower = lax.broadcasted_iota(jnp.int32, (half, half), 0) >= lax.broadcasted_iota(
            jnp.int32, (half, half), 1
        )
        upper = lax.broadcasted_iota(jnp.int32, (half, half), 0) <= lax.broadcasted_iota(
            jnp.int32, (half, half), 1
        )

        def part(t, s, mask):
            ts, ss = slice(t * half, t * half + half), slice(s * half, s * half + half)
            gap = jnp.minimum(cum_col[ts] - cum_row[:, ss], 0.0)
            w = jnp.exp(gap)
            if mask is not None:
                w = jnp.where(mask, w, 0.0)
            scores = dot(bc_ref[0, ts, 128:], bc_ref[0, ss, :128], ((1,), (1,)))
            mixing = (w * scores * step_row[:, ss]).astype(BF)
            return dot(mixing, x_ref[0, ss, :])

        def branch(b):
            early, late = (0, 1) if b == 0 else (1, 0)
            mask = lower if b == 0 else upper
            for t, y in (
                (early, part(early, early, mask)),
                (late, part(late, late, mask) + part(late, early, None)),
            ):
                ts = slice(t * half, t * half + half)
                y_ref[0, ts, :] = y + gain * x_ref[0, ts, :].astype(F32)

        for b in range(2):
            pl.when(pl.program_id(0) == b)(lambda b=b: branch(b))

    by = lambda *shape: pl.BlockSpec((1, *shape), lambda b, h: (b,) + (0,) * len(shape))
    head = pl.BlockSpec((1, rows, 128), lambda b, h: (b, 0, h))
    return pl.pallas_call(
        kernel,
        grid=(2, heads),
        in_specs=[
            head,
            by(rows, 256),
            by(8, rows),
            by(8, rows),
            by(rows, 128),
            pl.BlockSpec((1, 128), lambda b, h: (0, 0)),
        ],
        out_specs=head,
        out_shape=jax.ShapeDtypeStruct((2, rows, inner), F32),
        compiler_params=params(),
        cost_estimate=cost(4 * 10**9, 4 * 2**20),
        name="within_shard",
    )(xs, bc, step_t, cum_t, cum, skip)


def finish(local_y, incoming, bc, cum, gate, norm_gain):
    _, rows, inner = local_y.shape
    heads = inner // 128

    def kernel(y_ref, s_ref, bc_ref, cum_ref, g_ref, gain_ref, o_ref):
        h = pl.program_id(1)
        lane = lax.broadcasted_iota(jnp.int32, (1, 128), 1)
        cum_col = jnp.sum(jnp.where(lane == h, cum_ref[0], 0.0), axis=1, keepdims=True)
        entering = dot(bc_ref[0], s_ref[0, 0])
        y = y_ref[0] + jnp.exp(cum_col) * entering
        g = g_ref[0].astype(F32)
        gated = y * (g * jax.nn.sigmoid(g))
        scale = lax.rsqrt(jnp.mean(gated * gated, axis=-1, keepdims=True) + 1e-05)
        o_ref[...] = (gated * scale * gain_ref[...]).astype(BF)

    by = lambda *shape: pl.BlockSpec((1, *shape), lambda b, h: (b,) + (0,) * len(shape))
    head = pl.BlockSpec((1, rows, 128), lambda b, h: (b, 0, h))
    return pl.pallas_call(
        kernel,
        grid=(2, heads),
        in_specs=[
            head,
            pl.BlockSpec((1, 1, 128, 128), lambda b, h: (b, h, 0, 0)),
            pl.BlockSpec((1, rows, 128), lambda b, h: (b, 0, 1)),
            by(rows, 128),
            head,
            pl.BlockSpec((1, 128), lambda b, h: (0, h)),
        ],
        out_specs=pl.BlockSpec((rows, 128), lambda b, h: (0, b * heads + h)),
        out_shape=jax.ShapeDtypeStruct((rows, 2 * inner), BF),
        compiler_params=params(),
        cost_estimate=cost(10**9, 5 * 2**20),
        name="finish",
    )(local_y, incoming, bc, cum, gate, norm_gain)


def output_table(comp, out_proj):
    inner, d = out_proj.shape
    r = 512
    nb = d // r
    tiles = inner // 128

    def kernel(idx, o_ref, plain_o, perm_o, rows_f32, picked):
        i = pl.program_id(0)

        @pl.when(i < nb)
        def _():
            r0 = pl.multiple_of(i * r * tiles, r * tiles)
            for j in range(tiles):
                t = o_ref[128 * j : 128 * j + 128, :].astype(F32).T
                rows_f32[pl.ds(r0 + j, r, tiles), :] = t
                plain_o[:, 128 * j : 128 * j + 128] = t.astype(BF)

        @pl.when(i >= nb)
        def _():
            b0 = (i - nb) * r

            def body(n, _):
                for k in range(16):
                    row = n * 16 + k
                    src = pl.multiple_of(idx[b0 + row] * tiles, tiles)
                    dst = pl.multiple_of(row * tiles, tiles)
                    picked[pl.ds(dst, tiles), :] = rows_f32[pl.ds(src, tiles), :]
                return 0

            lax.fori_loop(0, r // 16, body, 0)
            for j in range(tiles):
                perm_o[:, 128 * j : 128 * j + 128] = picked[pl.ds(j, r, tiles), :].astype(BF)

    return pl.pallas_call(
        kernel,
        grid_spec=pltpu.PrefetchScalarGridSpec(
            num_scalar_prefetch=1,
            grid=(2 * nb,),
            in_specs=[pl.BlockSpec((inner, r), lambda i, s: (0, jnp.minimum(i, nb - 1)))],
            out_specs=[
                pl.BlockSpec((r, inner), lambda i, s: (jnp.minimum(i, nb - 1), 0)),
                pl.BlockSpec((r, inner), lambda i, s: (jnp.maximum(i - nb, 0), 0)),
            ],
            scratch_shapes=[
                pltpu.VMEM((d * tiles, 128), F32),
                pltpu.VMEM((r * tiles, 128), F32),
            ],
        ),
        out_shape=[jax.ShapeDtypeStruct((d, inner), BF)] * 2,
        compiler_params=params(),
        cost_estimate=cost(8 * 10**9, 12 * 2**20),
        name="output_table",
    )(comp, out_proj)


def output_stage(order, mine, others, plain, perm, plain_sib, perm_sib):
    rows, twice = mine.shape
    inner = twice // 2
    n = order.shape[0] // 2
    cols = 256

    def kernel(idx, a, b, p0, q0, p1, q1, o_ref):
        nt = ((1,), (1,))
        o_ref[0] = (
            dot(a[:, :inner], p0[...], nt)
            + dot(a[:, inner:], q0[...], nt)
            + dot(b[:, :inner], p1[...], nt)
            + dot(b[:, inner:], q1[...], nt)
        )

    own = pl.BlockSpec((cols, inner), lambda i, s: (s[2 * i], 0))
    sib = pl.BlockSpec((cols, inner), lambda i, s: (s[2 * i + 1], 0))
    whole = pl.BlockSpec((rows, twice), lambda i, s: (0, 0))
    return pl.pallas_call(
        kernel,
        grid_spec=pltpu.PrefetchScalarGridSpec(
            num_scalar_prefetch=1,
            grid=(n,),
            in_specs=[whole, whole, own, own, sib, sib],
            out_specs=pl.BlockSpec((1, rows, cols), lambda i, s: (i, 0, 0)),
        ),
        out_shape=jax.ShapeDtypeStruct((n, rows, cols), F32),
        compiler_params=params(),
        cost_estimate=cost(n * 4 * rows * twice * cols, n * 2 * 2**20),
        name="output_stage",
    )(order, mine, others, plain, perm, plain_sib, perm_sib)


def split(a):
    high = a.astype(BF)
    return high, (a - high.astype(F32)).astype(BF)


def join(high, low):
    return high.astype(F32) + low.astype(F32)


def halo_exchange(value, decay):
    rows = value.shape[1]
    fh, fl = split(decay)
    tail = jnp.stack([fh[0], fl[0], fh[1], fl[1]])
    tail = jnp.pad(tail, ((0, 1), (0, value.shape[2] - 128)))
    down = jnp.concatenate([value[0, rows - 3 :], tail], axis=0)
    up = jnp.concatenate([value[1, :3], tail], axis=0)
    from_below = lax.ppermute(down, "seq", [(i, i + 1) for i in range(7)])
    from_above = lax.ppermute(up, "seq", [(i + 1, i) for i in range(7)])
    return from_below, from_above


def shards(
    tokens,
    gate_proj,
    value_proj,
    state_proj,
    step_proj,
    step_bias,
    decay_rate,
    skip_gain,
    conv_kernel,
    norm_gain,
    out_proj,
    complement,
    keep_mask,
):
    rows, width = tokens.shape
    inner = gate_proj.shape[1]
    heads = step_proj.shape[1]
    d = gate_proj.shape[0]
    place = lax.axis_index("chan")
    core, chip = place % 2, place // 2
    y, x = chip // 4, chip % 4
    seq = lax.axis_index("seq")
    z, half = seq // 2, seq % 2

    def chip_at(dy, dx):
        return (y + dy) % 2 * 4 + (x + dx) % 4

    def lanes(a):
        return jnp.pad(a, (0, 128 - heads)).reshape(1, 128)

    comp = complement.reshape(1, d)
    small_proj = jnp.concatenate(
        [state_proj, step_proj, jnp.zeros((d, 128 - heads), BF)], axis=1
    )

    weights = (gate_proj, value_proj, small_proj)

    def stage(parts, before):
        blocks, chans = [], []
        for block, sib, dy, dx in parts:
            blocks += [block, sib]
            chans += [2 * chip_at(dy, dx) + core, 2 * chip_at(dy, dx) + 1 - core]
        return gather_stage(
            blocks, jnp.stack(chans).astype(jnp.int32), comp, before, *weights
        )

    own = tokens
    a = to_chip(own, 0, 1)
    b = to_chip(own, 0, -1)
    c = to_chip(own, 1, 0)
    own_s = to_sibling(own)
    acc = stage([(own, own_s, 0, 0)], None)
    a_s, b_s, c_s = to_sibling(a), to_sibling(b), to_sibling(c)
    dd = to_chip(a, 1, 0)
    e = to_chip(c, 0, -1)
    f = to_chip(a, 0, 1)
    acc = stage([(a, a_s, 0, -1), (b, b_s, 0, 1), (c, c_s, 1, 0)], acc)
    third = (168, 336)
    g = jnp.concatenate(
        [
            to_chip(dd[: third[0]], 0, 1),
            to_chip(e[third[0] : third[1]], 0, -1),
            to_chip(f[third[1] :], 1, 0),
        ]
    )
    d_s, e_s, f_s = to_sibling(dd), to_sibling(e), to_sibling(f)
    acc = stage([(dd, d_s, 1, -1), (e, e_s, 1, 1), (f, f_s, 0, 2)], acc)
    g_s = to_sibling(g)
    tp, acc_v, acc_g, acc_s = stage([(g, g_s, 1, 2)], acc)

    value, bc, raw = reverse_small(tp, value_proj, small_proj, acc_v, acc_s)
    step, cum, step_t, cum_t, decay = steps(raw, lanes(step_bias), lanes(decay_rate))
    below, above = halo_exchange(value, decay)
    zeros5 = jnp.zeros((5, inner), BF)
    halo = jnp.stack(
        [
            jnp.concatenate([zeros5, below[:3]], axis=0),
            jnp.concatenate([above[:3], zeros5], axis=0),
        ]
    )
    pair_msg = jnp.where(half == 0, above[3:7, :128], below[3:7, :128])
    pair = jnp.stack([join(pair_msg[0], pair_msg[1]), join(pair_msg[2], pair_msg[3])])
    xs, end = conv_states(value, halo, conv_kernel, bc, step, cum)

    d0 = jnp.where(half == 0, decay, pair)[:, :heads]
    d1 = jnp.where(half == 0, pair, decay)[:, :heads]

    def message(branch):
        parts = [*split(d0[branch]), *split(d1[branch])]
        rows4 = jnp.stack([jnp.pad(v, (0, 128 - heads)) for v in parts])
        rows4 = jnp.pad(rows4, ((0, 12), (0, 0)))
        return jnp.concatenate([end[branch].astype(BF).reshape(heads * 128, 128), rows4])

    msg_f, msg_b = message(0), message(1)
    got = []
    for k in range(1, 4):
        route = [(zz * 2 + hh, (zz + k) % 4 * 2 + hh) for zz in range(4) for hh in range(2)]
        got.append(lax.ppermute(jnp.where(z + k < 4, msg_f, msg_b), "seq", route))

    def opened(m):
        st = m[: heads * 128].astype(F32).reshape(heads, 128, 128)
        t = m[heads * 128 : heads * 128 + 4, :heads]
        return st, join(t[0], t[1]), join(t[2], t[3])

    opened_msgs = [opened(m) for m in got]
    wide = lambda v: v[:, None, None]

    def partial_sum(branch):
        total = jnp.zeros((heads, 128, 128), F32)
        passed = jnp.ones((heads,), F32)
        for j in range(1, 4):
            st, e0, e1 = opened_msgs[j - 1] if branch == 0 else opened_msgs[3 - j]
            valid = (z >= j) if branch == 0 else (z + j < 4)
            own_step = jnp.where(half == 0, e1, 1.0) if branch == 0 else jnp.where(half == 1, e0, 1.0)
            total = total + jnp.where(valid, wide(passed * own_step) * st, 0.0)
            passed = jnp.where(valid, passed * e0 * e1, passed)
        return total

    pf, pb = partial_sum(0), partial_sum(1)
    d0f, d1b = wide(d0[0]), wide(d1[1])
    send_f = jnp.where(half == 0, d0f * pf + end[0], pf)
    send_b = jnp.where(half == 1, d1b * pb + end[1], pb)
    recv = lax.ppermute(
        jnp.stack([send_f, send_b]).astype(BF), "seq", [(i, i ^ 1) for i in range(8)]
    ).astype(F32)
    in_f = jnp.where(half == 0, pf, d0f * pf) + recv[0]
    in_b = jnp.where(half == 1, pb, d1b * pb) + recv[1]
    incoming = jnp.stack([in_f, in_b]).astype(BF)

    gate = reverse_gate(tp, gate_proj, acc_g)
    local_y = within_shard(xs, bc, step_t, cum_t, cum, lanes(skip_gain))
    plain, perm = output_table(complement, out_proj)
    for_sib = lambda t: lax.dynamic_index_in_dim(
        t.reshape(8, 2, 256, inner), 1 - core, 1, False
    ).reshape(8 * 256, inner)
    plain_sib, perm_sib = to_sibling(for_sib(plain)), to_sibling(for_sib(perm))

    normed = finish(local_y, incoming, bc, cum, gate, norm_gain.reshape(1, inner))
    others = to_sibling(normed)

    def shares(*offsets):
        order = []
        for dy, dx in offsets:
            order += [2 * chip_at(dy, dx) + core, chip_at(dy, dx)]
        order = jnp.stack(order).astype(jnp.int32)
        return output_stage(order, normed, others, plain, perm, plain_sib, perm_sib)

    far = shares((1, 2))[0].astype(BF)
    r_a = to_chip(far[: third[0]], 0, 1)
    r_b = to_chip(far[third[0] : third[1]], 0, -1)
    r_c = to_chip(far[third[1] :], 1, 0)
    mid = shares((1, 1), (1, -1), (0, 2))
    m_a = mid[0].at[: third[0]].add(r_a.astype(F32)).astype(BF)
    m_b = mid[1].at[third[0] : third[1]].add(r_b.astype(F32)).astype(BF)
    m_c = mid[2].at[third[1] :].add(r_c.astype(F32)).astype(BF)
    s_a = to_chip(m_a, 1, 0)
    s_b = to_chip(m_b, 0, -1)
    s_c = to_chip(m_c, 0, 1)
    near = shares((0, 1), (0, -1), (1, 0), (0, 0))
    n_a = (near[0] + s_a.astype(F32) + s_c.astype(F32)).astype(BF)
    n_b = near[1].astype(BF)
    n_c = (near[2] + s_b.astype(F32)).astype(BF)
    t_a = to_chip(n_a, 0, 1).astype(F32)
    t_b = to_chip(n_b, 0, -1).astype(F32)
    t_c = to_chip(n_c, 1, 0).astype(F32)
    summed = near[3] + t_a + t_b + t_c
    return (summed * keep_mask.astype(F32) * (1.0 / 0.9)).astype(BF)


def solution(mesh):
    return jax.shard_map(
        shards,
        mesh=mesh,
        in_specs=(
            P("seq", "chan"),
            P(None, "chan"),
            P(None, "chan"),
            P(),
            P(None, "chan"),
            P("chan"),
            P("chan"),
            P("chan"),
            P(None, "chan"),
            P("chan"),
            P("chan", None),
            P(),
            P("seq", "chan"),
        ),
        out_specs=P("seq", "chan"),
        check_vma=False,
    )
```

time: 377 us -> 190 us (0.50)
  waiting for transfers between devices: 133 us -> 25.3 us
  Pallas kernels: 0 us -> 107 us
  local copies, waits for them, and re-layouts: 90.6 us -> 9.13 us
  matrix products: 54.9 us -> 0 us
  other arithmetic: 33.6 us -> 5.18 us
  blocking collectives: 24.8 us -> 0 us
  starting transfers between devices: 25.2 us -> 41.1 us
  between operations: 13.5 us -> 0.68 us
    pallas_call x0 -> x14, Pallas kernels: none -> 107 us  [the longest x4 47.2 us: gather_stage(): pl.pallas_call(kernel, grid_spec=pltpu.PrefetchScalarGridSpec(num_scalar_...]
    reduce_scatter x1 -> x0, waiting for transfers between devices: 67.7 us -> none  [shards(): lax.psum_scatter(partial_total.astype(jnp.bfloat16), 'chan', scatter_dime...]
    dot_general x12 -> x0, matrix products: 54.9 us -> none  [the longest x1 12.7 us: shards(): jnp.dot(lax.all_gather(mirrored, 'chan', axis=1, tiled=True), w_reverse,...]
    gather x2 -> x0, local copies, waits for them, and re-layouts: 49.8 us -> none  [the longest x1 29.6 us: shards(): w_reverse = jnp.take(w_forward, inverse, axis=0)]
    all_gather x3 -> x0, waiting for transfers between devices: 25.6 us -> none  [the longest x1 25.5 us: entering_2(): lax.all_gather(a.astype(kind), axis)]
    all_gather x1 -> x0, blocking collectives: 24.8 us -> none  [entering_2(): lax.all_gather(a.astype(kind), axis)]
    ppermute x7 -> x35, starting transfers between devices: 25.1 us -> 41.1 us  [the longest x18 21.7 us: to_chip(): return lax.ppermute(a, 'chan', chip_route(dy, dx))]
    scatter x1 -> x0, local copies, waits for them, and re-layouts: 15.5 us -> none  [shards(): inverse = jnp.zeros((width,), jnp.int32).at[complement].set(positions)]
  transfers between devices with their start and end apart: 11 -> 35, of which waited for: 8 -> 8; matrix products, arithmetic and copies ran while one was open for 29% -> 7% of each run, Pallas kernels for 0% -> 55%
where the time goes in v1:
time: 190 us; the launch traced here: 188 us
  Pallas kernels  107 us (56%)
  starting transfers between devices  41.1 us (22%)
  waiting for transfers between devices  25.3 us (13%)
  local copies, waits for them, and re-layouts  9.13 us (5%)
  other arithmetic  5.18 us (3%)
    pallas_call x4, Pallas kernels, gather_stage(): pl.pallas_call(kernel, grid_spec=pltpu.PrefetchScalarGridSpec(num_scalar_...  47.2 us
    ppermute x18, starting transfers between devices, to_chip(): return lax.ppermute(a, 'chan', chip_route(dy, dx))  21.7 us
    ppermute x18, waiting for transfers between devices, to_chip(): return lax.ppermute(a, 'chan', chip_route(dy, dx))  17.7 us
    pallas_call x1, Pallas kernels, output_table(): pl.pallas_call(kernel, grid_spec=pltpu.PrefetchScalarGridSpec(num_scalar_...  15.1 us
    pallas_call x3, Pallas kernels, output_stage(): pl.pallas_call(kernel, grid_spec=pltpu.PrefetchScalarGridSpec(num_scalar_...  13.3 us
    pallas_call x1, Pallas kernels, reverse_small(): pl.pallas_call(kernel, grid=(d // kb,), in_specs=[pl.BlockSpec((rows, kb)...  9.55 us
    ppermute x3, starting transfers between devices, shards(): got.append(lax.ppermute(jnp.where(z + k < 4, msg_f, msg_b), 'seq', route))  8.73 us
    pallas_call x1, Pallas kernels, reverse_gate(): pl.pallas_call(kernel, grid=(d // kb,), in_specs=[pl.BlockSpec((rows, kb)...  7.46 us
  transfers between devices with their start and end apart: 35, of which 8 were waited for; matrix products, arithmetic and copies ran while one was open for 7% of the time, Pallas kernels for 55%

profile of v1, /device:TPU:0, one launch (start us, length us, event | category | flops | bytes accessed | tf_op | source)
XLA Modules:
  0.0 188.3 jit_solution(3713284297390847008)
XLA Ops:
  0.0 1.6 collective-permute-start
  1.6 1.6 collective-permute-start.3
  3.2 1.7 collective-permute-start.13
  4.9 1.3 copy.26
  6.2 0.7 pad_bitcast_fusion.9.skip_ref
  6.9 0.7 pad_bitcast_fusion.10
  7.6 0.7 copy-done.3
  8.3 15.1 %output_table.1 = (bf16[4096,512]{1,0:T(8,128)(2,1)S(1)}, bf16[4096,512]{1,0:T(8,128)(2,1)}) custom-call(s32[4096]{0:T(1024)S(1)} %copy-done.3, bf16[512,4096]{1,0:T(8,128)(2,1)} %o_ref.1), custom_call_target="tpu_custom_call" | custom-call | flops 8000000000 | bytes 12582912 | tf_op jit(solution)/shard_map/output_table/pallas_call | solution.py:457
  23.5 2.7 %maximum_maximum_fusion.refs_5_.refs_9_.wsm = bf16[4096,384]{1,0:T(8,128)(2,1)} fusion(bf16[4096,4]{1,0:T(8,128)(2,1)S(1)} %copy.26, bf16[4096,256]{1,0:T(8,128)(2,1)S(1)} %copy-done.8, bf16[384]{0:T(512)(128)(2,1)S(1)} %pad.102.clone), kind=kLoop, calls=%fused_computation | loop fusion | flops 9437184 | bytes 5276416 | tf_op jit(solution)/shard_map/concatenate | solution.py:565
  26.7 3.2 %constant_dynamic-slice_fusion.1 = bf16[8,1,256,512]{3,2,1,0:T(8,128)(2,1)} fusion(bf16[8,2,256,512]{3,2,1,0:T(8,128)(2,1)} %bitcast.192, s32[]{:T(128)S(6)} %select_n.559), kind=kLoop, calls=%fused_computation.109 | loop fusion | bytes 4194308 | tf_op jit(solution)/shard_map/jit(dynamic_index_in_dim)/dynamic_slice | solution.py:666
  30.5 1.4 constant_dynamic-slice_fusion
  32.5 2.9 %collective-permute-start.4 = (bf16[512,256]{1,0:T(8,128)(2,1)S(1)}, bf16[512,256]{1,0:T(8,128)(2,1)S(1)}, u32[]{:S(2)}, u32[]{:S(2)}) collective-permute-start(bf16[512,256]{1,0:T(8,128)(2,1)S(1)} %collective-permute-done.3.refs_4_), channel_id=1, source_target_pairs={{0,6},{1,7},{2,0},{3,1},{4,2},{5,3},{6,4},{7,5},{8,14},{9,15},{10,... | collective-permute-start | bytes 786440 | tf_op jit(solution)/shard_map/ppermute | solution.py:24
  35.4 2.5 %collective-permute-done.1.refs_0_ = bf16[512,256]{1,0:T(8,128)(2,1)S(1)} collective-permute-done((bf16[512,256]{1,0:T(8,128)(2,1)S(1)}, bf16[512,256]{1,0:T(8,128)(2,1)S(1)}, u32[]{:S(2)}, u32[]{:S(2)}) %collective-permute-start.1) | collective-permute-done | bytes 262176 | tf_op jit(solution)/shard_map/ppermute | solution.py:24
  37.9 7.6 %gather_stage.4 = (bf16[512,4096]{1,0:T(8,128)(2,1)}, f32[512,512]{1,0:T(8,128)S(1)}, f32[512,512]{1,0:T(8,128)S(1)}, f32[512,384]{1,0:T(8,128)S(1)}) custom-call(s32[2]{0:T(128)S(1)} %pad_add_fusion.1.chan, bf16[512,256]{1,0:T(8,128)(2,1)S(1)} %copy-done.2, bf16[512,256]{1,0:T(8,128)(2,1)S(1)} %collective-permute-done.16.refs_1_, s32[1,4096]{1,0:T(1,128)S(1)} %bitcast.193, ...), custom_call_target="tpu_custom_call" | custom-call | flops 2885681152 | bytes 8388608 | tf_op jit(solution)/shard_map/gather_stage/pallas_call | solution.py:127
  45.6 0.6 collective-permute-start.24
  46.5 3.0 %collective-permute-start.5 = (bf16[168,256]{1,0:T(8,128)(2,1)S(1)}, bf16[168,256]{1,0:T(8,128)(2,1)S(1)}, u32[]{:S(2)}, u32[]{:S(2)}) collective-permute-start(bf16[168,256]{1,0:T(8,128)(2,1)S(1)} %slice.300), channel_id=1, source_target_pairs={{0,6},{1,7},{2,0},{3,1},{4,2},{5,3},{6,4},{7,5},{8,14},{9,15},{10,... | collective-permute-start | bytes 258056 | tf_op jit(solution)/shard_map/ppermute | solution.py:24
  49.5 0.5 collective-permute-start.11
  50.0 14.7 %gather_stage.5 = (bf16[512,4096]{1,0:T(8,128)(2,1)}, f32[512,512]{1,0:T(8,128)S(1)}, f32[512,512]{1,0:T(8,128)S(1)}, f32[512,384]{1,0:T(8,128)S(1)}) custom-call(s32[6]{0:T(128)S(1)} %stack.182.chan, bf16[512,256]{1,0:T(8,128)(2,1)S(1)} %collective-permute-done.refs_0_, ...), custom_call_target="tpu_custom_call", output_to_operand_aliasing={{0}: (11, {}), {1}: (12, {}), {2}: (13, {}), {3}: (14, {})} | custom-call | flops 8657043456 | bytes 8388608 | tf_op jit(solution)/shard_map/gather_stage/pallas_call | solution.py:127
  64.9 0.4 collective-permute-start.7
  65.4 4.6 %collective-permute-done.7 = bf16[176,256]{1,0:T(8,128)(2,1)S(1)} collective-permute-done((bf16[176,256]{1,0:T(8,128)(2,1)S(1)}, bf16[176,256]{1,0:T(8,128)(2,1)S(1)}, u32[]{:S(2)}, u32[]{:S(2)}) %collective-permute-start.7) | collective-permute-done | bytes 90144 | tf_op jit(solution)/shard_map/ppermute | solution.py:24
  70.0 0.8 collective-permute-start.8
  70.8 14.7 %gather_stage.6 = (bf16[512,4096]{1,0:T(8,128)(2,1)}, f32[512,512]{1,0:T(8,128)S(1)}, f32[512,512]{1,0:T(8,128)S(1)}, f32[512,384]{1,0:T(8,128)S(1)}) custom-call(s32[6]{0:T(128)S(1)} %stack.178.chan, bf16[512,256]{1,0:T(8,128)(2,1)S(1)} %collective-permute-done.1.refs_0_, ...), custom_call_target="tpu_custom_call", output_to_operand_aliasing={{0}: (11, {}), {1}: (12, {}), {2}: (13, {}), {3}: (14, {})} | custom-call | flops 8657043456 | bytes 8388608 | tf_op jit(solution)/shard_map/gather_stage/pallas_call | solution.py:127
  85.5 10.1 %gather_stage.7 = (bf16[512,4096]{1,0:T(8,128)(2,1)}, f32[512,512]{1,0:T(8,128)S(1)}, f32[512,512]{1,0:T(8,128)S(1)}, f32[512,384]{1,0:T(8,128)S(1)}) custom-call(s32[2]{0:T(128)S(1)} %pad_add_fusion.chan, bf16[512,256]{1,0:T(8,128)(2,1)S(1)} %constant_dynamic-update-slice_fusion.refs_0_, ...), custom_call_target="tpu_custom_call", output_to_operand_aliasing={{0}: (7, {}), {1}: (8, {}), {2}: (9, {}), {3}: (10, {})} | custom-call | flops 2885681152 | bytes 8388608 | tf_op jit(solution)/shard_map/gather_stage/pallas_call | solution.py:127
  95.6 9.6 %reverse_small.1 = (bf16[2,512,512]{2,1,0:T(8,128)(2,1)S(1)}, bf16[2,512,256]{2,1,0:T(8,128)(2,1)S(1)}, f32[2,512,128]{2,1,0:T(8,128)S(1)}) custom-call(bf16[512,4096]{1,0:T(8,128)(2,1)} %get-tuple-element.81.t, bf16[4096,512]{1,0:T(8,128)(2,1)} %wv.1, bf16[4096,384]{1,0:T(8,128)(2,1)} %maximum_maximum_fusion.refs_5_.refs_9_.wsm, ...), custom_call_target="tpu_custom_call" | custom-call | flops 3758096384 | bytes 12582912 | tf_op jit(solution)/shard_map/reverse_small/pallas_call | solution.py:175
  105.2 2.0 %steps.1 = (f32[2,512,128]{2,1,0:T(8,128)S(1)}, f32[2,512,128]{2,1,0:T(8,128)S(1)}, f32[2,8,512]{2,1,0:T(8,128)S(1)}, f32[2,8,512]{2,1,0:T(8,128)S(1)}, f32[2,128]{1,0:T(2,128)S(1)}) custom-call(f32[2,512,128]{2,1,0:T(8,128)S(1)} %get-tuple-element.85.raw_ref, f32[1,128]{1,0:T(1,128)S(1)} %get-tuple-element.139.bias_ref, ...), custom_call_target="tpu_custom_call" | custom-call | flops 1000000000 | bytes 1048576 | tf_op jit(solution)/shard_map/steps/pallas_call | solution.py:254
  107.3 4.8 %collective-permute-start.17 = (bf16[8,512]{1,0:T(8,128)(2,1)S(1)}, bf16[8,512]{1,0:T(8,128)(2,1)S(1)}, u32[]{:S(2)}, u32[]{:S(2)}) collective-permute-start(bf16[8,512]{1,0:T(8,128)(2,1)S(1)} %get-tuple-element.120), channel_id=1, source_target_pairs={{0,16},{16,32},{32,48},{48,64},{64,80},{80,96},{96,112},{1,17},{17... | collective-permute-start | bytes 24584 | tf_op jit(solution)/shard_map/ppermute | solution.py:528
  112.1 1.3 collective-permute-start.18
  113.5 7.5 %reverse_gate.1.g_ref = bf16[2,512,512]{2,1,0:T(8,128)(2,1)S(1)} custom-call(bf16[512,4096]{1,0:T(8,128)(2,1)} %get-tuple-element.81.t, bf16[4096,512]{1,0:T(8,128)(2,1)} %wg.1, f32[512,512]{1,0:T(8,128)S(1)} %get-tuple-element.94.ag), custom_call_target="tpu_custom_call" | custom-call | flops 2147483648 | bytes 10485760 | tf_op jit(solution)/shard_map/reverse_gate/pallas_call | solution.py:218
  121.3 2.9 %conv_states.1 = (bf16[2,512,512]{2,1,0:T(8,128)(2,1)S(1)}, f32[2,4,128,128]{3,2,1,0:T(8,128)S(1)}) custom-call(bf16[2,512,512]{2,1,0:T(8,128)(2,1)S(1)} %get-tuple-element.84.v_ref, bf16[2,8,512]{2,1,0:T(8,128)(2,1)S(1)} %pad_maximum_fusion.4.halo_ref, f32[4,512]{1,0:T(4,128)S(1)} %copy-done.6, bf16[2,512,256]{2,1,0:T(8,128)(2,1)S(1)} %get-tuple-element.87.bc_ref, ...), custom_call_target="tpu_custom_call" | custom-call | flops 1000000000 | bytes 3145728 | tf_op jit(solution)/shard_map/conv_states/pallas_call | solution.py:302
  124.3 4.1 %collective-permute-start.19 = (bf16[528,128]{1,0:T(8,128)(2,1)S(1)}, bf16[528,128]{1,0:T(8,128)(2,1)S(1)}, u32[]{:S(2)}, u32[]{:S(2)}) collective-permute-start(bf16[528,128]{1,0:T(8,128)(2,1)S(1)} %get-tuple-element.117), channel_id=1, source_target_pairs={{0,32},{16,48},{32,64},{48,80},{64,96},{80,112},{96,0},{112,16},{1... | collective-permute-start | bytes 405512 | tf_op jit(solution)/shard_map/ppermute | solution.py:631
  128.5 3.6 %collective-permute-start.20 = (bf16[528,128]{1,0:T(8,128)(2,1)S(1)}, bf16[528,128]{1,0:T(8,128)(2,1)S(1)}, u32[]{:S(2)}, u32[]{:S(2)}) collective-permute-start(bf16[528,128]{1,0:T(8,128)(2,1)S(1)} %get-tuple-element.116), channel_id=1, source_target_pairs={{0,64},{16,80},{32,96},{48,112},{64,0},{80,16},{96,32},{112,48},{1... | collective-permute-start | bytes 405512 | tf_op jit(solution)/shard_map/ppermute | solution.py:631
  132.0 1.0 collective-permute-start.21
  133.1 4.8 %collective-permute-done.20 = bf16[528,128]{1,0:T(8,128)(2,1)S(1)} collective-permute-done((bf16[528,128]{1,0:T(8,128)(2,1)S(1)}, bf16[528,128]{1,0:T(8,128)(2,1)S(1)}, u32[]{:S(2)}, u32[]{:S(2)}) %collective-permute-start.20) | collective-permute-done | bytes 135200 | tf_op jit(solution)/shard_map/ppermute | solution.py:631
  138.5 2.3 %collective-permute-start.22 = (bf16[2,4,128,128]{3,2,1,0:T(8,128)(2,1)S(1)}, bf16[2,4,128,128]{3,2,1,0:T(8,128)(2,1)S(1)}, u32[]{:S(2)}, u32[]{:S(2)}) collective-permute-start(bf16[2,4,128,128]{3,2,1,0:T(8,128)(2,1)S(1)} %pad_maximum_fusion), channel_id=1, source_target_pairs={{0,16},{16,0},{32,48},{48,32},{64,80},{80,64},{96,112},{112,96},{1... | collective-permute-start | bytes 786440 | tf_op jit(solution)/shard_map/ppermute | solution.py:656
  140.8 5.8 %within_shard.1.y_ref = f32[2,512,512]{2,1,0:T(8,128)S(1)} custom-call(bf16[2,512,512]{2,1,0:T(8,128)(2,1)S(1)} %get-tuple-element.90.x_ref, bf16[2,512,256]{2,1,0:T(8,128)(2,1)S(1)} %get-tuple-element.87.bc_ref, f32[2,8,512]{2,1,0:T(8,128)S(1)} %get-tuple-element.91.st_ref, f32[2,8,512]{2,1,0:T(8,128)S(1)} %get-tuple-element.92.ct_ref, ...), custom_call_target="tpu_custom_call" | custom-call | flops 4000000000 | bytes 4194304 | tf_op jit(solution)/shard_map/within_shard/pallas_call | solution.py:369
  147.4 3.4 %finish.1.a = bf16[512,1024]{1,0:T(8,128)(2,1)S(1)} custom-call(f32[2,512,512]{2,1,0:T(8,128)S(1)} %within_shard.1.y_ref, bf16[2,4,128,128]{3,2,1,0:T(8,128)(2,1)S(1)} %pad_maximum_fusion.1.s_ref, bf16[2,512,256]{2,1,0:T(8,128)(2,1)S(1)} %get-tuple-element.87.bc_ref, f32[2,512,128]{2,1,0:T(8,128)S(1)} %get-tuple-element.89.cum_ref, ...), custom_call_target="tpu_custom_call" | custom-call | flops 1000000000 | bytes 5242880 | tf_op jit(solution)/shard_map/finish/pallas_call | solution.py:405
  151.2 2.5 %collective-permute-done.23.b = bf16[512,1024]{1,0:T(8,128)(2,1)} collective-permute-done((bf16[512,1024]{1,0:T(8,128)(2,1)S(1)}, bf16[512,1024]{1,0:T(8,128)(2,1)}, u32[]{:S(2)}, u32[]{:S(2)}) %collective-permute-start.23) | collective-permute-done | bytes 1048608 | tf_op jit(solution)/shard_map/ppermute | solution.py:28
  153.7 2.7 %output_stage.5 = f32[1,512,256]{2,1,0:T(8,128)S(1)} custom-call(s32[2]{0:T(128)S(1)} %pad_add_fusion.2.idx, bf16[512,1024]{1,0:T(8,128)(2,1)S(1)} %finish.1.a, bf16[512,1024]{1,0:T(8,128)(2,1)} %collective-permute-done.23.b, bf16[4096,512]{1,0:T(8,128)(2,1)} %copy-done, bf16[4096,512]{1,0:T(8,128)(2,1)} %get-tuple-element.96.q0, ...), custom_call_target="tpu_custom_call" | custom-call | flops 536870912 | bytes 2097152 | tf_op jit(solution)/shard_map/output_stage/pallas_call | solution.py:497
  156.6 3.2 %collective-permute-start.32 = (bf16[168,256]{1,0:T(8,128)(2,1)S(1)}, bf16[168,256]{1,0:T(8,128)(2,1)S(1)}, u32[]{:S(2)}, u32[]{:S(2)}) collective-permute-start(bf16[168,256]{1,0:T(8,128)(2,1)S(1)} %get-tuple-element.119), channel_id=1, source_target_pairs={{0,6},{1,7},{2,0},{3,1},{4,2},{5,3},{6,4},{7,5},{8,14},{9,15},{10,... | collective-permute-start | bytes 258056 | tf_op jit(solution)/shard_map/ppermute | solution.py:24
  159.8 4.8 %output_stage.4 = f32[3,512,256]{2,1,0:T(8,128)S(1)} custom-call(s32[6]{0:T(128)S(1)} %stack.205.idx, bf16[512,1024]{1,0:T(8,128)(2,1)S(1)} %finish.1.a, bf16[512,1024]{1,0:T(8,128)(2,1)} %collective-permute-done.23.b, bf16[4096,512]{1,0:T(8,128)(2,1)} %copy-done, bf16[4096,512]{1,0:T(8,128)(2,1)} %get-tuple-element.96.q0, ...), custom_call_target="tpu_custom_call" | custom-call | flops 1610612736 | bytes 6291456 | tf_op jit(solution)/shard_map/output_stage/pallas_call | solution.py:497
  164.7 0.5 collective-permute-start.28
  165.3 1.7 collective-permute-start.27
  166.9 3.4 %collective-permute-done.28 = bf16[176,256]{1,0:T(8,128)(2,1)S(1)} collective-permute-done((bf16[176,256]{1,0:T(8,128)(2,1)S(1)}, bf16[176,256]{1,0:T(8,128)(2,1)S(1)}, u32[]{:S(2)}, u32[]{:S(2)}) %collective-permute-start.28) | collective-permute-done | bytes 90144 | tf_op jit(solution)/shard_map/ppermute | solution.py:24
  170.4 5.8 %output_stage.3 = f32[4,512,256]{2,1,0:T(8,128)S(1)} custom-call(s32[8]{0:T(128)S(1)} %stack.168.idx, bf16[512,1024]{1,0:T(8,128)(2,1)S(1)} %finish.1.a, bf16[512,1024]{1,0:T(8,128)(2,1)} %collective-permute-done.23.b, bf16[4096,512]{1,0:T(8,128)(2,1)} %copy-done, bf16[4096,512]{1,0:T(8,128)(2,1)} %get-tuple-element.96.q0, bf16[2048,512]{1,0:T(8,128)(2,1)} %copy-done.1, ...), custom_call_target="tpu_custom_call" | custom-call | flops 2147483648 | bytes 8388608 | tf_op jit(solution)/shard_map/output_stage/pallas_call | solution.py:497
  176.3 3.3 %collective-permute-start.31 = (bf16[512,256]{1,0:T(8,128)(2,1)S(1)}, bf16[512,256]{1,0:T(8,128)(2,1)S(1)}, u32[]{:S(2)}, u32[]{:S(2)}) collective-permute-start(bf16[512,256]{1,0:T(8,128)(2,1)S(1)} %fusion.29), channel_id=1, source_target_pairs={{0,6},{1,7},{2,0},{3,1},{4,2},{5,3},{6,4},{7,5},{8,14},{9,15},{10,... | collective-permute-start | bytes 786440 | tf_op jit(solution)/shard_map/ppermute | solution.py:24
  180.2 3.2 %collective-permute-done.31 = bf16[512,256]{1,0:T(8,128)(2,1)S(1)} collective-permute-done((bf16[512,256]{1,0:T(8,128)(2,1)S(1)}, bf16[512,256]{1,0:T(8,128)(2,1)S(1)}, u32[]{:S(2)}, u32[]{:S(2)}) %collective-permute-start.31) | collective-permute-done | bytes 262176 | tf_op jit(solution)/shard_map/ppermute | solution.py:24
  183.5 3.9 %collective-permute-done.30 = bf16[512,256]{1,0:T(8,128)(2,1)S(1)} collective-permute-done((bf16[512,256]{1,0:T(8,128)(2,1)S(1)}, bf16[512,256]{1,0:T(8,128)(2,1)S(1)}, u32[]{:S(2)}, u32[]{:S(2)}) %collective-permute-start.30) | collective-permute-done | bytes 262176 | tf_op jit(solution)/shard_map/ppermute | solution.py:24
  187.4 0.9 fusion.10
  (134 shorter events, 5.4 us)
Async XLA Ops:
  0.0 31.9 %collective-permute-start.16 = (bf16[512,256]{1,0:T(8,128)(2,1)}, bf16[512,256]{1,0:T(8,128)(2,1)S(1)}, u32[]{:S(2)}, u32[]{:S(2)}) collective-permute-start(bf16[512,256]{1,0:T(8,128)(2,1)} %refs_0_.1), channel_id=1, source_target_pairs={{0,1},{1,0},{2,3},{3,2},{4,5},{5,4},{6,7},{7,6},{8,9},{9,8},{10,11... | collective-permute-start | bytes 786440 | tf_op jit(solution)/shard_map/ppermute | solution.py:28
  0.0 29.9 %collective-permute-start = (bf16[512,256]{1,0:T(8,128)(2,1)}, bf16[512,256]{1,0:T(8,128)(2,1)S(1)}, u32[]{:S(2)}, u32[]{:S(2)}) collective-permute-start(bf16[512,256]{1,0:T(8,128)(2,1)} %refs_0_.1), channel_id=1, source_target_pairs={{0,2},{1,3},{2,4},{3,5},{4,6},{5,7},{6,0},{7,1},{8,10},{9,11},{10,... | collective-permute-start | bytes 786440 | tf_op jit(solution)/shard_map/ppermute | solution.py:24
  1.6 30.7 %collective-permute-start.3 = (bf16[512,256]{1,0:T(8,128)(2,1)}, bf16[512,256]{1,0:T(8,128)(2,1)S(1)}, u32[]{:S(2)}, u32[]{:S(2)}) collective-permute-start(bf16[512,256]{1,0:T(8,128)(2,1)} %refs_0_.1), channel_id=1, source_target_pairs={{0,8},{1,9},{2,10},{3,11},{4,12},{5,13},{6,14},{7,15},{8,0},{9,1},... | collective-permute-start | bytes 786440 | tf_op jit(solution)/shard_map/ppermute | solution.py:24
  3.2 29.4 %collective-permute-start.13 = (bf16[512,256]{1,0:T(8,128)(2,1)}, bf16[512,256]{1,0:T(8,128)(2,1)S(1)}, u32[]{:S(2)}, u32[]{:S(2)}) collective-permute-start(bf16[512,256]{1,0:T(8,128)(2,1)} %refs_0_.1), channel_id=1, source_target_pairs={{0,6},{1,7},{2,0},{3,1},{4,2},{5,3},{6,4},{7,5},{8,14},{9,15},{10,... | collective-permute-start | bytes 786440 | tf_op jit(solution)/shard_map/ppermute | solution.py:24
  7.6 0.7 copy-start.3
  8.3 15.2 %copy-start.8 = (bf16[4096,256]{1,0:T(8,128)(2,1)S(1)}, bf16[4096,256]{1,0:T(8,128)(2,1)}, u32[]{:S(2)}) copy-start(bf16[4096,256]{1,0:T(8,128)(2,1)} %param.22) | copy-start | bytes 6291460
  23.5 3.0 %copy-start = (bf16[4096,512]{1,0:T(8,128)(2,1)}, bf16[4096,512]{1,0:T(8,128)(2,1)S(1)}, u32[]{:S(2)}) copy-start(bf16[4096,512]{1,0:T(8,128)(2,1)S(1)} %get-tuple-element.95.p0) | copy-start | bytes 12582916
  26.6 3.8 %copy-start.7 = (bf16[4096,512]{1,0:T(8,128)(2,1)S(1)}, bf16[4096,512]{1,0:T(8,128)(2,1)}, u32[]{:S(2)}) copy-start(bf16[4096,512]{1,0:T(8,128)(2,1)} %get-tuple-element.96.q0) | copy-start | bytes 12582916
  29.9 8.0 %copy-start.2 = (bf16[512,256]{1,0:T(8,128)(2,1)S(1)}, bf16[512,256]{1,0:T(8,128)(2,1)}, u32[]{:S(2)}) copy-start(bf16[512,256]{1,0:T(8,128)(2,1)} %refs_0_.1) | copy-start | bytes 786436
  29.9 8.0 %copy-start.4 = (s32[4096]{0:T(1024)S(1)}, s32[4096]{0:T(1024)}, u32[]{:S(2)}) copy-start(s32[4096]{0:T(1024)} %idx.1) | copy-start | bytes 49156
  30.0 8.0 %collective-permute-start.1 = (bf16[512,256]{1,0:T(8,128)(2,1)S(1)}, bf16[512,256]{1,0:T(8,128)(2,1)S(1)}, u32[]{:S(2)}, u32[]{:S(2)}) collective-permute-start(bf16[512,256]{1,0:T(8,128)(2,1)S(1)} %collective-permute-done.refs_0_), channel_id=1, source_target_pairs={{0,8},{1,9},{2,10},{3,11},{4,12},{5,13},{6,14},{7,15},{8,0},{9,1},... | collective-permute-start | bytes 786440 | tf_op jit(solution)/shard_map/ppermute | solution.py:24
  31.9 14.3 %collective-permute-start.12 = (bf16[512,256]{1,0:T(8,128)(2,1)S(1)}, bf16[512,256]{1,0:T(8,128)(2,1)S(1)}, u32[]{:S(2)}, u32[]{:S(2)}) collective-permute-start(bf16[512,256]{1,0:T(8,128)(2,1)S(1)} %collective-permute-done.refs_0_), channel_id=1, source_target_pairs={{0,1},{1,0},{2,3},{3,2},{4,5},{5,4},{6,7},{7,6},{8,9},{9,8},{10,11... | collective-permute-start | bytes 786440 | tf_op jit(solution)/shard_map/ppermute | solution.py:28
  31.9 17.6 %collective-permute-start.6 = (bf16[512,256]{1,0:T(8,128)(2,1)S(1)}, bf16[512,256]{1,0:T(8,128)(2,1)S(1)}, u32[]{:S(2)}, u32[]{:S(2)}) collective-permute-start(bf16[512,256]{1,0:T(8,128)(2,1)S(1)} %collective-permute-done.refs_0_), channel_id=1, source_target_pairs={{0,2},{1,3},{2,4},{3,5},{4,6},{5,7},{6,0},{7,1},{8,10},{9,11},{10,... | collective-permute-start | bytes 786440 | tf_op jit(solution)/shard_map/ppermute | solution.py:24
  32.3 14.2 %collective-permute-start.15 = (bf16[512,256]{1,0:T(8,128)(2,1)S(1)}, bf16[512,256]{1,0:T(8,128)(2,1)S(1)}, u32[]{:S(2)}, u32[]{:S(2)}) collective-permute-start(bf16[512,256]{1,0:T(8,128)(2,1)S(1)} %collective-permute-done.3.refs_4_), channel_id=1, source_target_pairs={{0,1},{1,0},{2,3},{3,2},{4,5},{5,4},{6,7},{7,6},{8,9},{9,8},{10,11... | collective-permute-start | bytes 786440 | tf_op jit(solution)/shard_map/ppermute | solution.py:28
  32.5 13.1 %collective-permute-start.4 = (bf16[512,256]{1,0:T(8,128)(2,1)S(1)}, bf16[512,256]{1,0:T(8,128)(2,1)S(1)}, u32[]{:S(2)}, u32[]{:S(2)}) collective-permute-start(bf16[512,256]{1,0:T(8,128)(2,1)S(1)} %collective-permute-done.3.refs_4_), channel_id=1, source_target_pairs={{0,6},{1,7},{2,0},{3,1},{4,2},{5,3},{6,4},{7,5},{8,14},{9,15},{10,... | collective-permute-start | bytes 786440 | tf_op jit(solution)/shard_map/ppermute | solution.py:24
  37.9 11.6 %collective-permute-start.14 = (bf16[512,256]{1,0:T(8,128)(2,1)S(1)}, bf16[512,256]{1,0:T(8,128)(2,1)S(1)}, u32[]{:S(2)}, u32[]{:S(2)}) collective-permute-start(bf16[512,256]{1,0:T(8,128)(2,1)S(1)} %collective-permute-done.13.refs_2_), channel_id=1, source_target_pairs={{0,1},{1,0},{2,3},{3,2},{4,5},{5,4},{6,7},{7,6},{8,9},{9,8},{10,11... | collective-permute-start | bytes 786440 | tf_op jit(solution)/shard_map/ppermute | solution.py:28
  45.6 105.6 %collective-permute-start.24 = (bf16[2048,512]{1,0:T(8,128)(2,1)}, bf16[2048,512]{1,0:T(8,128)(2,1)S(1)}, u32[]{:S(2)}, u32[]{:S(2)}) collective-permute-start(bf16[2048,512]{1,0:T(8,128)(2,1)} %bitcast.58), channel_id=1, source_target_pairs={{0,1},{1,0},{2,3},{3,2},{4,5},{5,4},{6,7},{7,6},{8,9},{9,8},{10,11... | collective-permute-start | bytes 6291464 | tf_op jit(solution)/shard_map/ppermute | solution.py:28
  46.2 18.6 %collective-permute-start.2 = (bf16[168,256]{1,0:T(8,128)(2,1)S(1)}, bf16[168,256]{1,0:T(8,128)(2,1)S(1)}, u32[]{:S(2)}, u32[]{:S(2)}) collective-permute-start(bf16[168,256]{1,0:T(8,128)(2,1)S(1)} %slice.299), channel_id=1, source_target_pairs={{0,2},{1,3},{2,4},{3,5},{4,6},{5,7},{6,0},{7,1},{8,10},{9,11},{10,... | collective-permute-start | bytes 258056 | tf_op jit(solution)/shard_map/ppermute | solution.py:24
  46.5 18.4 %collective-permute-start.5 = (bf16[168,256]{1,0:T(8,128)(2,1)S(1)}, bf16[168,256]{1,0:T(8,128)(2,1)S(1)}, u32[]{:S(2)}, u32[]{:S(2)}) collective-permute-start(bf16[168,256]{1,0:T(8,128)(2,1)S(1)} %slice.300), channel_id=1, source_target_pairs={{0,6},{1,7},{2,0},{3,1},{4,2},{5,3},{6,4},{7,5},{8,14},{9,15},{10,... | collective-permute-start | bytes 258056 | tf_op jit(solution)/shard_map/ppermute | solution.py:24
  49.5 21.3 %collective-permute-start.9 = (bf16[512,256]{1,0:T(8,128)(2,1)S(1)}, bf16[512,256]{1,0:T(8,128)(2,1)S(1)}, u32[]{:S(2)}, u32[]{:S(2)}) collective-permute-start(bf16[512,256]{1,0:T(8,128)(2,1)S(1)} %collective-permute-done.1.refs_0_), channel_id=1, source_target_pairs={{0,1},{1,0},{2,3},{3,2},{4,5},{5,4},{6,7},{7,6},{8,9},{9,8},{10,11... | collective-permute-start | bytes 786440 | tf_op jit(solution)/shard_map/ppermute | solution.py:28
  49.5 20.5 %collective-permute-start.11 = (bf16[512,256]{1,0:T(8,128)(2,1)S(1)}, bf16[512,256]{1,0:T(8,128)(2,1)S(1)}, u32[]{:S(2)}, u32[]{:S(2)}) collective-permute-start(bf16[512,256]{1,0:T(8,128)(2,1)S(1)} %collective-permute-done.6.refs_4_), channel_id=1, source_target_pairs={{0,1},{1,0},{2,3},{3,2},{4,5},{5,4},{6,7},{7,6},{8,9},{9,8},{10,11... | collective-permute-start | bytes 786440 | tf_op jit(solution)/shard_map/ppermute | solution.py:28
  64.8 6.0 %collective-permute-start.10 = (bf16[512,256]{1,0:T(8,128)(2,1)S(1)}, bf16[512,256]{1,0:T(8,128)(2,1)S(1)}, u32[]{:S(2)}, u32[]{:S(2)}) collective-permute-start(bf16[512,256]{1,0:T(8,128)(2,1)S(1)} %collective-permute-done.4.refs_2_), channel_id=1, source_target_pairs={{0,1},{1,0},{2,3},{3,2},{4,5},{5,4},{6,7},{7,6},{8,9},{9,8},{10,11... | collective-permute-start | bytes 786440 | tf_op jit(solution)/shard_map/ppermute | solution.py:28
  64.9 5.0 %collective-permute-start.7 = (bf16[176,256]{1,0:T(8,128)(2,1)S(1)}, bf16[176,256]{1,0:T(8,128)(2,1)S(1)}, u32[]{:S(2)}, u32[]{:S(2)}) collective-permute-start(bf16[176,256]{1,0:T(8,128)(2,1)S(1)} %slice.301), channel_id=1, source_target_pairs={{0,8},{1,9},{2,10},{3,11},{4,12},{5,13},{6,14},{7,15},{8,0},{9,1},... | collective-permute-start | bytes 270344 | tf_op jit(solution)/shard_map/ppermute | solution.py:24
  70.0 81.2 %collective-permute-start.25 = (bf16[2048,512]{1,0:T(8,128)(2,1)}, bf16[2048,512]{1,0:T(8,128)(2,1)}, u32[]{:S(2)}, u32[]{:S(2)}) collective-permute-start(bf16[2048,512]{1,0:T(8,128)(2,1)} %bitcast.60), channel_id=1, source_target_pairs={{0,1},{1,0},{2,3},{3,2},{4,5},{5,4},{6,7},{7,6},{8,9},{9,8},{10,11... | collective-permute-start | bytes 6291464 | tf_op jit(solution)/shard_map/ppermute | solution.py:28
  70.0 15.5 %collective-permute-start.8 = (bf16[512,256]{1,0:T(8,128)(2,1)S(1)}, bf16[512,256]{1,0:T(8,128)(2,1)S(1)}, u32[]{:S(2)}, u32[]{:S(2)}) collective-permute-start(bf16[512,256]{1,0:T(8,128)(2,1)S(1)} %constant_dynamic-update-slice_fusion.refs_0_), channel_id=1, source_target_pairs={{0,1},{1,0},{2,3},{3,2},{4,5},{5,4},{6,7},{7,6},{8,9},{9,8},{10,11... | collective-permute-start | bytes 786440 | tf_op jit(solution)/shard_map/ppermute | solution.py:28
  107.3 13.6 %collective-permute-start.17 = (bf16[8,512]{1,0:T(8,128)(2,1)S(1)}, bf16[8,512]{1,0:T(8,128)(2,1)S(1)}, u32[]{:S(2)}, u32[]{:S(2)}) collective-permute-start(bf16[8,512]{1,0:T(8,128)(2,1)S(1)} %get-tuple-element.120), channel_id=1, source_target_pairs={{0,16},{16,32},{32,48},{48,64},{64,80},{80,96},{96,112},{1,17},{17... | collective-permute-start | bytes 24584 | tf_op jit(solution)/shard_map/ppermute | solution.py:528
  112.1 8.8 %collective-permute-start.18 = (bf16[8,512]{1,0:T(8,128)(2,1)S(1)}, bf16[8,512]{1,0:T(8,128)(2,1)S(1)}, u32[]{:S(2)}, u32[]{:S(2)}) collective-permute-start(bf16[8,512]{1,0:T(8,128)(2,1)S(1)} %get-tuple-element.121), channel_id=1, source_target_pairs={{16,0},{32,16},{48,32},{64,48},{80,64},{96,80},{112,96},{17,1},{33... | collective-permute-start | bytes 24584 | tf_op jit(solution)/shard_map/ppermute | solution.py:529
  113.4 7.7 %copy-start.10 = (pred[8]{0:T(512)(128)(4,1)S(1)}, pred[8]{0:T(512)(128)(4,1)}, u32[]{:S(2)}) copy-start(pred[8]{0:T(512)(128)(4,1)} %constant.306.clone.1) | copy-start | bytes 28
  113.4 7.8 %copy-start.6 = (f32[4,512]{1,0:T(4,128)S(1)}, f32[4,512]{1,0:T(4,128)}, u32[]{:S(2)}) copy-start(f32[4,512]{1,0:T(4,128)} %taps_ref.1) | copy-start | bytes 24580
  124.3 13.6 %collective-permute-start.19 = (bf16[528,128]{1,0:T(8,128)(2,1)S(1)}, bf16[528,128]{1,0:T(8,128)(2,1)S(1)}, u32[]{:S(2)}, u32[]{:S(2)}) collective-permute-start(bf16[528,128]{1,0:T(8,128)(2,1)S(1)} %get-tuple-element.117), channel_id=1, source_target_pairs={{0,32},{16,48},{32,64},{48,80},{64,96},{80,112},{96,0},{112,16},{1... | collective-permute-start | bytes 405512 | tf_op jit(solution)/shard_map/ppermute | solution.py:631
  128.5 9.4 %collective-permute-start.20 = (bf16[528,128]{1,0:T(8,128)(2,1)S(1)}, bf16[528,128]{1,0:T(8,128)(2,1)S(1)}, u32[]{:S(2)}, u32[]{:S(2)}) collective-permute-start(bf16[528,128]{1,0:T(8,128)(2,1)S(1)} %get-tuple-element.116), channel_id=1, source_target_pairs={{0,64},{16,80},{32,96},{48,112},{64,0},{80,16},{96,32},{112,48},{1... | collective-permute-start | bytes 405512 | tf_op jit(solution)/shard_map/ppermute | solution.py:631
  132.0 5.9 %collective-permute-start.21 = (bf16[528,128]{1,0:T(8,128)(2,1)S(1)}, bf16[528,128]{1,0:T(8,128)(2,1)S(1)}, u32[]{:S(2)}, u32[]{:S(2)}) collective-permute-start(bf16[528,128]{1,0:T(8,128)(2,1)S(1)} %get-tuple-element.115), channel_id=1, source_target_pairs={{0,96},{16,112},{32,0},{48,16},{64,32},{80,48},{96,64},{112,80},{1... | collective-permute-start | bytes 405512 | tf_op jit(solution)/shard_map/ppermute | solution.py:631
  138.5 8.4 %collective-permute-start.22 = (bf16[2,4,128,128]{3,2,1,0:T(8,128)(2,1)S(1)}, bf16[2,4,128,128]{3,2,1,0:T(8,128)(2,1)S(1)}, u32[]{:S(2)}, u32[]{:S(2)}) collective-permute-start(bf16[2,4,128,128]{3,2,1,0:T(8,128)(2,1)S(1)} %pad_maximum_fusion), channel_id=1, source_target_pairs={{0,16},{16,0},{32,48},{48,32},{64,80},{80,64},{96,112},{112,96},{1... | collective-permute-start | bytes 786440 | tf_op jit(solution)/shard_map/ppermute | solution.py:656
  140.8 6.6 %copy-start.5 = (f32[512]{0:T(512)S(1)}, f32[512]{0:T(512)}, u32[]{:S(2)}) copy-start(f32[512]{0:T(512)} %param.28) | copy-start | bytes 6148
  150.8 2.9 %collective-permute-start.23 = (bf16[512,1024]{1,0:T(8,128)(2,1)S(1)}, bf16[512,1024]{1,0:T(8,128)(2,1)}, u32[]{:S(2)}, u32[]{:S(2)}) collective-permute-start(bf16[512,1024]{1,0:T(8,128)(2,1)S(1)} %finish.1.a), channel_id=1, source_target_pairs={{0,1},{1,0},{2,3},{3,2},{4,5},{5,4},{6,7},{7,6},{8,9},{9,8},{10,11... | collective-permute-start | bytes 3145736 | tf_op jit(solution)/shard_map/ppermute | solution.py:28
  151.2 8.6 %copy-start.1 = (bf16[2048,512]{1,0:T(8,128)(2,1)}, bf16[2048,512]{1,0:T(8,128)(2,1)S(1)}, u32[]{:S(2)}) copy-start(bf16[2048,512]{1,0:T(8,128)(2,1)S(1)} %collective-permute-done.24.p1) | copy-start | bytes 6291460
  156.5 8.7 %collective-permute-start.26 = (bf16[168,256]{1,0:T(8,128)(2,1)S(1)}, bf16[168,256]{1,0:T(8,128)(2,1)S(1)}, u32[]{:S(2)}, u32[]{:S(2)}) collective-permute-start(bf16[168,256]{1,0:T(8,128)(2,1)S(1)} %get-tuple-element.118), channel_id=1, source_target_pairs={{0,2},{1,3},{2,4},{3,5},{4,6},{5,7},{6,0},{7,1},{8,10},{9,11},{10,... | collective-permute-start | bytes 258056 | tf_op jit(solution)/shard_map/ppermute | solution.py:24
  156.6 8.6 %collective-permute-start.32 = (bf16[168,256]{1,0:T(8,128)(2,1)S(1)}, bf16[168,256]{1,0:T(8,128)(2,1)S(1)}, u32[]{:S(2)}, u32[]{:S(2)}) collective-permute-start(bf16[168,256]{1,0:T(8,128)(2,1)S(1)} %get-tuple-element.119), channel_id=1, source_target_pairs={{0,6},{1,7},{2,0},{3,1},{4,2},{5,3},{6,4},{7,5},{8,14},{9,15},{10,... | collective-permute-start | bytes 258056 | tf_op jit(solution)/shard_map/ppermute | solution.py:24
  164.7 5.6 %collective-permute-start.28 = (bf16[176,256]{1,0:T(8,128)(2,1)S(1)}, bf16[176,256]{1,0:T(8,128)(2,1)S(1)}, u32[]{:S(2)}, u32[]{:S(2)}) collective-permute-start(bf16[176,256]{1,0:T(8,128)(2,1)S(1)} %slice_bitcast_fusion.9), channel_id=1, source_target_pairs={{0,8},{1,9},{2,10},{3,11},{4,12},{5,13},{6,14},{7,15},{8,0},{9,1},... | collective-permute-start | bytes 270344 | tf_op jit(solution)/shard_map/ppermute | solution.py:24
  165.3 14.3 %collective-permute-start.27 = (bf16[512,256]{1,0:T(8,128)(2,1)S(1)}, bf16[512,256]{1,0:T(8,128)(2,1)S(1)}, u32[]{:S(2)}, u32[]{:S(2)}) collective-permute-start(bf16[512,256]{1,0:T(8,128)(2,1)S(1)} %get-tuple-element.105), channel_id=1, source_target_pairs={{0,8},{1,9},{2,10},{3,11},{4,12},{5,13},{6,14},{7,15},{8,0},{9,1},... | collective-permute-start | bytes 786440 | tf_op jit(solution)/shard_map/ppermute | solution.py:24
  166.9 12.7 %collective-permute-start.33 = (bf16[512,256]{1,0:T(8,128)(2,1)S(1)}, bf16[512,256]{1,0:T(8,128)(2,1)S(1)}, u32[]{:S(2)}, u32[]{:S(2)}) collective-permute-start(bf16[512,256]{1,0:T(8,128)(2,1)S(1)} %get-tuple-element.106), channel_id=1, source_target_pairs={{0,6},{1,7},{2,0},{3,1},{4,2},{5,3},{6,4},{7,5},{8,14},{9,15},{10,... | collective-permute-start | bytes 786440 | tf_op jit(solution)/shard_map/ppermute | solution.py:24
  170.3 9.2 %collective-permute-start.29 = (bf16[512,256]{1,0:T(8,128)(2,1)S(1)}, bf16[512,256]{1,0:T(8,128)(2,1)S(1)}, u32[]{:S(2)}, u32[]{:S(2)}) collective-permute-start(bf16[512,256]{1,0:T(8,128)(2,1)S(1)} %fusion.31), channel_id=1, source_target_pairs={{0,2},{1,3},{2,4},{3,5},{4,6},{5,7},{6,0},{7,1},{8,10},{9,11},{10,... | collective-permute-start | bytes 786440 | tf_op jit(solution)/shard_map/ppermute | solution.py:24
  176.2 11.2 %copy-start.9 = (s32[512,256]{1,0:T(8,128)S(1)}, s32[512,256]{1,0:T(8,128)}, u32[]{:S(2)}) copy-start(s32[512,256]{1,0:T(8,128)} %param.31) | copy-start | bytes 1572868
  176.3 7.2 %collective-permute-start.31 = (bf16[512,256]{1,0:T(8,128)(2,1)S(1)}, bf16[512,256]{1,0:T(8,128)(2,1)S(1)}, u32[]{:S(2)}, u32[]{:S(2)}) collective-permute-start(bf16[512,256]{1,0:T(8,128)(2,1)S(1)} %fusion.29), channel_id=1, source_target_pairs={{0,6},{1,7},{2,0},{3,1},{4,2},{5,3},{6,4},{7,5},{8,14},{9,15},{10,... | collective-permute-start | bytes 786440 | tf_op jit(solution)/shard_map/ppermute | solution.py:24
  179.7 7.7 %collective-permute-start.30 = (bf16[512,256]{1,0:T(8,128)(2,1)S(1)}, bf16[512,256]{1,0:T(8,128)(2,1)S(1)}, u32[]{:S(2)}, u32[]{:S(2)}) collective-permute-start(bf16[512,256]{1,0:T(8,128)(2,1)S(1)} %get-tuple-element.103), channel_id=1, source_target_pairs={{0,2},{1,3},{2,4},{3,5},{4,6},{5,7},{6,0},{7,1},{8,10},{9,11},{10,... | collective-permute-start | bytes 786440 | tf_op jit(solution)/shard_map/ppermute | solution.py:24
  179.8 7.6 %collective-permute-start.34 = (bf16[512,256]{1,0:T(8,128)(2,1)S(1)}, bf16[512,256]{1,0:T(8,128)(2,1)S(1)}, u32[]{:S(2)}, u32[]{:S(2)}) collective-permute-start(bf16[512,256]{1,0:T(8,128)(2,1)S(1)} %get-tuple-element.104), channel_id=1, source_target_pairs={{0,8},{1,9},{2,10},{3,11},{4,12},{5,13},{6,14},{7,15},{8,0},{9,1},... | collective-permute-start | bytes 786440 | tf_op jit(solution)/shard_map/ppermute | solution.py:24

commit v2 on v1

v2 whole, which is shorter than its diff:
```python
import jax
import jax.numpy as jnp
from jax import lax
from jax.experimental import pallas as pl
from jax.experimental.pallas import tpu as pltpu
from jax.sharding import PartitionSpec as P

BF = jnp.bfloat16
F32 = jnp.float32
KW = 4


def chip_route(dy, dx):
    return [
        ((y * 4 + x) * 2 + c, ((y + dy) % 2 * 4 + (x + dx) % 4) * 2 + c)
        for y in range(2)
        for x in range(4)
        for c in range(2)
    ]


def to_chip(a, dy, dx):
    return lax.ppermute(a, "chan", chip_route(dy, dx))


def to_sibling(a):
    return lax.ppermute(a, "chan", [(i, i ^ 1) for i in range(16)])


def dot(a, b, dims=((1,), (0,)), precision=None):
    return lax.dot_general(
        a, b, (dims, ((), ())), preferred_element_type=F32, precision=precision
    )


def params(mib=24):
    return pltpu.CompilerParams(vmem_limit_bytes=mib * 2**20)


def cost(flops, nbytes):
    return pl.CostEstimate(flops=int(flops), bytes_accessed=int(nbytes), transcendentals=0)


def project(blocks, chans, comp, gate_proj, value_proj, state_proj, step_t, bias, rate):
    nb = len(blocks)
    rows, width = blocks[0].shape
    d = comp.shape[0]
    inner = gate_proj.shape[1]
    ns = state_proj.shape[1]
    heads = step_t.shape[0]
    tiles = rows // 128

    def kernel(chan, idx, *refs):
        tok = refs[:nb]
        wg_hbm, wv_hbm, ws_hbm, st_ref, bias_ref, rate_ref = refs[nb : nb + 6]
        v_out, g_out, bc_out, step_o, cum_o, step_to, cum_to, decay_o = refs[nb + 6 : nb + 14]
        t, tp, by_row, picked, wg, wv, ws, sem, wsem = refs[nb + 14 :]

        def token_copy(j, at):
            return pltpu.make_async_copy(tok[j], t.at[:, pl.ds(at, width)], sem.at[j])

        weight_copies = [
            pltpu.make_async_copy(a, b, wsem.at[i])
            for i, (a, b) in enumerate([(ws_hbm, ws.at[:, :ns]), (wv_hbm, wv), (wg_hbm, wg)])
        ]
        for j in range(nb):
            token_copy(j, pl.multiple_of(chan[j] * width, width)).start()
        for c in weight_copies:
            c.start()
        st = st_ref[...].astype(F32)
        wst = jnp.concatenate([st, jnp.zeros((128 - heads, d), F32)], axis=0).T
        ws[:, ns:] = wst.astype(BF)

        for j in range(nb):
            at = pl.multiple_of(chan[j] * width, width)
            token_copy(j, at).wait()
            for k in range(tiles):
                part = t[128 * k : 128 * k + 128, pl.ds(at, width)].astype(F32).T
                by_row[pl.ds(at * tiles + k, width, tiles), :] = part

        def permute(c, _):
            b0 = c * width

            def body(n, _):
                for k in range(32):
                    row = n * 32 + k
                    src = pl.multiple_of(idx[b0 + row], tiles)
                    dst = pl.multiple_of(row * tiles, tiles)
                    picked[pl.ds(dst, tiles), :] = by_row[pl.ds(src, tiles), :]
                return 0

            lax.fori_loop(0, width // 32, body, 0)
            for k in range(tiles):
                part = picked[pl.ds(k, width, tiles), :].T
                tp[128 * k : 128 * k + 128, pl.ds(pl.multiple_of(b0, width), width)] = part.astype(BF)
            return 0

        lax.fori_loop(0, d // width, permute, 0)
        weight_copies[0].wait()
        r = lax.broadcasted_iota(jnp.int32, (rows, rows), 0)
        q = lax.broadcasted_iota(jnp.int32, (rows, rows), 1)
        for b, u in enumerate((t, tp)):
            small = dot(u[...], ws[...])
            bc_out[b] = small[:, :ns].astype(BF)
            step = jax.nn.softplus(small[:, ns:] + bias_ref[...])
            tri = jnp.where((r >= q) if b == 0 else (r <= q), 1.0, 0.0).astype(BF)
            logdec = -step * rate_ref[...]
            high = logdec.astype(BF)
            rest = logdec - high.astype(F32)
            mid = rest.astype(BF)
            low = (rest - mid.astype(F32)).astype(BF)
            sums = dot(tri, jnp.concatenate([high, mid, low], axis=1))
            cum = sums[:, :128] + sums[:, 128:256] + sums[:, 256:]
            step_o[b] = step
            cum_o[b] = cum
            step_to[b] = step.T[:8]
            cum_to[b] = cum.T[:8]
            decay_o[b : b + 1] = jnp.exp(cum[rows - 1 : rows] if b == 0 else cum[0:1])
        weight_copies[1].wait()
        for b, u in enumerate((t, tp)):
            v_out[b] = dot(u[...], wv[...]).astype(BF)
        weight_copies[2].wait()
        for b, u in enumerate((t, tp)):
            g_out[b] = dot(u[...], wg[...]).astype(BF)

    shapes = [
        jax.ShapeDtypeStruct((2, rows, inner), BF),
        jax.ShapeDtypeStruct((2, rows, inner), BF),
        jax.ShapeDtypeStruct((2, rows, ns), BF),
        jax.ShapeDtypeStruct((2, rows, 128), F32),
        jax.ShapeDtypeStruct((2, rows, 128), F32),
        jax.ShapeDtypeStruct((2, 8, rows), F32),
        jax.ShapeDtypeStruct((2, 8, rows), F32),
        jax.ShapeDtypeStruct((2, 128), F32),
    ]
    whole = lambda shape: pl.BlockSpec(shape, lambda n, s, i: (0,) * len(shape))
    any_spec = pl.BlockSpec(memory_space=pl.ANY)
    return pl.pallas_call(
        kernel,
        grid_spec=pltpu.PrefetchScalarGridSpec(
            num_scalar_prefetch=2,
            grid=(1,),
            in_specs=[any_spec] * (nb + 3) + [whole((heads, d)), whole((1, 128)), whole((1, 128))],
            out_specs=[whole(o.shape) for o in shapes],
            scratch_shapes=[
                pltpu.VMEM((rows, d), BF),
                pltpu.VMEM((rows, d), BF),
                pltpu.VMEM((d * tiles, 128), F32),
                pltpu.VMEM((width * tiles, 128), F32),
                pltpu.VMEM((d, inner), BF),
                pltpu.VMEM((d, inner), BF),
                pltpu.VMEM((d, ns + 128), BF),
                pltpu.SemaphoreType.DMA((nb,)),
                pltpu.SemaphoreType.DMA((3,)),
            ],
        ),
        out_shape=shapes,
        compiler_params=params(60),
        cost_estimate=cost(4 * rows * d * (2 * inner + 512), 20 * 2**20),
        name="project",
    )(chans, comp * tiles, *blocks, gate_proj, value_proj, state_proj, step_t, bias, rate)


def conv_states(value, halo, taps, bc, step, cum):
    _, rows, inner = value.shape
    heads = inner // 128

    def kernel(v_ref, halo_ref, taps_ref, bc_ref, step_ref, cum_ref, xs_o, end_o):
        def branch(b):
            v = v_ref[0].astype(F32)
            hal = halo_ref[0].astype(F32)
            if b == 0:
                padded = jnp.concatenate([hal, v], axis=0)
                shift = lambda k: padded[5 + k : 5 + k + rows]
            else:
                padded = jnp.concatenate([v, hal], axis=0)
                shift = lambda k: padded[3 - k : 3 - k + rows]
            conv = taps_ref[0:1] * shift(0)
            for k in range(1, KW):
                conv = conv + taps_ref[k : k + 1] * shift(k)
            xs = (conv * jax.nn.sigmoid(conv)).astype(BF)
            xs_o[0] = xs
            cums = cum_ref[0]
            last = cums[rows - 1 : rows] if b == 0 else cums[0:1]
            towards = jnp.exp(last - cums) * step_ref[0]
            bm = bc_ref[0].astype(F32)
            for h in range(heads):
                weighted = (bm * towards[:, h : h + 1]).astype(BF)
                end_o[0, h] = dot(weighted, xs[:, h * 128 : h * 128 + 128], ((0,), (0,)))

        for b in range(2):
            pl.when(pl.program_id(0) == b)(lambda b=b: branch(b))

    by = lambda *shape: pl.BlockSpec((1, *shape), lambda b: (b,) + (0,) * len(shape))
    return pl.pallas_call(
        kernel,
        grid=(2,),
        in_specs=[
            by(rows, inner),
            by(8, inner),
            pl.BlockSpec(taps.shape, lambda b: (0, 0)),
            by(rows, 128),
            by(rows, 128),
            by(rows, 128),
        ],
        out_specs=[by(rows, inner), by(heads, 128, 128)],
        out_shape=[
            jax.ShapeDtypeStruct((2, rows, inner), BF),
            jax.ShapeDtypeStruct((2, heads, 128, 128), F32),
        ],
        compiler_params=params(24),
        cost_estimate=cost(10**9, 3 * 2**20),
        name="conv_states",
    )(value, halo, taps, bc, step, cum)


def within_shard(xs, bc, step_t, cum_t, cum, skip):
    _, rows, inner = xs.shape
    heads = inner // 128
    half = rows // 2

    def kernel(x_ref, bc_ref, st_ref, ct_ref, cum_ref, skip_ref, y_ref):
        h = pl.program_id(1)
        lane = lax.broadcasted_iota(jnp.int32, (1, 128), 1)
        pick = lane == h
        cum_col = jnp.sum(jnp.where(pick, cum_ref[0], 0.0), axis=1, keepdims=True)
        gain = jnp.sum(jnp.where(pick, skip_ref[...], 0.0), axis=1, keepdims=True)
        cum_row = ct_ref[0, pl.ds(h, 1), :]
        step_row = st_ref[0, pl.ds(h, 1), :]
        lower = lax.broadcasted_iota(jnp.int32, (half, half), 0) >= lax.broadcasted_iota(
            jnp.int32, (half, half), 1
        )
        upper = lax.broadcasted_iota(jnp.int32, (half, half), 0) <= lax.broadcasted_iota(
            jnp.int32, (half, half), 1
        )

        def part(t, s, mask):
            ts, ss = slice(t * half, t * half + half), slice(s * half, s * half + half)
            gap = jnp.minimum(cum_col[ts] - cum_row[:, ss], 0.0)
            w = jnp.exp(gap)
            if mask is not None:
                w = jnp.where(mask, w, 0.0)
            scores = dot(bc_ref[0, ts, 128:], bc_ref[0, ss, :128], ((1,), (1,)))
            mixing = (w * scores * step_row[:, ss]).astype(BF)
            return dot(mixing, x_ref[0, ss, :])

        def branch(b):
            early, late = (0, 1) if b == 0 else (1, 0)
            mask = lower if b == 0 else upper
            for t, y in (
                (early, part(early, early, mask)),
                (late, part(late, late, mask) + part(late, early, None)),
            ):
                ts = slice(t * half, t * half + half)
                y_ref[0, ts, :] = y + gain * x_ref[0, ts, :].astype(F32)

        for b in range(2):
            pl.when(pl.program_id(0) == b)(lambda b=b: branch(b))

    by = lambda *shape: pl.BlockSpec((1, *shape), lambda b, h: (b,) + (0,) * len(shape))
    head = pl.BlockSpec((1, rows, 128), lambda b, h: (b, 0, h))
    return pl.pallas_call(
        kernel,
        grid=(2, heads),
        in_specs=[
            head,
            by(rows, 256),
            by(8, rows),
            by(8, rows),
            by(rows, 128),
            pl.BlockSpec((1, 128), lambda b, h: (0, 0)),
        ],
        out_specs=head,
        out_shape=jax.ShapeDtypeStruct((2, rows, inner), F32),
        compiler_params=params(),
        cost_estimate=cost(4 * 10**9, 4 * 2**20),
        name="within_shard",
    )(xs, bc, step_t, cum_t, cum, skip)


def finish(local_y, incoming, bc, cum, gate, norm_gain):
    _, rows, inner = local_y.shape
    heads = inner // 128

    def kernel(y_ref, s_ref, bc_ref, cum_ref, g_ref, gain_ref, o_ref):
        h = pl.program_id(1)
        lane = lax.broadcasted_iota(jnp.int32, (1, 128), 1)
        cum_col = jnp.sum(jnp.where(lane == h, cum_ref[0], 0.0), axis=1, keepdims=True)
        entering = dot(bc_ref[0], s_ref[0, 0])
        y = y_ref[0] + jnp.exp(cum_col) * entering
        g = g_ref[0].astype(F32)
        gated = y * (g * jax.nn.sigmoid(g))
        scale = lax.rsqrt(jnp.mean(gated * gated, axis=-1, keepdims=True) + 1e-05)
        o_ref[...] = (gated * scale * gain_ref[...]).astype(BF)

    by = lambda *shape: pl.BlockSpec((1, *shape), lambda b, h: (b,) + (0,) * len(shape))
    head = pl.BlockSpec((1, rows, 128), lambda b, h: (b, 0, h))
    return pl.pallas_call(
        kernel,
        grid=(2, heads),
        in_specs=[
            head,
            pl.BlockSpec((1, 1, 128, 128), lambda b, h: (b, h, 0, 0)),
            pl.BlockSpec((1, rows, 128), lambda b, h: (b, 0, 1)),
            by(rows, 128),
            head,
            pl.BlockSpec((1, 128), lambda b, h: (0, h)),
        ],
        out_specs=pl.BlockSpec((rows, 128), lambda b, h: (0, b * heads + h)),
        out_shape=jax.ShapeDtypeStruct((rows, 2 * inner), BF),
        compiler_params=params(),
        cost_estimate=cost(10**9, 5 * 2**20),
        name="finish",
    )(local_y, incoming, bc, cum, gate, norm_gain)


def output_table(comp, core, out_proj):
    inner, d = out_proj.shape
    r = 512
    nb = d // r
    tiles = inner // 128
    half = r // 2

    def kernel(idx, core_ref, o_ref, plain_keep, plain_send, perm_keep, perm_send, rows_f32, picked):
        i = pl.program_id(0)
        even = core_ref[0] == 0

        def put(keep, send, j, t):
            keep[:, 128 * j : 128 * j + 128] = jnp.where(even, t[:half], t[half:]).astype(BF)
            send[:, 128 * j : 128 * j + 128] = jnp.where(even, t[half:], t[:half]).astype(BF)

        @pl.when(i < nb)
        def _():
            r0 = pl.multiple_of(i * r * tiles, r * tiles)
            for j in range(tiles):
                t = o_ref[128 * j : 128 * j + 128, :].astype(F32).T
                rows_f32[pl.ds(r0 + j, r, tiles), :] = t
                put(plain_keep, plain_send, j, t)

        @pl.when(i >= nb)
        def _():
            b0 = (i - nb) * r

            def body(n, _):
                for k in range(16):
                    row = n * 16 + k
                    src = pl.multiple_of(idx[b0 + row] * tiles, tiles)
                    dst = pl.multiple_of(row * tiles, tiles)
                    picked[pl.ds(dst, tiles), :] = rows_f32[pl.ds(src, tiles), :]
                return 0

            lax.fori_loop(0, r // 16, body, 0)
            for j in range(tiles):
                put(perm_keep, perm_send, j, picked[pl.ds(j, r, tiles), :])

    early = pl.BlockSpec((half, inner), lambda i, s, c: (jnp.minimum(i, nb - 1), 0))
    late = pl.BlockSpec((half, inner), lambda i, s, c: (jnp.maximum(i - nb, 0), 0))
    return pl.pallas_call(
        kernel,
        grid_spec=pltpu.PrefetchScalarGridSpec(
            num_scalar_prefetch=2,
            grid=(2 * nb,),
            in_specs=[pl.BlockSpec((inner, r), lambda i, s, c: (0, jnp.minimum(i, nb - 1)))],
            out_specs=[early, early, late, late],
            scratch_shapes=[
                pltpu.VMEM((d * tiles, 128), F32),
                pltpu.VMEM((r * tiles, 128), F32),
            ],
        ),
        out_shape=[jax.ShapeDtypeStruct((d // 2, inner), BF)] * 4,
        compiler_params=params(24),
        cost_estimate=cost(8 * 10**9, 12 * 2**20),
        name="output_table",
    )(comp, core, out_proj)


def output_stage(order, mine, others, tables, added, out_dtype):
    rows, twice = mine.shape
    inner = twice // 2
    n = order.shape[0]
    cols = 256
    na = len(added)

    def kernel(idx, a, b, p0, q0, p1, q1, *rest):
        o_ref = rest[na]
        nt = ((1,), (1,))
        left = jnp.concatenate([a[...], b[...]], axis=1)
        table = jnp.concatenate([p0[...], q0[...], p1[...], q1[...]], axis=1)
        total = dot(left, table, nt)
        for place in range(n):
            mask = pl.program_id(0) == place
            for (at, _), ref in zip(added, rest[:na]):
                if at == place and n == 1:
                    total = total + ref[...].astype(F32)
                elif at == place:
                    total = total + jnp.where(mask, ref[...].astype(F32), 0.0)
        o_ref[0] = total.astype(out_dtype)

    table = pl.BlockSpec((cols, inner), lambda i, s: (s[i], 0))
    whole = lambda c: pl.BlockSpec((rows, c), lambda i, s: (0, 0))
    return pl.pallas_call(
        kernel,
        grid_spec=pltpu.PrefetchScalarGridSpec(
            num_scalar_prefetch=1,
            grid=(n,),
            in_specs=[whole(twice), whole(twice)] + [table] * 4 + [whole(cols)] * na,
            out_specs=pl.BlockSpec((1, rows, cols), lambda i, s: (i, 0, 0)),
        ),
        out_shape=jax.ShapeDtypeStruct((n, rows, cols), out_dtype),
        compiler_params=params(24),
        cost_estimate=cost(n * 4 * rows * twice * cols, n * 3 * 2**20),
        name="output_stage",
    )(order, mine, others, *tables, *[v for _, v in added])


def split(a):
    high = a.astype(BF)
    return high, (a - high.astype(F32)).astype(BF)


def join(high, low):
    return high.astype(F32) + low.astype(F32)


def halo_exchange(value, decay):
    rows = value.shape[1]
    fh, fl = split(decay)
    tail = jnp.stack([fh[0], fl[0], fh[1], fl[1]])
    tail = jnp.pad(tail, ((0, 1), (0, value.shape[2] - 128)))
    down = jnp.concatenate([value[0, rows - 3 :], tail], axis=0)
    up = jnp.concatenate([value[1, :3], tail], axis=0)
    from_below = lax.ppermute(down, "seq", [(i, i + 1) for i in range(7)])
    from_above = lax.ppermute(up, "seq", [(i + 1, i) for i in range(7)])
    return from_below, from_above


def shards(
    tokens,
    gate_proj,
    value_proj,
    state_proj,
    step_proj,
    step_bias,
    decay_rate,
    skip_gain,
    conv_kernel,
    norm_gain,
    out_proj,
    complement,
    keep_mask,
):
    rows, width = tokens.shape
    inner = gate_proj.shape[1]
    heads = step_proj.shape[1]
    d = gate_proj.shape[0]
    place = lax.axis_index("chan")
    core, chip = place % 2, place // 2
    y, x = chip // 4, chip % 4
    seq = lax.axis_index("seq")
    z, half = seq // 2, seq % 2

    core1 = core.reshape(1).astype(jnp.int32)

    def chip_at(dy, dx):
        return (y + dy) % 2 * 4 + (x + dx) % 4

    def lanes(a):
        return jnp.pad(a, (0, 128 - heads)).reshape(1, 128)

    own = tokens
    a = to_chip(own, 0, 1)
    b = to_chip(own, 0, -1)
    c = to_chip(own, 1, 0)
    own_s = to_sibling(own)
    a_s, b_s, c_s = to_sibling(a), to_sibling(b), to_sibling(c)
    dd = to_chip(a, 1, 0)
    e = to_chip(c, 0, -1)
    f = to_chip(a, 0, 1)
    g = to_chip(f, 1, 0)
    d_s, e_s, f_s = to_sibling(dd), to_sibling(e), to_sibling(f)
    g_s = to_sibling(g)
    parts = [
        (own, own_s, 0, 0),
        (a, a_s, 0, -1),
        (b, b_s, 0, 1),
        (c, c_s, 1, 0),
        (dd, d_s, 1, -1),
        (e, e_s, 1, 1),
        (f, f_s, 0, 2),
        (g, g_s, 1, 2),
    ]
    blocks, chans = [], []
    for block, sib, dy, dx in parts:
        blocks += [block, sib]
        chans += [2 * chip_at(dy, dx) + core, 2 * chip_at(dy, dx) + 1 - core]
    chans = jnp.stack(chans).astype(jnp.int32)
    value, gate, bc, step, cum, step_t, cum_t, decay = project(
        blocks,
        chans,
        complement,
        gate_proj,
        value_proj,
        state_proj,
        step_proj.T,
        lanes(step_bias),
        lanes(decay_rate),
    )
    comp_after, value = lax.optimization_barrier((complement, value))
    below, above = halo_exchange(value, decay)
    table = output_table(comp_after, core1, out_proj)
    below, above, *table = lax.optimization_barrier((below, above, *table))
    plain, plain_send, perm, perm_send = table
    tables = (plain, perm, to_sibling(plain_send), to_sibling(perm_send))
    zeros5 = jnp.zeros((5, inner), BF)
    halo = jnp.stack(
        [
            jnp.concatenate([zeros5, below[:3]], axis=0),
            jnp.concatenate([above[:3], zeros5], axis=0),
        ]
    )
    pair_msg = jnp.where(half == 0, above[3:7, :128], below[3:7, :128])
    pair = jnp.stack([join(pair_msg[0], pair_msg[1]), join(pair_msg[2], pair_msg[3])])
    xs, end = conv_states(value, halo, conv_kernel, bc, step, cum)

    d0 = jnp.where(half == 0, decay, pair)[:, :heads]
    d1 = jnp.where(half == 0, pair, decay)[:, :heads]

    def message(branch):
        parts = [*split(d0[branch]), *split(d1[branch])]
        rows4 = jnp.stack([jnp.pad(v, (0, 128 - heads)) for v in parts])
        rows4 = jnp.pad(rows4, ((0, 12), (0, 0)))
        return jnp.concatenate([end[branch].astype(BF).reshape(heads * 128, 128), rows4])

    msg_f, msg_b = message(0), message(1)
    got = []
    for k in range(1, 4):
        route = [(zz * 2 + hh, (zz + k) % 4 * 2 + hh) for zz in range(4) for hh in range(2)]
        got.append(lax.ppermute(jnp.where(z + k < 4, msg_f, msg_b), "seq", route))

    def opened(m):
        st = m[: heads * 128].astype(F32).reshape(heads, 128, 128)
        t = m[heads * 128 : heads * 128 + 4, :heads]
        return st, join(t[0], t[1]), join(t[2], t[3])

    opened_msgs = [opened(m) for m in got]
    wide = lambda v: v[:, None, None]

    def partial_sum(branch):
        total = jnp.zeros((heads, 128, 128), F32)
        passed = jnp.ones((heads,), F32)
        for j in range(1, 4):
            st, e0, e1 = opened_msgs[j - 1] if branch == 0 else opened_msgs[3 - j]
            valid = (z >= j) if branch == 0 else (z + j < 4)
            own_step = jnp.where(half == 0, e1, 1.0) if branch == 0 else jnp.where(half == 1, e0, 1.0)
            total = total + jnp.where(valid, wide(passed * own_step) * st, 0.0)
            passed = jnp.where(valid, passed * e0 * e1, passed)
        return total

    pf, pb = partial_sum(0), partial_sum(1)
    d0f, d1b = wide(d0[0]), wide(d1[1])
    send_f = jnp.where(half == 0, d0f * pf + end[0], pf)
    send_b = jnp.where(half == 1, d1b * pb + end[1], pb)
    recv = lax.ppermute(
        jnp.stack([send_f, send_b]).astype(BF), "seq", [(i, i ^ 1) for i in range(8)]
    ).astype(F32)
    in_f = jnp.where(half == 0, pf, d0f * pf) + recv[0]
    in_b = jnp.where(half == 1, pb, d1b * pb) + recv[1]
    incoming = jnp.stack([in_f, in_b]).astype(BF)

    local_y = within_shard(xs, bc, step_t, cum_t, cum, lanes(skip_gain))
    normed = finish(local_y, incoming, bc, cum, gate, norm_gain.reshape(1, inner))
    others = to_sibling(normed)

    def shares(offsets, added=(), out_dtype=BF):
        order = jnp.stack([chip_at(dy, dx) for dy, dx in offsets]).astype(jnp.int32)
        return output_stage(order, normed, others, tables, added, out_dtype)

    r = to_chip(shares([(1, 2)])[0], 1, 0)
    s_a = to_chip(shares([(1, 1)])[0], 1, 0)
    s_b = to_chip(shares([(1, -1)])[0], 0, -1)
    s_c = to_chip(shares([(0, 2)], [(0, r)])[0], 0, 1)
    t_b = to_chip(shares([(0, -1)])[0], 0, -1)
    here = shares([(0, 0)], out_dtype=F32)[0]
    t_c = to_chip(shares([(1, 0)], [(0, s_b)])[0], 1, 0)
    t_a = to_chip(shares([(0, 1)], [(0, s_a), (0, s_c)])[0], 0, 1)
    summed = here + t_a.astype(F32) + t_b.astype(F32) + t_c.astype(F32)
    return (summed * keep_mask.astype(F32) * (1.0 / 0.9)).astype(BF)


def solution(mesh):
    return jax.shard_map(
        shards,
        mesh=mesh,
        in_specs=(
            P("seq", "chan"),
            P(None, "chan"),
            P(None, "chan"),
            P(),
            P(None, "chan"),
            P("chan"),
            P("chan"),
            P("chan"),
            P(None, "chan"),
            P("chan"),
            P("chan", None),
            P(),
            P("seq", "chan"),
        ),
        out_specs=P("seq", "chan"),
        check_vma=False,
    )
```

time: 190 us -> 142 us (0.75)
  Pallas kernels: 107 us -> 58.9 us
  waiting for transfers between devices: 25.3 us -> 32 us
  local copies, waits for them, and re-layouts: 9.13 us -> 6.54 us
  starting transfers between devices: 41.1 us -> 39.1 us
    pallas_call x7 -> x1, Pallas kernels: 66.2 us -> 29 us  [project(): pl.pallas_call(kernel, grid_spec=pltpu.PrefetchScalarGridSpec(num_scalar_...]
    pallas_call x3 -> x8, Pallas kernels: 13.3 us -> 5.97 us  [output_stage(): pl.pallas_call(kernel, grid_spec=pltpu.PrefetchScalarGridSpec(num_scalar_...]
    dynamic_slice x2 -> x0, local copies, waits for them, and re-layouts: 4.67 us -> none  [shards(): lax.dynamic_index_in_dim(t.reshape(8, 2, 256, inner), 1 - core, 1, False)]
    pallas_call x1, Pallas kernels: 15.1 us -> 11.8 us  [output_table(): pl.pallas_call(kernel, grid_spec=pltpu.PrefetchScalarGridSpec(num_scalar_...]
    ppermute x3, starting transfers between devices: 8.73 us -> 5.49 us  [shards(): got.append(lax.ppermute(jnp.where(z + k < 4, msg_f, msg_b), 'seq', route))]
    concatenate x2 -> x1, other arithmetic: 2.68 us -> 0.01 us  [halo_exchange(): up = jnp.concatenate([value[1, :3], tail], axis=0)]
    ppermute x3, waiting for transfers between devices: 4.82 us -> 7.44 us  [shards(): got.append(lax.ppermute(jnp.where(z + k < 4, msg_f, msg_b), 'seq', route))]
    ppermute x18 -> x14, waiting for transfers between devices: 17.7 us -> 20 us  [to_chip(): return lax.ppermute(a, 'chan', chip_route(dy, dx))]
  transfers between devices with their start and end apart: 35 -> 31, of which waited for: 8 -> 13; matrix products, arithmetic and copies ran while one was open for 7% -> 3% of each run, Pallas kernels for 55% -> 19%
where the time goes in v2:
time: 142 us; the launch traced here: 141 us
  Pallas kernels  58.9 us (41%)
  starting transfers between devices  39.1 us (28%)
  waiting for transfers between devices  32 us (23%)
  local copies, waits for them, and re-layouts  6.54 us (5%)
  other arithmetic  4.06 us (3%)
    pallas_call x1, Pallas kernels, project(): pl.pallas_call(kernel, grid_spec=pltpu.PrefetchScalarGridSpec(num_scalar_...  29 us
    ppermute x14, starting transfers between devices, to_chip(): return lax.ppermute(a, 'chan', chip_route(dy, dx))  22.8 us
    ppermute x14, waiting for transfers between devices, to_chip(): return lax.ppermute(a, 'chan', chip_route(dy, dx))  20 us
    pallas_call x1, Pallas kernels, output_table(): pl.pallas_call(kernel, grid_spec=pltpu.PrefetchScalarGridSpec(num_scalar_...  11.8 us
    ppermute x3, waiting for transfers between devices, shards(): got.append(lax.ppermute(jnp.where(z + k < 4, msg_f, msg_b), 'seq', route))  7.44 us
    ppermute x1, starting transfers between devices, halo_exchange(): from_below = lax.ppermute(down, 'seq', [(i, i + 1) for i in range(7)])  6.05 us
    pallas_call x8, Pallas kernels, output_stage(): pl.pallas_call(kernel, grid_spec=pltpu.PrefetchScalarGridSpec(num_scalar_...  5.97 us
    pallas_call x1, Pallas kernels, within_shard(): pl.pallas_call(kernel, grid=(2, heads), in_specs=[head, by(rows, 256), by...  5.84 us
  transfers between devices with their start and end apart: 31, of which 13 were waited for; matrix products, arithmetic and copies ran while one was open for 3% of the time, Pallas kernels for 19%

profile of v2, /device:TPU:0, one launch (start us, length us, event | category | flops | bytes accessed | tf_op | source)
XLA Modules:
  0.0 141.4 jit_solution(4037900060552600327)
XLA Ops:
  0.0 1.6 %collective-permute-start.1 = (bf16[512,256]{1,0:T(8,128)(2,1)}, bf16[512,256]{1,0:T(8,128)(2,1)S(1)}, u32[]{:S(2)}, u32[]{:S(2)}) collective-permute-start(bf16[512,256]{1,0:T(8,128)(2,1)} %refs_0_.1), channel_id=1, source_target_pairs={{0,2},{1,3},{2,4},{3,5},{4,6},{5,7},{6,0},{7,1},{8,10},{9,11},{10,... | collective-permute-start | bytes 786440 | tf_op jit(solution)/shard_map/ppermute | solution.py:23
  1.6 1.7 %collective-permute-start.3 = (bf16[512,256]{1,0:T(8,128)(2,1)}, bf16[512,256]{1,0:T(8,128)(2,1)S(1)}, u32[]{:S(2)}, u32[]{:S(2)}) collective-permute-start(bf16[512,256]{1,0:T(8,128)(2,1)} %refs_0_.1), channel_id=1, source_target_pairs={{0,6},{1,7},{2,0},{3,1},{4,2},{5,3},{6,4},{7,5},{8,14},{9,15},{10,... | collective-permute-start | bytes 786440 | tf_op jit(solution)/shard_map/ppermute | solution.py:23
  3.2 1.7 %collective-permute-start.5 = (bf16[512,256]{1,0:T(8,128)(2,1)}, bf16[512,256]{1,0:T(8,128)(2,1)S(1)}, u32[]{:S(2)}, u32[]{:S(2)}) collective-permute-start(bf16[512,256]{1,0:T(8,128)(2,1)} %refs_0_.1), channel_id=1, source_target_pairs={{0,8},{1,9},{2,10},{3,11},{4,12},{5,13},{6,14},{7,15},{8,0},{9,1},... | collective-permute-start | bytes 786440 | tf_op jit(solution)/shard_map/ppermute | solution.py:23
  4.9 4.5 %collective-permute-done.1.refs_2_ = bf16[512,256]{1,0:T(8,128)(2,1)S(1)} collective-permute-done((bf16[512,256]{1,0:T(8,128)(2,1)}, bf16[512,256]{1,0:T(8,128)(2,1)S(1)}, u32[]{:S(2)}, u32[]{:S(2)}) %collective-permute-start.1) | collective-permute-done | bytes 262176 | tf_op jit(solution)/shard_map/ppermute | solution.py:23
  9.8 1.7 %collective-permute-start.7 = (bf16[512,256]{1,0:T(8,128)(2,1)S(1)}, bf16[512,256]{1,0:T(8,128)(2,1)S(1)}, u32[]{:S(2)}, u32[]{:S(2)}) collective-permute-start(bf16[512,256]{1,0:T(8,128)(2,1)S(1)} %collective-permute-done.1.refs_2_), channel_id=1, source_target_pairs={{0,8},{1,9},{2,10},{3,11},{4,12},{5,13},{6,14},{7,15},{8,0},{9,1},... | collective-permute-start | bytes 786440 | tf_op jit(solution)/shard_map/ppermute | solution.py:23
  12.2 2.5 %collective-permute-start.9 = (bf16[512,256]{1,0:T(8,128)(2,1)S(1)}, bf16[512,256]{1,0:T(8,128)(2,1)S(1)}, u32[]{:S(2)}, u32[]{:S(2)}) collective-permute-start(bf16[512,256]{1,0:T(8,128)(2,1)S(1)} %collective-permute-done.5.refs_6_), channel_id=1, source_target_pairs={{0,6},{1,7},{2,0},{3,1},{4,2},{5,3},{6,4},{7,5},{8,14},{9,15},{10,... | collective-permute-start | bytes 786440 | tf_op jit(solution)/shard_map/ppermute | solution.py:23
  14.6 3.0 %collective-permute-done.11.refs_12_ = bf16[512,256]{1,0:T(8,128)(2,1)S(1)} collective-permute-done((bf16[512,256]{1,0:T(8,128)(2,1)S(1)}, bf16[512,256]{1,0:T(8,128)(2,1)S(1)}, u32[]{:S(2)}, u32[]{:S(2)}) %collective-permute-start.11) | collective-permute-done | bytes 262176 | tf_op jit(solution)/shard_map/ppermute | solution.py:23
  17.6 1.9 %collective-permute-start.13 = (bf16[512,256]{1,0:T(8,128)(2,1)S(1)}, bf16[512,256]{1,0:T(8,128)(2,1)S(1)}, u32[]{:S(2)}, u32[]{:S(2)}) collective-permute-start(bf16[512,256]{1,0:T(8,128)(2,1)S(1)} %collective-permute-done.11.refs_12_), channel_id=1, source_target_pairs={{0,8},{1,9},{2,10},{3,11},{4,12},{5,13},{6,14},{7,15},{8,0},{9,1},... | collective-permute-start | bytes 786440 | tf_op jit(solution)/shard_map/ppermute | solution.py:23
  19.5 1.3 pad_bitcast_fusion.10
  21.9 2.3 %collective-permute-done.13.refs_14_ = bf16[512,256]{1,0:T(8,128)(2,1)S(1)} collective-permute-done((bf16[512,256]{1,0:T(8,128)(2,1)S(1)}, bf16[512,256]{1,0:T(8,128)(2,1)S(1)}, u32[]{:S(2)}, u32[]{:S(2)}) %collective-permute-start.13) | collective-permute-done | bytes 262176 | tf_op jit(solution)/shard_map/ppermute | solution.py:23
  24.9 0.7 stack.151.chan
  25.6 1.3 broadcast_multiply_fusion.idx
  27.8 29.0 %project.1 = (bf16[2,512,512]{2,1,0:T(8,128)(2,1)}, bf16[2,512,512]{2,1,0:T(8,128)(2,1)}, bf16[2,512,256]{2,1,0:T(8,128)(2,1)}, f32[2,512,128]{2,1,0:T(8,128)}, ...) custom-call(s32[16]{0:T(128)} %stack.151.chan, ...), custom_call_target="tpu_custom_call" | custom-call | flops 12884901888 | bytes 20971520 | tf_op jit(solution)/shard_map/project/pallas_call | solution.py:138
  56.8 0.7 subtract_convert_fusion
  57.5 0.7 slice_bitcast_fusion
  58.2 1.3 collective-permute-start.16
  59.5 6.1 %collective-permute-start.15 = (bf16[8,512]{1,0:T(8,128)(2,1)S(1)}, bf16[8,512]{1,0:T(8,128)(2,1)S(1)}, u32[]{:S(2)}, u32[]{:S(2)}) collective-permute-start(bf16[8,512]{1,0:T(8,128)(2,1)S(1)} %get-tuple-element.64), channel_id=1, source_target_pairs={{0,16},{16,32},{32,48},{48,64},{64,80},{80,96},{96,112},{1,17},{17... | collective-permute-start | bytes 24584 | tf_op jit(solution)/shard_map/ppermute | solution.py:432
  65.6 2.2 %copy-done.6 = bf16[512,4096]{1,0:T(8,128)(2,1)S(1)} copy-done((bf16[512,4096]{1,0:T(8,128)(2,1)S(1)}, bf16[512,4096]{1,0:T(8,128)(2,1)}, u32[]{:S(2)}) %copy-start.6) | copy-done | bytes 4194328
  67.9 11.8 %output_table.1 = (bf16[2048,512]{1,0:T(8,128)(2,1)S(1)}, bf16[2048,512]{1,0:T(8,128)(2,1)S(1)}, bf16[2048,512]{1,0:T(8,128)(2,1)S(1)}, bf16[2048,512]{1,0:T(8,128)(2,1)S(1)}) custom-call(s32[4096]{0:T(1024)S(1)} %copy-done.3, s32[1]{0:T(128)} %bitcast.22.core_ref, bf16[512,4096]{1,0:T(8,128)(2,1)S(1)} %copy-done.6), custom_call_target="tpu_custom_call" | custom-call | flops 8000000000 | bytes 12582912 | tf_op jit(solution)/shard_map/output_table/pallas_call | solution.py:358
  80.0 2.9 %conv_states.1 = (bf16[2,512,512]{2,1,0:T(8,128)(2,1)S(1)}, f32[2,4,128,128]{3,2,1,0:T(8,128)S(1)}) custom-call(bf16[2,512,512]{2,1,0:T(8,128)(2,1)S(1)} %copy-done.5, bf16[2,8,512]{2,1,0:T(8,128)(2,1)S(1)} %pad_maximum_fusion.4.halo_ref, f32[4,512]{1,0:T(4,128)S(1)} %copy-done.7, bf16[2,512,256]{2,1,0:T(8,128)(2,1)S(1)} %copy-done.1, ...), custom_call_target="tpu_custom_call" | custom-call | flops 1000000000 | bytes 3145728 | tf_op jit(solution)/shard_map/conv_states/pallas_call | solution.py:195
  83.1 4.2 %collective-permute-start.19 = (bf16[528,128]{1,0:T(8,128)(2,1)S(1)}, bf16[528,128]{1,0:T(8,128)(2,1)S(1)}, u32[]{:S(2)}, u32[]{:S(2)}) collective-permute-start(bf16[528,128]{1,0:T(8,128)(2,1)S(1)} %get-tuple-element.60), channel_id=1, source_target_pairs={{0,96},{16,112},{32,0},{48,16},{64,32},{80,48},{96,64},{112,80},{1... | collective-permute-start | bytes 405512 | tf_op jit(solution)/shard_map/ppermute | solution.py:538
  87.3 1.3 collective-permute-start.17
  89.1 4.1 %collective-permute-done.19 = bf16[528,128]{1,0:T(8,128)(2,1)S(1)} collective-permute-done((bf16[528,128]{1,0:T(8,128)(2,1)S(1)}, bf16[528,128]{1,0:T(8,128)(2,1)S(1)}, u32[]{:S(2)}, u32[]{:S(2)}) %collective-permute-start.19) | collective-permute-done | bytes 135200 | tf_op jit(solution)/shard_map/ppermute | solution.py:538
  93.2 2.1 %collective-permute-done.18 = bf16[528,128]{1,0:T(8,128)(2,1)S(1)} collective-permute-done((bf16[528,128]{1,0:T(8,128)(2,1)S(1)}, bf16[528,128]{1,0:T(8,128)(2,1)S(1)}, u32[]{:S(2)}, u32[]{:S(2)}) %collective-permute-start.18) | collective-permute-done | bytes 135200 | tf_op jit(solution)/shard_map/ppermute | solution.py:538
  95.4 1.2 collective-permute-done.17
  97.1 1.7 %collective-permute-start.20 = (bf16[2,4,128,128]{3,2,1,0:T(8,128)(2,1)S(1)}, bf16[2,4,128,128]{3,2,1,0:T(8,128)(2,1)S(1)}, u32[]{:S(2)}, u32[]{:S(2)}) collective-permute-start(bf16[2,4,128,128]{3,2,1,0:T(8,128)(2,1)S(1)} %pad_maximum_fusion), channel_id=1, source_target_pairs={{0,16},{16,0},{32,48},{48,32},{64,80},{80,64},{96,112},{112,96},{1... | collective-permute-start | bytes 786440 | tf_op jit(solution)/shard_map/ppermute | solution.py:563
  98.8 5.8 %within_shard.1.y_ref = f32[2,512,512]{2,1,0:T(8,128)S(1)} custom-call(bf16[2,512,512]{2,1,0:T(8,128)(2,1)S(1)} %get-tuple-element.40.x_ref, bf16[2,512,256]{2,1,0:T(8,128)(2,1)S(1)} %copy-done.1, f32[2,8,512]{2,1,0:T(8,128)S(1)} %copy-done.9, f32[2,8,512]{2,1,0:T(8,128)S(1)} %copy-done.10, f32[2,512,128]{2,1,0:T(8,128)S(1)} %copy-done.2, ...), custom_call_target="tpu_custom_call" | custom-call | flops 4000000000 | bytes 4194304 | tf_op jit(solution)/shard_map/within_shard/pallas_call | solution.py:262
  104.7 1.9 %collective-permute-done.20 = bf16[2,4,128,128]{3,2,1,0:T(8,128)(2,1)S(1)} collective-permute-done((bf16[2,4,128,128]{3,2,1,0:T(8,128)(2,1)S(1)}, bf16[2,4,128,128]{3,2,1,0:T(8,128)(2,1)S(1)}, u32[]{:S(2)}, u32[]{:S(2)}) %collective-permute-start.20) | collective-permute-done | bytes 262176 | tf_op jit(solution)/shard_map/ppermute | solution.py:563
  107.1 3.5 %finish.1.a = bf16[512,1024]{1,0:T(8,128)(2,1)S(1)} custom-call(f32[2,512,512]{2,1,0:T(8,128)S(1)} %within_shard.1.y_ref, bf16[2,4,128,128]{3,2,1,0:T(8,128)(2,1)S(1)} %pad_maximum_fusion.1.s_ref, bf16[2,512,256]{2,1,0:T(8,128)(2,1)S(1)} %copy-done.1, f32[2,512,128]{2,1,0:T(8,128)S(1)} %copy-done.2, bf16[2,512,512]{2,1,0:T(8,128)(2,1)S(1)} %copy-done, ...), custom_call_target="tpu_custom_call" | custom-call | flops 1000000000 | bytes 5242880 | tf_op jit(solution)/shard_map/finish/pallas_call | solution.py:298
  110.7 2.6 %collective-permute-done.21.b = bf16[512,1024]{1,0:T(8,128)(2,1)S(1)} collective-permute-done((bf16[512,1024]{1,0:T(8,128)(2,1)S(1)}, bf16[512,1024]{1,0:T(8,128)(2,1)S(1)}, u32[]{:S(2)}, u32[]{:S(2)}) %collective-permute-start.21) | collective-permute-done | bytes 1048608 | tf_op jit(solution)/shard_map/ppermute | solution.py:27
  113.3 0.7 output_stage.10
  114.1 1.7 %collective-permute-start.25 = (bf16[512,256]{1,0:T(8,128)(2,1)S(1)}, bf16[512,256]{1,0:T(8,128)(2,1)S(1)}, u32[]{:S(2)}, u32[]{:S(2)}) collective-permute-start(bf16[512,256]{1,0:T(8,128)(2,1)S(1)} %bitcast.150), channel_id=1, source_target_pairs={{0,8},{1,9},{2,10},{3,11},{4,12},{5,13},{6,14},{7,15},{8,0},{9,1},... | collective-permute-start | bytes 786440 | tf_op jit(solution)/shard_map/ppermute | solution.py:23
  115.8 0.7 output_stage.14
  116.5 2.9 %collective-permute-start.29 = (bf16[512,256]{1,0:T(8,128)(2,1)S(1)}, bf16[512,256]{1,0:T(8,128)(2,1)S(1)}, u32[]{:S(2)}, u32[]{:S(2)}) collective-permute-start(bf16[512,256]{1,0:T(8,128)(2,1)S(1)} %bitcast.147), channel_id=1, source_target_pairs={{0,6},{1,7},{2,0},{3,1},{4,2},{5,3},{6,4},{7,5},{8,14},{9,15},{10,... | collective-permute-start | bytes 786440 | tf_op jit(solution)/shard_map/ppermute | solution.py:23
  119.4 0.7 output_stage.9
  120.7 1.9 %collective-permute-done.25.rest_0_ = bf16[512,256]{1,0:T(8,128)(2,1)S(1)} collective-permute-done((bf16[512,256]{1,0:T(8,128)(2,1)S(1)}, bf16[512,256]{1,0:T(8,128)(2,1)S(1)}, u32[]{:S(2)}, u32[]{:S(2)}) %collective-permute-start.25) | collective-permute-done | bytes 262176 | tf_op jit(solution)/shard_map/ppermute | solution.py:23
  122.6 0.7 output_stage.11
  123.3 2.2 %collective-permute-start.26 = (bf16[512,256]{1,0:T(8,128)(2,1)S(1)}, bf16[512,256]{1,0:T(8,128)(2,1)S(1)}, u32[]{:S(2)}, u32[]{:S(2)}) collective-permute-start(bf16[512,256]{1,0:T(8,128)(2,1)S(1)} %bitcast.148), channel_id=1, source_target_pairs={{0,2},{1,3},{2,4},{3,5},{4,6},{5,7},{6,0},{7,1},{8,10},{9,11},{10,... | collective-permute-start | bytes 786440 | tf_op jit(solution)/shard_map/ppermute | solution.py:23
  125.5 0.7 output_stage.13
  126.3 1.8 %collective-permute-start.28 = (bf16[512,256]{1,0:T(8,128)(2,1)S(1)}, bf16[512,256]{1,0:T(8,128)(2,1)S(1)}, u32[]{:S(2)}, u32[]{:S(2)}) collective-permute-start(bf16[512,256]{1,0:T(8,128)(2,1)S(1)} %bitcast.144), channel_id=1, source_target_pairs={{0,6},{1,7},{2,0},{3,1},{4,2},{5,3},{6,4},{7,5},{8,14},{9,15},{10,... | collective-permute-start | bytes 786440 | tf_op jit(solution)/shard_map/ppermute | solution.py:23
  128.1 0.7 output_stage.15
  128.8 2.0 %collective-permute-start.30 = (bf16[512,256]{1,0:T(8,128)(2,1)S(1)}, bf16[512,256]{1,0:T(8,128)(2,1)S(1)}, u32[]{:S(2)}, u32[]{:S(2)}) collective-permute-start(bf16[512,256]{1,0:T(8,128)(2,1)S(1)} %bitcast.145), channel_id=1, source_target_pairs={{0,8},{1,9},{2,10},{3,11},{4,12},{5,13},{6,14},{7,15},{8,0},{9,1},... | collective-permute-start | bytes 786440 | tf_op jit(solution)/shard_map/ppermute | solution.py:23
  130.9 1.2 collective-permute-done.26.rest_1_
  132.1 0.7 output_stage.12
  133.1 0.7 output_stage.8
  133.8 1.6 %collective-permute-done.30 = bf16[512,256]{1,0:T(8,128)(2,1)S(1)} collective-permute-done((bf16[512,256]{1,0:T(8,128)(2,1)S(1)}, bf16[512,256]{1,0:T(8,128)(2,1)S(1)}, u32[]{:S(2)}, u32[]{:S(2)}) %collective-permute-start.30) | collective-permute-done | bytes 262176 | tf_op jit(solution)/shard_map/ppermute | solution.py:23
  135.5 5.0 %collective-permute-done.27 = bf16[512,256]{1,0:T(8,128)(2,1)S(1)} collective-permute-done((bf16[512,256]{1,0:T(8,128)(2,1)S(1)}, bf16[512,256]{1,0:T(8,128)(2,1)S(1)}, u32[]{:S(2)}, u32[]{:S(2)}) %collective-permute-start.27) | collective-permute-done | bytes 262176 | tf_op jit(solution)/shard_map/ppermute | solution.py:23
  140.5 0.9 fusion.4
  (132 shorter events, 6.5 us)
Async XLA Ops:
  0.0 9.4 %collective-permute-start.1 = (bf16[512,256]{1,0:T(8,128)(2,1)}, bf16[512,256]{1,0:T(8,128)(2,1)S(1)}, u32[]{:S(2)}, u32[]{:S(2)}) collective-permute-start(bf16[512,256]{1,0:T(8,128)(2,1)} %refs_0_.1), channel_id=1, source_target_pairs={{0,2},{1,3},{2,4},{3,5},{4,6},{5,7},{6,0},{7,1},{8,10},{9,11},{10,... | collective-permute-start | bytes 786440 | tf_op jit(solution)/shard_map/ppermute | solution.py:23
  1.6 8.3 %collective-permute-start.3 = (bf16[512,256]{1,0:T(8,128)(2,1)}, bf16[512,256]{1,0:T(8,128)(2,1)S(1)}, u32[]{:S(2)}, u32[]{:S(2)}) collective-permute-start(bf16[512,256]{1,0:T(8,128)(2,1)} %refs_0_.1), channel_id=1, source_target_pairs={{0,6},{1,7},{2,0},{3,1},{4,2},{5,3},{6,4},{7,5},{8,14},{9,15},{10,... | collective-permute-start | bytes 786440 | tf_op jit(solution)/shard_map/ppermute | solution.py:23
  3.2 8.3 %collective-permute-start = (bf16[512,256]{1,0:T(8,128)(2,1)}, bf16[512,256]{1,0:T(8,128)(2,1)S(1)}, u32[]{:S(2)}, u32[]{:S(2)}) collective-permute-start(bf16[512,256]{1,0:T(8,128)(2,1)} %refs_0_.1), channel_id=1, source_target_pairs={{0,1},{1,0},{2,3},{3,2},{4,5},{5,4},{6,7},{7,6},{8,9},{9,8},{10,11... | collective-permute-start | bytes 786440 | tf_op jit(solution)/shard_map/ppermute | solution.py:27
  3.2 8.9 %collective-permute-start.5 = (bf16[512,256]{1,0:T(8,128)(2,1)}, bf16[512,256]{1,0:T(8,128)(2,1)S(1)}, u32[]{:S(2)}, u32[]{:S(2)}) collective-permute-start(bf16[512,256]{1,0:T(8,128)(2,1)} %refs_0_.1), channel_id=1, source_target_pairs={{0,8},{1,9},{2,10},{3,11},{4,12},{5,13},{6,14},{7,15},{8,0},{9,1},... | collective-permute-start | bytes 786440 | tf_op jit(solution)/shard_map/ppermute | solution.py:23
  9.4 17.6 %copy-start.14 = (bf16[512,256]{1,0:T(8,128)(2,1)}, bf16[512,256]{1,0:T(8,128)(2,1)S(1)}, u32[]{:S(2)}) copy-start(bf16[512,256]{1,0:T(8,128)(2,1)S(1)} %collective-permute-done.1.refs_2_) | copy-start | bytes 786436
  9.4 8.3 %collective-permute-start.11 = (bf16[512,256]{1,0:T(8,128)(2,1)S(1)}, bf16[512,256]{1,0:T(8,128)(2,1)S(1)}, u32[]{:S(2)}, u32[]{:S(2)}) collective-permute-start(bf16[512,256]{1,0:T(8,128)(2,1)S(1)} %collective-permute-done.1.refs_2_), channel_id=1, source_target_pairs={{0,2},{1,3},{2,4},{3,5},{4,6},{5,7},{6,0},{7,1},{8,10},{9,11},{10,... | collective-permute-start | bytes 786440 | tf_op jit(solution)/shard_map/ppermute | solution.py:23
  9.8 17.1 %copy-start.15 = (bf16[512,256]{1,0:T(8,128)(2,1)}, bf16[512,256]{1,0:T(8,128)(2,1)S(1)}, u32[]{:S(2)}) copy-start(bf16[512,256]{1,0:T(8,128)(2,1)S(1)} %collective-permute-done.3.refs_4_) | copy-start | bytes 786436
  9.8 10.9 %collective-permute-start.4 = (bf16[512,256]{1,0:T(8,128)(2,1)S(1)}, bf16[512,256]{1,0:T(8,128)(2,1)S(1)}, u32[]{:S(2)}, u32[]{:S(2)}) collective-permute-start(bf16[512,256]{1,0:T(8,128)(2,1)S(1)} %collective-permute-done.3.refs_4_), channel_id=1, source_target_pairs={{0,1},{1,0},{2,3},{3,2},{4,5},{5,4},{6,7},{7,6},{8,9},{9,8},{10,11... | collective-permute-start | bytes 786440 | tf_op jit(solution)/shard_map/ppermute | solution.py:27
  9.8 11.0 %collective-permute-start.7 = (bf16[512,256]{1,0:T(8,128)(2,1)S(1)}, bf16[512,256]{1,0:T(8,128)(2,1)S(1)}, u32[]{:S(2)}, u32[]{:S(2)}) collective-permute-start(bf16[512,256]{1,0:T(8,128)(2,1)S(1)} %collective-permute-done.1.refs_2_), channel_id=1, source_target_pairs={{0,8},{1,9},{2,10},{3,11},{4,12},{5,13},{6,14},{7,15},{8,0},{9,1},... | collective-permute-start | bytes 786440 | tf_op jit(solution)/shard_map/ppermute | solution.py:23
  11.5 15.4 %copy-start.16 = (bf16[512,256]{1,0:T(8,128)(2,1)}, bf16[512,256]{1,0:T(8,128)(2,1)S(1)}, u32[]{:S(2)}) copy-start(bf16[512,256]{1,0:T(8,128)(2,1)S(1)} %collective-permute-done.refs_1_) | copy-start | bytes 786436
  11.5 9.9 %collective-permute-start.2 = (bf16[512,256]{1,0:T(8,128)(2,1)S(1)}, bf16[512,256]{1,0:T(8,128)(2,1)S(1)}, u32[]{:S(2)}, u32[]{:S(2)}) collective-permute-start(bf16[512,256]{1,0:T(8,128)(2,1)S(1)} %collective-permute-done.1.refs_2_), channel_id=1, source_target_pairs={{0,1},{1,0},{2,3},{3,2},{4,5},{5,4},{6,7},{7,6},{8,9},{9,8},{10,11... | collective-permute-start | bytes 786440 | tf_op jit(solution)/shard_map/ppermute | solution.py:27
  12.2 14.8 %copy-start.17 = (bf16[512,256]{1,0:T(8,128)(2,1)}, bf16[512,256]{1,0:T(8,128)(2,1)S(1)}, u32[]{:S(2)}) copy-start(bf16[512,256]{1,0:T(8,128)(2,1)S(1)} %collective-permute-done.5.refs_6_) | copy-start | bytes 786436
  12.2 9.3 %collective-permute-start.9 = (bf16[512,256]{1,0:T(8,128)(2,1)S(1)}, bf16[512,256]{1,0:T(8,128)(2,1)S(1)}, u32[]{:S(2)}, u32[]{:S(2)}) collective-permute-start(bf16[512,256]{1,0:T(8,128)(2,1)S(1)} %collective-permute-done.5.refs_6_), channel_id=1, source_target_pairs={{0,6},{1,7},{2,0},{3,1},{4,2},{5,3},{6,4},{7,5},{8,14},{9,15},{10,... | collective-permute-start | bytes 786440 | tf_op jit(solution)/shard_map/ppermute | solution.py:23
  17.6 9.4 %copy-start.18 = (bf16[512,256]{1,0:T(8,128)(2,1)}, bf16[512,256]{1,0:T(8,128)(2,1)S(1)}, u32[]{:S(2)}) copy-start(bf16[512,256]{1,0:T(8,128)(2,1)S(1)} %collective-permute-done.11.refs_12_) | copy-start | bytes 786436
  17.6 6.6 %collective-permute-start.13 = (bf16[512,256]{1,0:T(8,128)(2,1)S(1)}, bf16[512,256]{1,0:T(8,128)(2,1)S(1)}, u32[]{:S(2)}, u32[]{:S(2)}) collective-permute-start(bf16[512,256]{1,0:T(8,128)(2,1)S(1)} %collective-permute-done.11.refs_12_), channel_id=1, source_target_pairs={{0,8},{1,9},{2,10},{3,11},{4,12},{5,13},{6,14},{7,15},{8,0},{9,1},... | collective-permute-start | bytes 786440 | tf_op jit(solution)/shard_map/ppermute | solution.py:23
  20.8 6.2 %copy-start.19 = (bf16[512,256]{1,0:T(8,128)(2,1)}, bf16[512,256]{1,0:T(8,128)(2,1)S(1)}, u32[]{:S(2)}) copy-start(bf16[512,256]{1,0:T(8,128)(2,1)S(1)} %collective-permute-done.4.refs_5_) | copy-start | bytes 786436
  20.8 6.1 %collective-permute-start.6 = (bf16[512,256]{1,0:T(8,128)(2,1)S(1)}, bf16[512,256]{1,0:T(8,128)(2,1)S(1)}, u32[]{:S(2)}, u32[]{:S(2)}) collective-permute-start(bf16[512,256]{1,0:T(8,128)(2,1)S(1)} %collective-permute-done.5.refs_6_), channel_id=1, source_target_pairs={{0,1},{1,0},{2,3},{3,2},{4,5},{5,4},{6,7},{7,6},{8,9},{9,8},{10,11... | collective-permute-start | bytes 786440 | tf_op jit(solution)/shard_map/ppermute | solution.py:27
  20.9 6.0 %collective-permute-start.12 = (bf16[512,256]{1,0:T(8,128)(2,1)S(1)}, bf16[512,256]{1,0:T(8,128)(2,1)S(1)}, u32[]{:S(2)}, u32[]{:S(2)}) collective-permute-start(bf16[512,256]{1,0:T(8,128)(2,1)S(1)} %collective-permute-done.11.refs_12_), channel_id=1, source_target_pairs={{0,1},{1,0},{2,3},{3,2},{4,5},{5,4},{6,7},{7,6},{8,9},{9,8},{10,11... | collective-permute-start | bytes 786440 | tf_op jit(solution)/shard_map/ppermute | solution.py:27
  21.4 5.5 %collective-permute-start.8 = (bf16[512,256]{1,0:T(8,128)(2,1)S(1)}, bf16[512,256]{1,0:T(8,128)(2,1)S(1)}, u32[]{:S(2)}, u32[]{:S(2)}) collective-permute-start(bf16[512,256]{1,0:T(8,128)(2,1)S(1)} %collective-permute-done.7.refs_8_), channel_id=1, source_target_pairs={{0,1},{1,0},{2,3},{3,2},{4,5},{5,4},{6,7},{7,6},{8,9},{9,8},{10,11... | collective-permute-start | bytes 786440 | tf_op jit(solution)/shard_map/ppermute | solution.py:27
  21.5 5.4 %collective-permute-start.10 = (bf16[512,256]{1,0:T(8,128)(2,1)S(1)}, bf16[512,256]{1,0:T(8,128)(2,1)}, u32[]{:S(2)}, u32[]{:S(2)}) collective-permute-start(bf16[512,256]{1,0:T(8,128)(2,1)S(1)} %collective-permute-done.9.refs_10_), channel_id=1, source_target_pairs={{0,1},{1,0},{2,3},{3,2},{4,5},{5,4},{6,7},{7,6},{8,9},{9,8},{10,11... | collective-permute-start | bytes 786440 | tf_op jit(solution)/shard_map/ppermute | solution.py:27
  24.2 2.7 %collective-permute-start.14 = (bf16[512,256]{1,0:T(8,128)(2,1)S(1)}, bf16[512,256]{1,0:T(8,128)(2,1)}, u32[]{:S(2)}, u32[]{:S(2)}) collective-permute-start(bf16[512,256]{1,0:T(8,128)(2,1)S(1)} %collective-permute-done.13.refs_14_), channel_id=1, source_target_pairs={{0,1},{1,0},{2,3},{3,2},{4,5},{5,4},{6,7},{7,6},{8,9},{9,8},{10,11... | collective-permute-start | bytes 786440 | tf_op jit(solution)/shard_map/ppermute | solution.py:27
  27.8 37.8 %copy-start.3 = (s32[4096]{0:T(1024)S(1)}, s32[4096]{0:T(1024)}, u32[]{:S(2)}) copy-start(s32[4096]{0:T(1024)} %idx) | copy-start | bytes 49156
  58.2 21.4 %collective-permute-start.16 = (bf16[8,512]{1,0:T(8,128)(2,1)S(1)}, bf16[8,512]{1,0:T(8,128)(2,1)S(1)}, u32[]{:S(2)}, u32[]{:S(2)}) collective-permute-start(bf16[8,512]{1,0:T(8,128)(2,1)S(1)} %get-tuple-element.63), channel_id=1, source_target_pairs={{16,0},{32,16},{48,32},{64,48},{80,64},{96,80},{112,96},{17,1},{33... | collective-permute-start | bytes 24584 | tf_op jit(solution)/shard_map/ppermute | solution.py:433
  59.5 20.1 %collective-permute-start.15 = (bf16[8,512]{1,0:T(8,128)(2,1)S(1)}, bf16[8,512]{1,0:T(8,128)(2,1)S(1)}, u32[]{:S(2)}, u32[]{:S(2)}) collective-permute-start(bf16[8,512]{1,0:T(8,128)(2,1)S(1)} %get-tuple-element.64), channel_id=1, source_target_pairs={{0,16},{16,32},{32,48},{48,64},{64,80},{80,96},{96,112},{1,17},{17... | collective-permute-start | bytes 24584 | tf_op jit(solution)/shard_map/ppermute | solution.py:432
  67.8 11.9 %copy-start.12 = (f32[2,128]{1,0:T(2,128)S(1)}, f32[2,128]{1,0:T(2,128)}, u32[]{:S(2)}) copy-start(f32[2,128]{1,0:T(2,128)} %get-tuple-element.29) | copy-start | bytes 3076
  67.8 12.0 %copy-start.13 = (pred[8]{0:T(512)(128)(4,1)S(1)}, pred[8]{0:T(512)(128)(4,1)}, u32[]{:S(2)}) copy-start(pred[8]{0:T(512)(128)(4,1)} %constant.183.clone.1) | copy-start | bytes 28
  67.8 12.2 %copy-start.1 = (bf16[2,512,256]{2,1,0:T(8,128)(2,1)S(1)}, bf16[2,512,256]{2,1,0:T(8,128)(2,1)}, u32[]{:S(2)}) copy-start(bf16[2,512,256]{2,1,0:T(8,128)(2,1)} %get-tuple-element.37.bc_ref) | copy-start | bytes 1572868
  67.8 12.2 %copy-start.2 = (f32[2,512,128]{2,1,0:T(8,128)S(1)}, f32[2,512,128]{2,1,0:T(8,128)}, u32[]{:S(2)}) copy-start(f32[2,512,128]{2,1,0:T(8,128)} %get-tuple-element.39.cum_ref) | copy-start | bytes 1572868
  67.8 12.2 %copy-start.5 = (bf16[2,512,512]{2,1,0:T(8,128)(2,1)S(1)}, bf16[2,512,512]{2,1,0:T(8,128)(2,1)}, u32[]{:S(2)}) copy-start(bf16[2,512,512]{2,1,0:T(8,128)(2,1)} %get-tuple-element.28.v_ref) | copy-start | bytes 3145732
  67.8 12.2 %copy-start.7 = (f32[4,512]{1,0:T(4,128)S(1)}, f32[4,512]{1,0:T(4,128)}, u32[]{:S(2)}) copy-start(f32[4,512]{1,0:T(4,128)} %taps_ref.1) | copy-start | bytes 24580
  67.8 12.2 %copy-start.8 = (f32[2,512,128]{2,1,0:T(8,128)S(1)}, f32[2,512,128]{2,1,0:T(8,128)}, u32[]{:S(2)}) copy-start(f32[2,512,128]{2,1,0:T(8,128)} %get-tuple-element.38.step_ref) | copy-start | bytes 1572868
  82.9 15.9 %copy-start.9 = (f32[2,8,512]{2,1,0:T(8,128)S(1)}, f32[2,8,512]{2,1,0:T(8,128)}, u32[]{:S(2)}) copy-start(f32[2,8,512]{2,1,0:T(8,128)} %get-tuple-element.41.st_ref) | copy-start | bytes 98308
  82.9 15.9 %copy-start.10 = (f32[2,8,512]{2,1,0:T(8,128)S(1)}, f32[2,8,512]{2,1,0:T(8,128)}, u32[]{:S(2)}) copy-start(f32[2,8,512]{2,1,0:T(8,128)} %get-tuple-element.42.ct_ref) | copy-start | bytes 98308
  83.1 10.1 %collective-permute-start.19 = (bf16[528,128]{1,0:T(8,128)(2,1)S(1)}, bf16[528,128]{1,0:T(8,128)(2,1)S(1)}, u32[]{:S(2)}, u32[]{:S(2)}) collective-permute-start(bf16[528,128]{1,0:T(8,128)(2,1)S(1)} %get-tuple-element.60), channel_id=1, source_target_pairs={{0,96},{16,112},{32,0},{48,16},{64,32},{80,48},{96,64},{112,80},{1... | collective-permute-start | bytes 405512 | tf_op jit(solution)/shard_map/ppermute | solution.py:538
  87.3 8.0 %collective-permute-start.18 = (bf16[528,128]{1,0:T(8,128)(2,1)S(1)}, bf16[528,128]{1,0:T(8,128)(2,1)S(1)}, u32[]{:S(2)}, u32[]{:S(2)}) collective-permute-start(bf16[528,128]{1,0:T(8,128)(2,1)S(1)} %get-tuple-element.61), channel_id=1, source_target_pairs={{0,64},{16,80},{32,96},{48,112},{64,0},{80,16},{96,32},{112,48},{1... | collective-permute-start | bytes 405512 | tf_op jit(solution)/shard_map/ppermute | solution.py:538
  87.3 9.3 %collective-permute-start.17 = (bf16[528,128]{1,0:T(8,128)(2,1)S(1)}, bf16[528,128]{1,0:T(8,128)(2,1)S(1)}, u32[]{:S(2)}, u32[]{:S(2)}) collective-permute-start(bf16[528,128]{1,0:T(8,128)(2,1)S(1)} %get-tuple-element.62), channel_id=1, source_target_pairs={{0,32},{16,48},{32,64},{48,80},{64,96},{80,112},{96,0},{112,16},{1... | collective-permute-start | bytes 405512 | tf_op jit(solution)/shard_map/ppermute | solution.py:538
  88.6 24.7 %collective-permute-start.22 = (bf16[2048,512]{1,0:T(8,128)(2,1)S(1)}, bf16[2048,512]{1,0:T(8,128)(2,1)S(1)}, u32[]{:S(2)}, u32[]{:S(2)}) collective-permute-start(bf16[2048,512]{1,0:T(8,128)(2,1)S(1)} %get-tuple-element.47), channel_id=1, source_target_pairs={{0,1},{1,0},{2,3},{3,2},{4,5},{5,4},{6,7},{7,6},{8,9},{9,8},{10,11... | collective-permute-start | bytes 6291464 | tf_op jit(solution)/shard_map/ppermute | solution.py:27
  88.6 24.7 %collective-permute-start.23 = (bf16[2048,512]{1,0:T(8,128)(2,1)S(1)}, bf16[2048,512]{1,0:T(8,128)(2,1)S(1)}, u32[]{:S(2)}, u32[]{:S(2)}) collective-permute-start(bf16[2048,512]{1,0:T(8,128)(2,1)S(1)} %get-tuple-element.48), channel_id=1, source_target_pairs={{0,1},{1,0},{2,3},{3,2},{4,5},{5,4},{6,7},{7,6},{8,9},{9,8},{10,11... | collective-permute-start | bytes 6291464 | tf_op jit(solution)/shard_map/ppermute | solution.py:27
  97.1 9.5 %collective-permute-start.20 = (bf16[2,4,128,128]{3,2,1,0:T(8,128)(2,1)S(1)}, bf16[2,4,128,128]{3,2,1,0:T(8,128)(2,1)S(1)}, u32[]{:S(2)}, u32[]{:S(2)}) collective-permute-start(bf16[2,4,128,128]{3,2,1,0:T(8,128)(2,1)S(1)} %pad_maximum_fusion), channel_id=1, source_target_pairs={{0,16},{16,0},{32,48},{48,32},{64,80},{80,64},{96,112},{112,96},{1... | collective-permute-start | bytes 786440 | tf_op jit(solution)/shard_map/ppermute | solution.py:563
  110.6 2.7 %collective-permute-start.21 = (bf16[512,1024]{1,0:T(8,128)(2,1)S(1)}, bf16[512,1024]{1,0:T(8,128)(2,1)S(1)}, u32[]{:S(2)}, u32[]{:S(2)}) collective-permute-start(bf16[512,1024]{1,0:T(8,128)(2,1)S(1)} %finish.1.a), channel_id=1, source_target_pairs={{0,1},{1,0},{2,3},{3,2},{4,5},{5,4},{6,7},{7,6},{8,9},{9,8},{10,11... | collective-permute-start | bytes 3145736 | tf_op jit(solution)/shard_map/ppermute | solution.py:27
  114.1 8.5 %collective-permute-start.25 = (bf16[512,256]{1,0:T(8,128)(2,1)S(1)}, bf16[512,256]{1,0:T(8,128)(2,1)S(1)}, u32[]{:S(2)}, u32[]{:S(2)}) collective-permute-start(bf16[512,256]{1,0:T(8,128)(2,1)S(1)} %bitcast.150), channel_id=1, source_target_pairs={{0,8},{1,9},{2,10},{3,11},{4,12},{5,13},{6,14},{7,15},{8,0},{9,1},... | collective-permute-start | bytes 786440 | tf_op jit(solution)/shard_map/ppermute | solution.py:23
  116.5 11.6 %collective-permute-start.29 = (bf16[512,256]{1,0:T(8,128)(2,1)S(1)}, bf16[512,256]{1,0:T(8,128)(2,1)S(1)}, u32[]{:S(2)}, u32[]{:S(2)}) collective-permute-start(bf16[512,256]{1,0:T(8,128)(2,1)S(1)} %bitcast.147), channel_id=1, source_target_pairs={{0,6},{1,7},{2,0},{3,1},{4,2},{5,3},{6,4},{7,5},{8,14},{9,15},{10,... | collective-permute-start | bytes 786440 | tf_op jit(solution)/shard_map/ppermute | solution.py:23
  120.1 10.7 %collective-permute-start.24 = (bf16[512,256]{1,0:T(8,128)(2,1)S(1)}, bf16[512,256]{1,0:T(8,128)(2,1)S(1)}, u32[]{:S(2)}, u32[]{:S(2)}) collective-permute-start(bf16[512,256]{1,0:T(8,128)(2,1)S(1)} %bitcast.146), channel_id=1, source_target_pairs={{0,8},{1,9},{2,10},{3,11},{4,12},{5,13},{6,14},{7,15},{8,0},{9,1},... | collective-permute-start | bytes 786440 | tf_op jit(solution)/shard_map/ppermute | solution.py:23
  123.3 8.8 %collective-permute-start.26 = (bf16[512,256]{1,0:T(8,128)(2,1)S(1)}, bf16[512,256]{1,0:T(8,128)(2,1)S(1)}, u32[]{:S(2)}, u32[]{:S(2)}) collective-permute-start(bf16[512,256]{1,0:T(8,128)(2,1)S(1)} %bitcast.148), channel_id=1, source_target_pairs={{0,2},{1,3},{2,4},{3,5},{4,6},{5,7},{6,0},{7,1},{8,10},{9,11},{10,... | collective-permute-start | bytes 786440 | tf_op jit(solution)/shard_map/ppermute | solution.py:23
  126.3 7.5 %collective-permute-start.28 = (bf16[512,256]{1,0:T(8,128)(2,1)S(1)}, bf16[512,256]{1,0:T(8,128)(2,1)S(1)}, u32[]{:S(2)}, u32[]{:S(2)}) collective-permute-start(bf16[512,256]{1,0:T(8,128)(2,1)S(1)} %bitcast.144), channel_id=1, source_target_pairs={{0,6},{1,7},{2,0},{3,1},{4,2},{5,3},{6,4},{7,5},{8,14},{9,15},{10,... | collective-permute-start | bytes 786440 | tf_op jit(solution)/shard_map/ppermute | solution.py:23
  128.8 6.6 %collective-permute-start.30 = (bf16[512,256]{1,0:T(8,128)(2,1)S(1)}, bf16[512,256]{1,0:T(8,128)(2,1)S(1)}, u32[]{:S(2)}, u32[]{:S(2)}) collective-permute-start(bf16[512,256]{1,0:T(8,128)(2,1)S(1)} %bitcast.145), channel_id=1, source_target_pairs={{0,8},{1,9},{2,10},{3,11},{4,12},{5,13},{6,14},{7,15},{8,0},{9,1},... | collective-permute-start | bytes 786440 | tf_op jit(solution)/shard_map/ppermute | solution.py:23
  132.8 7.7 %collective-permute-start.27 = (bf16[512,256]{1,0:T(8,128)(2,1)S(1)}, bf16[512,256]{1,0:T(8,128)(2,1)S(1)}, u32[]{:S(2)}, u32[]{:S(2)}) collective-permute-start(bf16[512,256]{1,0:T(8,128)(2,1)S(1)} %bitcast.149), channel_id=1, source_target_pairs={{0,2},{1,3},{2,4},{3,5},{4,6},{5,7},{6,0},{7,1},{8,10},{9,11},{10,... | collective-permute-start | bytes 786440 | tf_op jit(solution)/shard_map/ppermute | solution.py:23
  133.0 7.4 %copy-start.11 = (s32[512,256]{1,0:T(8,128)S(1)}, s32[512,256]{1,0:T(8,128)}, u32[]{:S(2)}) copy-start(s32[512,256]{1,0:T(8,128)} %param.25) | copy-start | bytes 1572868
  (10 other events, 29.6 us)

commit v3 on v2

--- a/solution.py
+++ b/solution.py
@@ -41,7 +41,12 @@
     return pl.CostEstimate(flops=int(flops), bytes_accessed=int(nbytes), transcendentals=0)
 
 
-def project(blocks, chans, comp, gate_proj, value_proj, state_proj, step_t, bias, rate):
+def lanes(ref):
+    row = ref[...]
+    return jnp.concatenate([row, jnp.zeros((1, 128 - row.shape[1]), F32)], axis=1)
+
+
+def project(blocks, offsets, place, comp, gate_proj, value_proj, state_proj, step_t, bias, rate):
     nb = len(blocks)
     rows, width = blocks[0].shape
     d = comp.shape[0]
@@ -50,11 +55,12 @@
     heads = step_t.shape[0]
     tiles = rows // 128
 
-    def kernel(chan, idx, *refs):
+    def kernel(place_ref, idx, *refs):
+        chan = place_ref
         tok = refs[:nb]
         wg_hbm, wv_hbm, ws_hbm, st_ref, bias_ref, rate_ref = refs[nb : nb + 6]
-        v_out, g_out, bc_out, step_o, cum_o, step_to, cum_to, decay_o = refs[nb + 6 : nb + 14]
-        t, tp, by_row, picked, wg, wv, ws, sem, wsem = refs[nb + 14 :]
+        v_out, g_out, bc_out, step_o, cum_o, step_to, cum_to, decay_o, down_o, up_o = refs[nb + 6 : nb + 16]
+        t, tp, by_row, picked, wg, wv, ws, sem, wsem = refs[nb + 16 :]
 
         def token_copy(j, at):
             return pltpu.make_async_copy(tok[j], t.at[:, pl.ds(at, width)], sem.at[j])
@@ -84,7 +90,7 @@
             def body(n, _):
                 for k in range(32):
                     row = n * 32 + k
-                    src = pl.multiple_of(idx[b0 + row], tiles)
+                    src = pl.multiple_of(idx[b0 + row] * tiles, tiles)
                     dst = pl.multiple_of(row * tiles, tiles)
                     picked[pl.ds(dst, tiles), :] = by_row[pl.ds(src, tiles), :]
                 return 0
@@ -99,12 +105,13 @@
         weight_copies[0].wait()
         r = lax.broadcasted_iota(jnp.int32, (rows, rows), 0)
         q = lax.broadcasted_iota(jnp.int32, (rows, rows), 1)
+        decays = []
         for b, u in enumerate((t, tp)):
             small = dot(u[...], ws[...])
             bc_out[b] = small[:, :ns].astype(BF)
-            step = jax.nn.softplus(small[:, ns:] + bias_ref[...])
+            step = jax.nn.softplus(small[:, ns:] + lanes(bias_ref))
             tri = jnp.where((r >= q) if b == 0 else (r <= q), 1.0, 0.0).astype(BF)
-            logdec = -step * rate_ref[...]
+            logdec = -step * lanes(rate_ref)
             high = logdec.astype(BF)
             rest = logdec - high.astype(F32)
             mid = rest.astype(BF)
@@ -115,10 +122,19 @@
             cum_o[b] = cum
             step_to[b] = step.T[:8]
             cum_to[b] = cum.T[:8]
-            decay_o[b : b + 1] = jnp.exp(cum[rows - 1 : rows] if b == 0 else cum[0:1])
+            decay = jnp.exp(cum[rows - 1 : rows] if b == 0 else cum[0:1])
+            decay_o[b : b + 1] = decay
+            decays += [decay, decay - decay.astype(BF).astype(F32)]
         weight_copies[1].wait()
+        row8 = lax.broadcasted_iota(jnp.int32, (8, inner), 0)
         for b, u in enumerate((t, tp)):
-            v_out[b] = dot(u[...], wv[...]).astype(BF)
+            v = dot(u[...], wv[...])
+            v_out[b] = v.astype(BF)
+            message = pltpu.roll(v[rows - 8 :], 3, 0) if b == 0 else v[:8]
+            for i, part in enumerate(decays):
+                wide = jnp.concatenate([part, jnp.zeros((1, inner - 128), F32)], axis=1)
+                message = jnp.where(row8 == 3 + i, wide, message)
+            (down_o if b == 0 else up_o)[...] = message.astype(BF)
         weight_copies[2].wait()
         for b, u in enumerate((t, tp)):
             g_out[b] = dot(u[...], wg[...]).astype(BF)
@@ -132,6 +148,8 @@
         jax.ShapeDtypeStruct((2, 8, rows), F32),
         jax.ShapeDtypeStruct((2, 8, rows), F32),
         jax.ShapeDtypeStruct((2, 128), F32),
+        jax.ShapeDtypeStruct((8, inner), BF),
+        jax.ShapeDtypeStruct((8, inner), BF),
     ]
     whole = lambda shape: pl.BlockSpec(shape, lambda n, s, i: (0,) * len(shape))
     any_spec = pl.BlockSpec(memory_space=pl.ANY)
@@ -140,7 +158,7 @@
         grid_spec=pltpu.PrefetchScalarGridSpec(
             num_scalar_prefetch=2,
             grid=(1,),
-            in_specs=[any_spec] * (nb + 3) + [whole((heads, d)), whole((1, 128)), whole((1, 128))],
+            in_specs=[any_spec] * (nb + 3) + [whole((heads, d)), whole((1, heads)), whole((1, heads))],
             out_specs=[whole(o.shape) for o in shapes],
             scratch_shapes=[
                 pltpu.VMEM((rows, d), BF),
@@ -158,22 +176,21 @@
         compiler_params=params(60),
         cost_estimate=cost(4 * rows * d * (2 * inner + 512), 20 * 2**20),
         name="project",
-    )(chans, comp * tiles, *blocks, gate_proj, value_proj, state_proj, step_t, bias, rate)
-
-
-def conv_states(value, halo, taps, bc, step, cum):
+    )(place, comp, *blocks, gate_proj, value_proj, state_proj, step_t, bias, rate)
+
+
+def conv_states(value, below, above, taps, bc, step, cum):
     _, rows, inner = value.shape
     heads = inner // 128
 
-    def kernel(v_ref, halo_ref, taps_ref, bc_ref, step_ref, cum_ref, xs_o, end_o):
+    def kernel(v_ref, below_ref, above_ref, taps_ref, bc_ref, step_ref, cum_ref, xs_o, end_o):
         def branch(b):
             v = v_ref[0].astype(F32)
-            hal = halo_ref[0].astype(F32)
             if b == 0:
-                padded = jnp.concatenate([hal, v], axis=0)
+                padded = jnp.concatenate([pltpu.roll(below_ref[...].astype(F32), 5, 0), v], axis=0)
                 shift = lambda k: padded[5 + k : 5 + k + rows]
             else:
-                padded = jnp.concatenate([v, hal], axis=0)
+                padded = jnp.concatenate([v, above_ref[...].astype(F32)], axis=0)
                 shift = lambda k: padded[3 - k : 3 - k + rows]
             conv = taps_ref[0:1] * shift(0)
             for k in range(1, KW):
@@ -197,7 +214,8 @@
         grid=(2,),
         in_specs=[
             by(rows, inner),
-            by(8, inner),
+            pl.BlockSpec((8, inner), lambda b: (0, 0)),
+            pl.BlockSpec((8, inner), lambda b: (0, 0)),
             pl.BlockSpec(taps.shape, lambda b: (0, 0)),
             by(rows, 128),
             by(rows, 128),
@@ -211,7 +229,7 @@
         compiler_params=params(24),
         cost_estimate=cost(10**9, 3 * 2**20),
         name="conv_states",
-    )(value, halo, taps, bc, step, cum)
+    )(value, below, above, taps, bc, step, cum)
 
 
 def within_shard(xs, bc, step_t, cum_t, cum, skip):
@@ -224,7 +242,7 @@
         lane = lax.broadcasted_iota(jnp.int32, (1, 128), 1)
         pick = lane == h
         cum_col = jnp.sum(jnp.where(pick, cum_ref[0], 0.0), axis=1, keepdims=True)
-        gain = jnp.sum(jnp.where(pick, skip_ref[...], 0.0), axis=1, keepdims=True)
+        gain = jnp.sum(jnp.where(pick, lanes(skip_ref), 0.0), axis=1, keepdims=True)
         cum_row = ct_ref[0, pl.ds(h, 1), :]
         step_row = st_ref[0, pl.ds(h, 1), :]
         lower = lax.broadcasted_iota(jnp.int32, (half, half), 0) >= lax.broadcasted_iota(
@@ -268,7 +286,7 @@
             by(8, rows),
             by(8, rows),
             by(rows, 128),
-            pl.BlockSpec((1, 128), lambda b, h: (0, 0)),
+            pl.BlockSpec((1, heads), lambda b, h: (0, 0)),
         ],
         out_specs=head,
         out_shape=jax.ShapeDtypeStruct((2, rows, inner), F32),
@@ -420,18 +438,6 @@
 
 def join(high, low):
     return high.astype(F32) + low.astype(F32)
-
-
-def halo_exchange(value, decay):
-    rows = value.shape[1]
-    fh, fl = split(decay)
-    tail = jnp.stack([fh[0], fl[0], fh[1], fl[1]])
-    tail = jnp.pad(tail, ((0, 1), (0, value.shape[2] - 128)))
-    down = jnp.concatenate([value[0, rows - 3 :], tail], axis=0)
-    up = jnp.concatenate([value[1, :3], tail], axis=0)
-    from_below = lax.ppermute(down, "seq", [(i, i + 1) for i in range(7)])
-    from_above = lax.ppermute(up, "seq", [(i + 1, i) for i in range(7)])
-    return from_below, from_above
 
 
 def shards(
@@ -464,9 +470,6 @@
     def chip_at(dy, dx):
         return (y + dy) % 2 * 4 + (x + dx) % 4
 
-    def lanes(a):
-        return jnp.pad(a, (0, 128 - heads)).reshape(1, 128)
-
     own = tokens
     a = to_chip(own, 0, 1)
     b = to_chip(own, 0, -1)
@@ -489,38 +492,32 @@
         (f, f_s, 0, 2),
         (g, g_s, 1, 2),
     ]
-    blocks, chans = [], []
+    blocks, offsets = [], []
     for block, sib, dy, dx in parts:
         blocks += [block, sib]
-        chans += [2 * chip_at(dy, dx) + core, 2 * chip_at(dy, dx) + 1 - core]
-    chans = jnp.stack(chans).astype(jnp.int32)
-    value, gate, bc, step, cum, step_t, cum_t, decay = project(
+        offsets += [(dy, dx, 0), (dy, dx, 1)]
+    value, gate, bc, step, cum, step_t, cum_t, decay, down, up = project(
         blocks,
-        chans,
+        offsets,
+        jnp.stack([2 * chip_at(dy, dx) + (core + o) % 2 for dy, dx, o in offsets]).astype(jnp.int32),
         complement,
         gate_proj,
         value_proj,
         state_proj,
         step_proj.T,
-        lanes(step_bias),
-        lanes(decay_rate),
+        step_bias.reshape(1, heads),
+        decay_rate.reshape(1, heads),
     )
     comp_after, value = lax.optimization_barrier((complement, value))
-    below, above = halo_exchange(value, decay)
+    below = lax.ppermute(down, "seq", [(i, i + 1) for i in range(7)])
+    above = lax.ppermute(up, "seq", [(i + 1, i) for i in range(7)])
     table = output_table(comp_after, core1, out_proj)
     below, above, *table = lax.optimization_barrier((below, above, *table))
     plain, plain_send, perm, perm_send = table
     tables = (plain, perm, to_sibling(plain_send), to_sibling(perm_send))
-    zeros5 = jnp.zeros((5, inner), BF)
-    halo = jnp.stack(
-        [
-            jnp.concatenate([zeros5, below[:3]], axis=0),
-            jnp.concatenate([above[:3], zeros5], axis=0),
-        ]
-    )
     pair_msg = jnp.where(half == 0, above[3:7, :128], below[3:7, :128])
     pair = jnp.stack([join(pair_msg[0], pair_msg[1]), join(pair_msg[2], pair_msg[3])])
-    xs, end = conv_states(value, halo, conv_kernel, bc, step, cum)
+    xs, end = conv_states(value, below, above, conv_kernel, bc, step, cum)
 
     d0 = jnp.where(half == 0, decay, pair)[:, :heads]
     d1 = jnp.where(half == 0, pair, decay)[:, :heads]
@@ -567,7 +564,7 @@
     in_b = jnp.where(half == 1, pb, d1b * pb) + recv[1]
     incoming = jnp.stack([in_f, in_b]).astype(BF)
 
-    local_y = within_shard(xs, bc, step_t, cum_t, cum, lanes(skip_gain))
+    local_y = within_shard(xs, bc, step_t, cum_t, cum, skip_gain.reshape(1, heads))
     normed = finish(local_y, incoming, bc, cum, gate, norm_gain.reshape(1, inner))
     others = to_sibling(normed)
 

time: 142 us -> 140 us (0.986)
  local copies, waits for them, and re-layouts: 6.54 us -> 3.09 us
  other arithmetic: 4.06 us -> 1.95 us
  waiting for transfers between devices: 32 us -> 34 us
    reshape x2 -> x0, local copies, waits for them, and re-layouts: 1.91 us -> none  [lanes(): return jnp.pad(a, (0, 128 - heads)).reshape(1, 128)]
    ppermute x14, waiting for transfers between devices: 20 us -> 21.8 us  [to_chip(): return lax.ppermute(a, 'chan', chip_route(dy, dx))]
    ppermute x3, starting transfers between devices: 5.49 us -> 7.22 us  [shards(): got.append(lax.ppermute(jnp.where(z + k < 4, msg_f, msg_b), 'seq', route))]
  transfers between devices with their start and end apart: 31 -> 31, of which waited for: 13 -> 15; matrix products, arithmetic and copies ran while one was open for 3% -> 1% of each run, Pallas kernels for 19% -> 19%
where the time goes in v3:
time: 140 us
  Pallas kernels  59.9 us (43%)
  starting transfers between devices  40.1 us (29%)
  waiting for transfers between devices  34 us (24%)
  local copies, waits for them, and re-layouts  3.09 us (2%)
  other arithmetic  1.95 us (1%)
    pallas_call x1, Pallas kernels, project(): pl.pallas_call(kernel, grid_spec=pltpu.PrefetchScalarGridSpec(num_scalar_...  29.9 us
    ppermute x14, starting transfers between devices, to_chip(): return lax.ppermute(a, 'chan', chip_route(dy, dx))  22.6 us
    ppermute x14, waiting for transfers between devices, to_chip(): return lax.ppermute(a, 'chan', chip_route(dy, dx))  21.8 us
    pallas_call x1, Pallas kernels, output_table(): pl.pallas_call(kernel, grid_spec=pltpu.PrefetchScalarGridSpec(num_scalar_...  11.8 us
    ppermute x3, waiting for transfers between devices, shards(): got.append(lax.ppermute(jnp.where(z + k < 4, msg_f, msg_b), 'seq', route))  7.34 us
    ppermute x3, starting transfers between devices, shards(): got.append(lax.ppermute(jnp.where(z + k < 4, msg_f, msg_b), 'seq', route))  7.22 us
    pallas_call x8, Pallas kernels, output_stage(): pl.pallas_call(kernel, grid_spec=pltpu.PrefetchScalarGridSpec(num_scalar_...  5.97 us
    pallas_call x1, Pallas kernels, within_shard(): pl.pallas_call(kernel, grid=(2, heads), in_specs=[head, by(rows, 256), by...  5.86 us
  transfers between devices with their start and end apart: 31, of which 15 were waited for; matrix products, arithmetic and copies ran while one was open for 1% of the time, Pallas kernels for 19%

profile of v3, /device:TPU:0, one launch (start us, length us, event | category | flops | bytes accessed | tf_op | source)
XLA Modules:
  0.0 139.7 jit_solution(6139917074865110829)
XLA Ops:
  0.0 1.6 %collective-permute-start.1 = (bf16[512,256]{1,0:T(8,128)(2,1)}, bf16[512,256]{1,0:T(8,128)(2,1)S(1)}, u32[]{:S(2)}, u32[]{:S(2)}) collective-permute-start(bf16[512,256]{1,0:T(8,128)(2,1)} %refs_0_.1), channel_id=1, source_target_pairs={{0,2},{1,3},{2,4},{3,5},{4,6},{5,7},{6,0},{7,1},{8,10},{9,11},{10,... | collective-permute-start | bytes 786440 | tf_op jit(solution)/shard_map/ppermute | solution.py:23
  1.6 1.7 %collective-permute-start.3 = (bf16[512,256]{1,0:T(8,128)(2,1)}, bf16[512,256]{1,0:T(8,128)(2,1)S(1)}, u32[]{:S(2)}, u32[]{:S(2)}) collective-permute-start(bf16[512,256]{1,0:T(8,128)(2,1)} %refs_0_.1), channel_id=1, source_target_pairs={{0,6},{1,7},{2,0},{3,1},{4,2},{5,3},{6,4},{7,5},{8,14},{9,15},{10,... | collective-permute-start | bytes 786440 | tf_op jit(solution)/shard_map/ppermute | solution.py:23
  3.2 1.7 %collective-permute-start.5 = (bf16[512,256]{1,0:T(8,128)(2,1)}, bf16[512,256]{1,0:T(8,128)(2,1)S(1)}, u32[]{:S(2)}, u32[]{:S(2)}) collective-permute-start(bf16[512,256]{1,0:T(8,128)(2,1)} %refs_0_.1), channel_id=1, source_target_pairs={{0,8},{1,9},{2,10},{3,11},{4,12},{5,13},{6,14},{7,15},{8,0},{9,1},... | collective-permute-start | bytes 786440 | tf_op jit(solution)/shard_map/ppermute | solution.py:23
  4.9 4.5 %collective-permute-done.1.refs_2_ = bf16[512,256]{1,0:T(8,128)(2,1)S(1)} collective-permute-done((bf16[512,256]{1,0:T(8,128)(2,1)}, bf16[512,256]{1,0:T(8,128)(2,1)S(1)}, u32[]{:S(2)}, u32[]{:S(2)}) %collective-permute-start.1) | collective-permute-done | bytes 262176 | tf_op jit(solution)/shard_map/ppermute | solution.py:23
  9.8 1.7 %collective-permute-start.7 = (bf16[512,256]{1,0:T(8,128)(2,1)S(1)}, bf16[512,256]{1,0:T(8,128)(2,1)S(1)}, u32[]{:S(2)}, u32[]{:S(2)}) collective-permute-start(bf16[512,256]{1,0:T(8,128)(2,1)S(1)} %collective-permute-done.1.refs_2_), channel_id=1, source_target_pairs={{0,8},{1,9},{2,10},{3,11},{4,12},{5,13},{6,14},{7,15},{8,0},{9,1},... | collective-permute-start | bytes 786440 | tf_op jit(solution)/shard_map/ppermute | solution.py:23
  12.2 2.5 %collective-permute-start.9 = (bf16[512,256]{1,0:T(8,128)(2,1)S(1)}, bf16[512,256]{1,0:T(8,128)(2,1)S(1)}, u32[]{:S(2)}, u32[]{:S(2)}) collective-permute-start(bf16[512,256]{1,0:T(8,128)(2,1)S(1)} %collective-permute-done.5.refs_6_), channel_id=1, source_target_pairs={{0,6},{1,7},{2,0},{3,1},{4,2},{5,3},{6,4},{7,5},{8,14},{9,15},{10,... | collective-permute-start | bytes 786440 | tf_op jit(solution)/shard_map/ppermute | solution.py:23
  14.6 3.0 %collective-permute-done.11.refs_12_ = bf16[512,256]{1,0:T(8,128)(2,1)S(1)} collective-permute-done((bf16[512,256]{1,0:T(8,128)(2,1)S(1)}, bf16[512,256]{1,0:T(8,128)(2,1)S(1)}, u32[]{:S(2)}, u32[]{:S(2)}) %collective-permute-start.11) | collective-permute-done | bytes 262176 | tf_op jit(solution)/shard_map/ppermute | solution.py:23
  17.6 1.9 %collective-permute-start.13 = (bf16[512,256]{1,0:T(8,128)(2,1)S(1)}, bf16[512,256]{1,0:T(8,128)(2,1)S(1)}, u32[]{:S(2)}, u32[]{:S(2)}) collective-permute-start(bf16[512,256]{1,0:T(8,128)(2,1)S(1)} %collective-permute-done.11.refs_12_), channel_id=1, source_target_pairs={{0,8},{1,9},{2,10},{3,11},{4,12},{5,13},{6,14},{7,15},{8,0},{9,1},... | collective-permute-start | bytes 786440 | tf_op jit(solution)/shard_map/ppermute | solution.py:23
  20.1 0.6 collective-permute-done.9.refs_10_
  20.7 3.5 %collective-permute-done.13.refs_14_ = bf16[512,256]{1,0:T(8,128)(2,1)S(1)} collective-permute-done((bf16[512,256]{1,0:T(8,128)(2,1)S(1)}, bf16[512,256]{1,0:T(8,128)(2,1)S(1)}, u32[]{:S(2)}, u32[]{:S(2)}) %collective-permute-start.13) | collective-permute-done | bytes 262176 | tf_op jit(solution)/shard_map/ppermute | solution.py:23
  24.2 0.7 stack.139.place_ref
  24.9 0.9 collective-permute-done.14.refs_15_
  26.0 29.9 %project.1 = (bf16[2,512,512]{2,1,0:T(8,128)(2,1)}, bf16[2,512,512]{2,1,0:T(8,128)(2,1)}, bf16[2,512,256]{2,1,0:T(8,128)(2,1)}, f32[2,512,128]{2,1,0:T(8,128)}, ...) custom-call(s32[16]{0:T(128)} %stack.139.place_ref, ...), custom_call_target="tpu_custom_call" | custom-call | flops 12884901888 | bytes 20971520 | tf_op jit(solution)/shard_map/project/pallas_call | solution.py:156
  55.9 5.3 %collective-permute-start.15 = (bf16[8,512]{1,0:T(8,128)(2,1)}, bf16[8,512]{1,0:T(8,128)(2,1)S(1)}, u32[]{:S(2)}, u32[]{:S(2)}) collective-permute-start(bf16[8,512]{1,0:T(8,128)(2,1)} %get-tuple-element.31), channel_id=1, source_target_pairs={{0,16},{16,32},{32,48},{48,64},{64,80},{80,96},{96,112},{1,17},{17... | collective-permute-start | bytes 24584 | tf_op jit(solution)/shard_map/ppermute | solution.py:512
  61.2 1.3 collective-permute-start.16
  62.5 2.2 %copy-done.4 = bf16[512,4096]{1,0:T(8,128)(2,1)S(1)} copy-done((bf16[512,4096]{1,0:T(8,128)(2,1)S(1)}, bf16[512,4096]{1,0:T(8,128)(2,1)}, u32[]{:S(2)}) %copy-start.4) | copy-done | bytes 4194328
  64.7 11.8 %output_table.1 = (bf16[2048,512]{1,0:T(8,128)(2,1)S(1)}, bf16[2048,512]{1,0:T(8,128)(2,1)S(1)}, bf16[2048,512]{1,0:T(8,128)(2,1)S(1)}, bf16[2048,512]{1,0:T(8,128)(2,1)S(1)}) custom-call(s32[4096]{0:T(1024)S(1)} %copy-done.5, s32[1]{0:T(128)} %bitcast.20.core_ref, bf16[512,4096]{1,0:T(8,128)(2,1)S(1)} %copy-done.4), custom_call_target="tpu_custom_call" | custom-call | flops 8000000000 | bytes 12582912 | tf_op jit(solution)/shard_map/output_table/pallas_call | solution.py:376
  76.8 2.9 %conv_states.1 = (bf16[2,512,512]{2,1,0:T(8,128)(2,1)S(1)}, f32[2,4,128,128]{3,2,1,0:T(8,128)S(1)}) custom-call(bf16[2,512,512]{2,1,0:T(8,128)(2,1)S(1)} %copy-done.8, bf16[8,512]{1,0:T(8,128)(2,1)S(1)} %collective-permute-done.15.below_ref, bf16[8,512]{1,0:T(8,128)(2,1)S(1)} %collective-permute-done.16.above_ref, f32[4,512]{1,0:T(4,128)S(1)} %copy-done.6, ...), custom_call_target="tpu_custom_call" | custom-call | flops 1000000000 | bytes 3145728 | tf_op jit(solution)/shard_map/conv_states/pallas_call | solution.py:212
  79.9 5.9 %collective-permute-start.19 = (bf16[528,128]{1,0:T(8,128)(2,1)S(1)}, bf16[528,128]{1,0:T(8,128)(2,1)S(1)}, u32[]{:S(2)}, u32[]{:S(2)}) collective-permute-start(bf16[528,128]{1,0:T(8,128)(2,1)S(1)} %get-tuple-element.60), channel_id=1, source_target_pairs={{0,96},{16,112},{32,0},{48,16},{64,32},{80,48},{96,64},{112,80},{1... | collective-permute-start | bytes 405512 | tf_op jit(solution)/shard_map/ppermute | solution.py:535
  85.8 1.3 collective-permute-start.17
  87.1 0.5 collective-permute-start.23
  87.6 4.0 %collective-permute-done.19 = bf16[528,128]{1,0:T(8,128)(2,1)S(1)} collective-permute-done((bf16[528,128]{1,0:T(8,128)(2,1)S(1)}, bf16[528,128]{1,0:T(8,128)(2,1)S(1)}, u32[]{:S(2)}, u32[]{:S(2)}) %collective-permute-start.19) | collective-permute-done | bytes 135200 | tf_op jit(solution)/shard_map/ppermute | solution.py:535
  91.6 2.2 %collective-permute-done.18 = bf16[528,128]{1,0:T(8,128)(2,1)S(1)} collective-permute-done((bf16[528,128]{1,0:T(8,128)(2,1)S(1)}, bf16[528,128]{1,0:T(8,128)(2,1)S(1)}, u32[]{:S(2)}, u32[]{:S(2)}) %collective-permute-start.18) | collective-permute-done | bytes 135200 | tf_op jit(solution)/shard_map/ppermute | solution.py:535
  93.8 1.1 collective-permute-done.17
  95.5 2.4 %collective-permute-start.20 = (bf16[2,4,128,128]{3,2,1,0:T(8,128)(2,1)S(1)}, bf16[2,4,128,128]{3,2,1,0:T(8,128)(2,1)S(1)}, u32[]{:S(2)}, u32[]{:S(2)}) collective-permute-start(bf16[2,4,128,128]{3,2,1,0:T(8,128)(2,1)S(1)} %pad_maximum_fusion), channel_id=1, source_target_pairs={{0,16},{16,0},{32,48},{48,32},{64,80},{80,64},{96,112},{112,96},{1... | collective-permute-start | bytes 786440 | tf_op jit(solution)/shard_map/ppermute | solution.py:560
  97.9 5.9 %within_shard.1.y_ref = f32[2,512,512]{2,1,0:T(8,128)S(1)} custom-call(bf16[2,512,512]{2,1,0:T(8,128)(2,1)S(1)} %get-tuple-element.43.x_ref, bf16[2,512,256]{2,1,0:T(8,128)(2,1)S(1)} %copy-done.1, f32[2,8,512]{2,1,0:T(8,128)S(1)} %copy-done.10, f32[2,8,512]{2,1,0:T(8,128)S(1)} %copy-done.11, f32[2,512,128]{2,1,0:T(8,128)S(1)} %copy-done.2, f32[1,4]{1,0:T(1,128)S(1)} %bitcast.141), custom_call_target="tpu_custom_call" | custom-call | flops 4000000000 | bytes 4194304 | tf_op jit(solution)/shard_map/within_shard/pallas_call | solution.py:280
  103.8 1.2 collective-permute-done.20
  105.5 3.5 %finish.1.a = bf16[512,1024]{1,0:T(8,128)(2,1)S(1)} custom-call(f32[2,512,512]{2,1,0:T(8,128)S(1)} %within_shard.1.y_ref, bf16[2,4,128,128]{3,2,1,0:T(8,128)(2,1)S(1)} %pad_maximum_fusion.1.s_ref, bf16[2,512,256]{2,1,0:T(8,128)(2,1)S(1)} %copy-done.1, f32[2,512,128]{2,1,0:T(8,128)S(1)} %copy-done.2, bf16[2,512,512]{2,1,0:T(8,128)(2,1)S(1)} %copy-done, ...), custom_call_target="tpu_custom_call" | custom-call | flops 1000000000 | bytes 5242880 | tf_op jit(solution)/shard_map/finish/pallas_call | solution.py:316
  109.0 2.6 %collective-permute-done.21.b = bf16[512,1024]{1,0:T(8,128)(2,1)S(1)} collective-permute-done((bf16[512,1024]{1,0:T(8,128)(2,1)S(1)}, bf16[512,1024]{1,0:T(8,128)(2,1)S(1)}, u32[]{:S(2)}, u32[]{:S(2)}) %collective-permute-start.21) | collective-permute-done | bytes 1048608 | tf_op jit(solution)/shard_map/ppermute | solution.py:27
  111.7 0.7 output_stage.10
  112.5 1.7 %collective-permute-start.25 = (bf16[512,256]{1,0:T(8,128)(2,1)S(1)}, bf16[512,256]{1,0:T(8,128)(2,1)S(1)}, u32[]{:S(2)}, u32[]{:S(2)}) collective-permute-start(bf16[512,256]{1,0:T(8,128)(2,1)S(1)} %bitcast.139), channel_id=1, source_target_pairs={{0,8},{1,9},{2,10},{3,11},{4,12},{5,13},{6,14},{7,15},{8,0},{9,1},... | collective-permute-start | bytes 786440 | tf_op jit(solution)/shard_map/ppermute | solution.py:23
  114.1 0.7 output_stage.14
  114.9 2.9 %collective-permute-start.29 = (bf16[512,256]{1,0:T(8,128)(2,1)S(1)}, bf16[512,256]{1,0:T(8,128)(2,1)S(1)}, u32[]{:S(2)}, u32[]{:S(2)}) collective-permute-start(bf16[512,256]{1,0:T(8,128)(2,1)S(1)} %bitcast.136), channel_id=1, source_target_pairs={{0,6},{1,7},{2,0},{3,1},{4,2},{5,3},{6,4},{7,5},{8,14},{9,15},{10,... | collective-permute-start | bytes 786440 | tf_op jit(solution)/shard_map/ppermute | solution.py:23
  117.7 0.7 output_stage.9
  118.5 0.5 collective-permute-start.24
  119.0 2.0 %collective-permute-done.25.rest_0_ = bf16[512,256]{1,0:T(8,128)(2,1)S(1)} collective-permute-done((bf16[512,256]{1,0:T(8,128)(2,1)S(1)}, bf16[512,256]{1,0:T(8,128)(2,1)S(1)}, u32[]{:S(2)}, u32[]{:S(2)}) %collective-permute-start.25) | collective-permute-done | bytes 262176 | tf_op jit(solution)/shard_map/ppermute | solution.py:23
  121.0 0.7 output_stage.11
  121.7 2.1 %collective-permute-start.26 = (bf16[512,256]{1,0:T(8,128)(2,1)S(1)}, bf16[512,256]{1,0:T(8,128)(2,1)S(1)}, u32[]{:S(2)}, u32[]{:S(2)}) collective-permute-start(bf16[512,256]{1,0:T(8,128)(2,1)S(1)} %bitcast.137), channel_id=1, source_target_pairs={{0,2},{1,3},{2,4},{3,5},{4,6},{5,7},{6,0},{7,1},{8,10},{9,11},{10,... | collective-permute-start | bytes 786440 | tf_op jit(solution)/shard_map/ppermute | solution.py:23
  123.8 0.7 output_stage.13
  124.6 1.8 %collective-permute-start.28 = (bf16[512,256]{1,0:T(8,128)(2,1)S(1)}, bf16[512,256]{1,0:T(8,128)(2,1)S(1)}, u32[]{:S(2)}, u32[]{:S(2)}) collective-permute-start(bf16[512,256]{1,0:T(8,128)(2,1)S(1)} %bitcast.133), channel_id=1, source_target_pairs={{0,6},{1,7},{2,0},{3,1},{4,2},{5,3},{6,4},{7,5},{8,14},{9,15},{10,... | collective-permute-start | bytes 786440 | tf_op jit(solution)/shard_map/ppermute | solution.py:23
  126.4 0.7 output_stage.15
  127.2 2.1 %collective-permute-start.30 = (bf16[512,256]{1,0:T(8,128)(2,1)S(1)}, bf16[512,256]{1,0:T(8,128)(2,1)S(1)}, u32[]{:S(2)}, u32[]{:S(2)}) collective-permute-start(bf16[512,256]{1,0:T(8,128)(2,1)S(1)} %bitcast.134), channel_id=1, source_target_pairs={{0,8},{1,9},{2,10},{3,11},{4,12},{5,13},{6,14},{7,15},{8,0},{9,1},... | collective-permute-start | bytes 786440 | tf_op jit(solution)/shard_map/ppermute | solution.py:23
  129.2 1.2 collective-permute-done.26.rest_1_
  130.4 0.7 output_stage.12
  131.4 0.7 output_stage.8
  132.1 1.7 %collective-permute-done.30 = bf16[512,256]{1,0:T(8,128)(2,1)S(1)} collective-permute-done((bf16[512,256]{1,0:T(8,128)(2,1)S(1)}, bf16[512,256]{1,0:T(8,128)(2,1)S(1)}, u32[]{:S(2)}, u32[]{:S(2)}) %collective-permute-start.30) | collective-permute-done | bytes 262176 | tf_op jit(solution)/shard_map/ppermute | solution.py:23
  133.8 5.0 %collective-permute-done.27 = bf16[512,256]{1,0:T(8,128)(2,1)S(1)} collective-permute-done((bf16[512,256]{1,0:T(8,128)(2,1)S(1)}, bf16[512,256]{1,0:T(8,128)(2,1)S(1)}, u32[]{:S(2)}, u32[]{:S(2)}) %collective-permute-start.27) | collective-permute-done | bytes 262176 | tf_op jit(solution)/shard_map/ppermute | solution.py:23
  138.8 0.9 fusion.4
  (116 shorter events, 3.4 us)
Async XLA Ops:
  0.0 9.4 %collective-permute-start.1 = (bf16[512,256]{1,0:T(8,128)(2,1)}, bf16[512,256]{1,0:T(8,128)(2,1)S(1)}, u32[]{:S(2)}, u32[]{:S(2)}) collective-permute-start(bf16[512,256]{1,0:T(8,128)(2,1)} %refs_0_.1), channel_id=1, source_target_pairs={{0,2},{1,3},{2,4},{3,5},{4,6},{5,7},{6,0},{7,1},{8,10},{9,11},{10,... | collective-permute-start | bytes 786440 | tf_op jit(solution)/shard_map/ppermute | solution.py:23
  1.6 8.3 %collective-permute-start.3 = (bf16[512,256]{1,0:T(8,128)(2,1)}, bf16[512,256]{1,0:T(8,128)(2,1)S(1)}, u32[]{:S(2)}, u32[]{:S(2)}) collective-permute-start(bf16[512,256]{1,0:T(8,128)(2,1)} %refs_0_.1), channel_id=1, source_target_pairs={{0,6},{1,7},{2,0},{3,1},{4,2},{5,3},{6,4},{7,5},{8,14},{9,15},{10,... | collective-permute-start | bytes 786440 | tf_op jit(solution)/shard_map/ppermute | solution.py:23
  3.2 8.3 %collective-permute-start = (bf16[512,256]{1,0:T(8,128)(2,1)}, bf16[512,256]{1,0:T(8,128)(2,1)S(1)}, u32[]{:S(2)}, u32[]{:S(2)}) collective-permute-start(bf16[512,256]{1,0:T(8,128)(2,1)} %refs_0_.1), channel_id=1, source_target_pairs={{0,1},{1,0},{2,3},{3,2},{4,5},{5,4},{6,7},{7,6},{8,9},{9,8},{10,11... | collective-permute-start | bytes 786440 | tf_op jit(solution)/shard_map/ppermute | solution.py:27
  3.2 8.9 %collective-permute-start.5 = (bf16[512,256]{1,0:T(8,128)(2,1)}, bf16[512,256]{1,0:T(8,128)(2,1)S(1)}, u32[]{:S(2)}, u32[]{:S(2)}) collective-permute-start(bf16[512,256]{1,0:T(8,128)(2,1)} %refs_0_.1), channel_id=1, source_target_pairs={{0,8},{1,9},{2,10},{3,11},{4,12},{5,13},{6,14},{7,15},{8,0},{9,1},... | collective-permute-start | bytes 786440 | tf_op jit(solution)/shard_map/ppermute | solution.py:23
  9.4 16.5 %copy-start.14 = (bf16[512,256]{1,0:T(8,128)(2,1)}, bf16[512,256]{1,0:T(8,128)(2,1)S(1)}, u32[]{:S(2)}) copy-start(bf16[512,256]{1,0:T(8,128)(2,1)S(1)} %collective-permute-done.1.refs_2_) | copy-start | bytes 786436
  9.4 8.3 %collective-permute-start.11 = (bf16[512,256]{1,0:T(8,128)(2,1)S(1)}, bf16[512,256]{1,0:T(8,128)(2,1)S(1)}, u32[]{:S(2)}, u32[]{:S(2)}) collective-permute-start(bf16[512,256]{1,0:T(8,128)(2,1)S(1)} %collective-permute-done.1.refs_2_), channel_id=1, source_target_pairs={{0,2},{1,3},{2,4},{3,5},{4,6},{5,7},{6,0},{7,1},{8,10},{9,11},{10,... | collective-permute-start | bytes 786440 | tf_op jit(solution)/shard_map/ppermute | solution.py:23
  9.8 16.0 %copy-start.15 = (bf16[512,256]{1,0:T(8,128)(2,1)}, bf16[512,256]{1,0:T(8,128)(2,1)S(1)}, u32[]{:S(2)}) copy-start(bf16[512,256]{1,0:T(8,128)(2,1)S(1)} %collective-permute-done.3.refs_4_) | copy-start | bytes 786436
  9.8 9.7 %collective-permute-start.4 = (bf16[512,256]{1,0:T(8,128)(2,1)S(1)}, bf16[512,256]{1,0:T(8,128)(2,1)S(1)}, u32[]{:S(2)}, u32[]{:S(2)}) collective-permute-start(bf16[512,256]{1,0:T(8,128)(2,1)S(1)} %collective-permute-done.3.refs_4_), channel_id=1, source_target_pairs={{0,1},{1,0},{2,3},{3,2},{4,5},{5,4},{6,7},{7,6},{8,9},{9,8},{10,11... | collective-permute-start | bytes 786440 | tf_op jit(solution)/shard_map/ppermute | solution.py:27
  9.8 9.7 %collective-permute-start.7 = (bf16[512,256]{1,0:T(8,128)(2,1)S(1)}, bf16[512,256]{1,0:T(8,128)(2,1)S(1)}, u32[]{:S(2)}, u32[]{:S(2)}) collective-permute-start(bf16[512,256]{1,0:T(8,128)(2,1)S(1)} %collective-permute-done.1.refs_2_), channel_id=1, source_target_pairs={{0,8},{1,9},{2,10},{3,11},{4,12},{5,13},{6,14},{7,15},{8,0},{9,1},... | collective-permute-start | bytes 786440 | tf_op jit(solution)/shard_map/ppermute | solution.py:23
  11.5 14.4 %copy-start.16 = (bf16[512,256]{1,0:T(8,128)(2,1)}, bf16[512,256]{1,0:T(8,128)(2,1)S(1)}, u32[]{:S(2)}) copy-start(bf16[512,256]{1,0:T(8,128)(2,1)S(1)} %collective-permute-done.refs_1_) | copy-start | bytes 786436
  11.5 8.5 %collective-permute-start.2 = (bf16[512,256]{1,0:T(8,128)(2,1)S(1)}, bf16[512,256]{1,0:T(8,128)(2,1)S(1)}, u32[]{:S(2)}, u32[]{:S(2)}) collective-permute-start(bf16[512,256]{1,0:T(8,128)(2,1)S(1)} %collective-permute-done.1.refs_2_), channel_id=1, source_target_pairs={{0,1},{1,0},{2,3},{3,2},{4,5},{5,4},{6,7},{7,6},{8,9},{9,8},{10,11... | collective-permute-start | bytes 786440 | tf_op jit(solution)/shard_map/ppermute | solution.py:27
  12.2 13.7 %copy-start.17 = (bf16[512,256]{1,0:T(8,128)(2,1)}, bf16[512,256]{1,0:T(8,128)(2,1)S(1)}, u32[]{:S(2)}) copy-start(bf16[512,256]{1,0:T(8,128)(2,1)S(1)} %collective-permute-done.5.refs_6_) | copy-start | bytes 786436
  12.2 8.5 %collective-permute-start.9 = (bf16[512,256]{1,0:T(8,128)(2,1)S(1)}, bf16[512,256]{1,0:T(8,128)(2,1)S(1)}, u32[]{:S(2)}, u32[]{:S(2)}) collective-permute-start(bf16[512,256]{1,0:T(8,128)(2,1)S(1)} %collective-permute-done.5.refs_6_), channel_id=1, source_target_pairs={{0,6},{1,7},{2,0},{3,1},{4,2},{5,3},{6,4},{7,5},{8,14},{9,15},{10,... | collective-permute-start | bytes 786440 | tf_op jit(solution)/shard_map/ppermute | solution.py:23
  17.6 8.3 %copy-start.18 = (bf16[512,256]{1,0:T(8,128)(2,1)}, bf16[512,256]{1,0:T(8,128)(2,1)S(1)}, u32[]{:S(2)}) copy-start(bf16[512,256]{1,0:T(8,128)(2,1)S(1)} %collective-permute-done.11.refs_12_) | copy-start | bytes 786436
  17.6 6.6 %collective-permute-start.13 = (bf16[512,256]{1,0:T(8,128)(2,1)S(1)}, bf16[512,256]{1,0:T(8,128)(2,1)S(1)}, u32[]{:S(2)}, u32[]{:S(2)}) collective-permute-start(bf16[512,256]{1,0:T(8,128)(2,1)S(1)} %collective-permute-done.11.refs_12_), channel_id=1, source_target_pairs={{0,8},{1,9},{2,10},{3,11},{4,12},{5,13},{6,14},{7,15},{8,0},{9,1},... | collective-permute-start | bytes 786440 | tf_op jit(solution)/shard_map/ppermute | solution.py:23
  19.5 6.4 %copy-start.19 = (bf16[512,256]{1,0:T(8,128)(2,1)}, bf16[512,256]{1,0:T(8,128)(2,1)S(1)}, u32[]{:S(2)}) copy-start(bf16[512,256]{1,0:T(8,128)(2,1)S(1)} %collective-permute-done.4.refs_5_) | copy-start | bytes 786436
  19.5 5.4 %collective-permute-start.6 = (bf16[512,256]{1,0:T(8,128)(2,1)S(1)}, bf16[512,256]{1,0:T(8,128)(2,1)S(1)}, u32[]{:S(2)}, u32[]{:S(2)}) collective-permute-start(bf16[512,256]{1,0:T(8,128)(2,1)S(1)} %collective-permute-done.5.refs_6_), channel_id=1, source_target_pairs={{0,1},{1,0},{2,3},{3,2},{4,5},{5,4},{6,7},{7,6},{8,9},{9,8},{10,11... | collective-permute-start | bytes 786440 | tf_op jit(solution)/shard_map/ppermute | solution.py:27
  19.5 5.3 %collective-permute-start.12 = (bf16[512,256]{1,0:T(8,128)(2,1)S(1)}, bf16[512,256]{1,0:T(8,128)(2,1)S(1)}, u32[]{:S(2)}, u32[]{:S(2)}) collective-permute-start(bf16[512,256]{1,0:T(8,128)(2,1)S(1)} %collective-permute-done.11.refs_12_), channel_id=1, source_target_pairs={{0,1},{1,0},{2,3},{3,2},{4,5},{5,4},{6,7},{7,6},{8,9},{9,8},{10,11... | collective-permute-start | bytes 786440 | tf_op jit(solution)/shard_map/ppermute | solution.py:27
  20.0 4.9 %collective-permute-start.8 = (bf16[512,256]{1,0:T(8,128)(2,1)S(1)}, bf16[512,256]{1,0:T(8,128)(2,1)S(1)}, u32[]{:S(2)}, u32[]{:S(2)}) collective-permute-start(bf16[512,256]{1,0:T(8,128)(2,1)S(1)} %collective-permute-done.7.refs_8_), channel_id=1, source_target_pairs={{0,1},{1,0},{2,3},{3,2},{4,5},{5,4},{6,7},{7,6},{8,9},{9,8},{10,11... | collective-permute-start | bytes 786440 | tf_op jit(solution)/shard_map/ppermute | solution.py:27
  20.7 4.2 %collective-permute-start.10 = (bf16[512,256]{1,0:T(8,128)(2,1)S(1)}, bf16[512,256]{1,0:T(8,128)(2,1)}, u32[]{:S(2)}, u32[]{:S(2)}) collective-permute-start(bf16[512,256]{1,0:T(8,128)(2,1)S(1)} %collective-permute-done.9.refs_10_), channel_id=1, source_target_pairs={{0,1},{1,0},{2,3},{3,2},{4,5},{5,4},{6,7},{7,6},{8,9},{9,8},{10,11... | collective-permute-start | bytes 786440 | tf_op jit(solution)/shard_map/ppermute | solution.py:27
  24.2 1.7 %collective-permute-start.14 = (bf16[512,256]{1,0:T(8,128)(2,1)S(1)}, bf16[512,256]{1,0:T(8,128)(2,1)}, u32[]{:S(2)}, u32[]{:S(2)}) collective-permute-start(bf16[512,256]{1,0:T(8,128)(2,1)S(1)} %collective-permute-done.13.refs_14_), channel_id=1, source_target_pairs={{0,1},{1,0},{2,3},{3,2},{4,5},{5,4},{6,7},{7,6},{8,9},{9,8},{10,11... | collective-permute-start | bytes 786440 | tf_op jit(solution)/shard_map/ppermute | solution.py:27
  26.0 36.5 %copy-start.5 = (s32[4096]{0:T(1024)S(1)}, s32[4096]{0:T(1024)}, u32[]{:S(2)}) copy-start(s32[4096]{0:T(1024)} %idx.2) | copy-start | bytes 49156
  55.9 20.6 %collective-permute-start.15 = (bf16[8,512]{1,0:T(8,128)(2,1)}, bf16[8,512]{1,0:T(8,128)(2,1)S(1)}, u32[]{:S(2)}, u32[]{:S(2)}) collective-permute-start(bf16[8,512]{1,0:T(8,128)(2,1)} %get-tuple-element.31), channel_id=1, source_target_pairs={{0,16},{16,32},{32,48},{48,64},{64,80},{80,96},{96,112},{1,17},{17... | collective-permute-start | bytes 24584 | tf_op jit(solution)/shard_map/ppermute | solution.py:512
  61.2 15.3 %collective-permute-start.16 = (bf16[8,512]{1,0:T(8,128)(2,1)}, bf16[8,512]{1,0:T(8,128)(2,1)S(1)}, u32[]{:S(2)}, u32[]{:S(2)}) collective-permute-start(bf16[8,512]{1,0:T(8,128)(2,1)} %get-tuple-element.32), channel_id=1, source_target_pairs={{16,0},{32,16},{48,32},{64,48},{80,64},{96,80},{112,96},{17,1},{33... | collective-permute-start | bytes 24584 | tf_op jit(solution)/shard_map/ppermute | solution.py:513
  64.7 11.9 %copy-start.13 = (f32[2,128]{1,0:T(2,128)S(1)}, f32[2,128]{1,0:T(2,128)}, u32[]{:S(2)}) copy-start(f32[2,128]{1,0:T(2,128)} %get-tuple-element.47) | copy-start | bytes 3076
  64.7 12.0 %copy-start.1 = (bf16[2,512,256]{2,1,0:T(8,128)(2,1)S(1)}, bf16[2,512,256]{2,1,0:T(8,128)(2,1)}, u32[]{:S(2)}) copy-start(bf16[2,512,256]{2,1,0:T(8,128)(2,1)} %get-tuple-element.40.bc_ref) | copy-start | bytes 1572868
  64.7 12.0 %copy-start.2 = (f32[2,512,128]{2,1,0:T(8,128)S(1)}, f32[2,512,128]{2,1,0:T(8,128)}, u32[]{:S(2)}) copy-start(f32[2,512,128]{2,1,0:T(8,128)} %get-tuple-element.42.cum_ref) | copy-start | bytes 1572868
  64.7 12.0 %copy-start.6 = (f32[4,512]{1,0:T(4,128)S(1)}, f32[4,512]{1,0:T(4,128)}, u32[]{:S(2)}) copy-start(f32[4,512]{1,0:T(4,128)} %taps_ref.1) | copy-start | bytes 24580
  64.7 12.0 %copy-start.8 = (bf16[2,512,512]{2,1,0:T(8,128)(2,1)S(1)}, bf16[2,512,512]{2,1,0:T(8,128)(2,1)}, u32[]{:S(2)}) copy-start(bf16[2,512,512]{2,1,0:T(8,128)(2,1)} %get-tuple-element.30.v_ref) | copy-start | bytes 3145732
  64.7 12.0 %copy-start.9 = (f32[2,512,128]{2,1,0:T(8,128)S(1)}, f32[2,512,128]{2,1,0:T(8,128)}, u32[]{:S(2)}) copy-start(f32[2,512,128]{2,1,0:T(8,128)} %get-tuple-element.41.step_ref) | copy-start | bytes 1572868
  79.7 18.2 %copy-start.7 = (f32[4]{0:T(128)S(1)}, f32[4]{0:T(128)}, u32[]{:S(2)}) copy-start(f32[4]{0:T(128)} %param.20) | copy-start | bytes 52
  79.7 18.2 %copy-start.10 = (f32[2,8,512]{2,1,0:T(8,128)S(1)}, f32[2,8,512]{2,1,0:T(8,128)}, u32[]{:S(2)}) copy-start(f32[2,8,512]{2,1,0:T(8,128)} %get-tuple-element.44.st_ref) | copy-start | bytes 98308
  79.7 18.2 %copy-start.11 = (f32[2,8,512]{2,1,0:T(8,128)S(1)}, f32[2,8,512]{2,1,0:T(8,128)}, u32[]{:S(2)}) copy-start(f32[2,8,512]{2,1,0:T(8,128)} %get-tuple-element.45.ct_ref) | copy-start | bytes 98308
  79.9 11.7 %collective-permute-start.19 = (bf16[528,128]{1,0:T(8,128)(2,1)S(1)}, bf16[528,128]{1,0:T(8,128)(2,1)S(1)}, u32[]{:S(2)}, u32[]{:S(2)}) collective-permute-start(bf16[528,128]{1,0:T(8,128)(2,1)S(1)} %get-tuple-element.60), channel_id=1, source_target_pairs={{0,96},{16,112},{32,0},{48,16},{64,32},{80,48},{96,64},{112,80},{1... | collective-permute-start | bytes 405512 | tf_op jit(solution)/shard_map/ppermute | solution.py:535
  85.8 8.0 %collective-permute-start.18 = (bf16[528,128]{1,0:T(8,128)(2,1)S(1)}, bf16[528,128]{1,0:T(8,128)(2,1)S(1)}, u32[]{:S(2)}, u32[]{:S(2)}) collective-permute-start(bf16[528,128]{1,0:T(8,128)(2,1)S(1)} %get-tuple-element.61), channel_id=1, source_target_pairs={{0,64},{16,80},{32,96},{48,112},{64,0},{80,16},{96,32},{112,48},{1... | collective-permute-start | bytes 405512 | tf_op jit(solution)/shard_map/ppermute | solution.py:535
  85.8 9.2 %collective-permute-start.17 = (bf16[528,128]{1,0:T(8,128)(2,1)S(1)}, bf16[528,128]{1,0:T(8,128)(2,1)S(1)}, u32[]{:S(2)}, u32[]{:S(2)}) collective-permute-start(bf16[528,128]{1,0:T(8,128)(2,1)S(1)} %get-tuple-element.62), channel_id=1, source_target_pairs={{0,32},{16,48},{32,64},{48,80},{64,96},{80,112},{96,0},{112,16},{1... | collective-permute-start | bytes 405512 | tf_op jit(solution)/shard_map/ppermute | solution.py:535
  87.1 24.6 %collective-permute-start.22 = (bf16[2048,512]{1,0:T(8,128)(2,1)S(1)}, bf16[2048,512]{1,0:T(8,128)(2,1)S(1)}, u32[]{:S(2)}, u32[]{:S(2)}) collective-permute-start(bf16[2048,512]{1,0:T(8,128)(2,1)S(1)} %get-tuple-element.51), channel_id=1, source_target_pairs={{0,1},{1,0},{2,3},{3,2},{4,5},{5,4},{6,7},{7,6},{8,9},{9,8},{10,11... | collective-permute-start | bytes 6291464 | tf_op jit(solution)/shard_map/ppermute | solution.py:27
  87.1 24.6 %collective-permute-start.23 = (bf16[2048,512]{1,0:T(8,128)(2,1)S(1)}, bf16[2048,512]{1,0:T(8,128)(2,1)S(1)}, u32[]{:S(2)}, u32[]{:S(2)}) collective-permute-start(bf16[2048,512]{1,0:T(8,128)(2,1)S(1)} %get-tuple-element.52), channel_id=1, source_target_pairs={{0,1},{1,0},{2,3},{3,2},{4,5},{5,4},{6,7},{7,6},{8,9},{9,8},{10,11... | collective-permute-start | bytes 6291464 | tf_op jit(solution)/shard_map/ppermute | solution.py:27
  95.5 9.5 %collective-permute-start.20 = (bf16[2,4,128,128]{3,2,1,0:T(8,128)(2,1)S(1)}, bf16[2,4,128,128]{3,2,1,0:T(8,128)(2,1)S(1)}, u32[]{:S(2)}, u32[]{:S(2)}) collective-permute-start(bf16[2,4,128,128]{3,2,1,0:T(8,128)(2,1)S(1)} %pad_maximum_fusion), channel_id=1, source_target_pairs={{0,16},{16,0},{32,48},{48,32},{64,80},{80,64},{96,112},{112,96},{1... | collective-permute-start | bytes 786440 | tf_op jit(solution)/shard_map/ppermute | solution.py:560
  109.0 2.7 %collective-permute-start.21 = (bf16[512,1024]{1,0:T(8,128)(2,1)S(1)}, bf16[512,1024]{1,0:T(8,128)(2,1)S(1)}, u32[]{:S(2)}, u32[]{:S(2)}) collective-permute-start(bf16[512,1024]{1,0:T(8,128)(2,1)S(1)} %finish.1.a), channel_id=1, source_target_pairs={{0,1},{1,0},{2,3},{3,2},{4,5},{5,4},{6,7},{7,6},{8,9},{9,8},{10,11... | collective-permute-start | bytes 3145736 | tf_op jit(solution)/shard_map/ppermute | solution.py:27
  112.5 8.5 %collective-permute-start.25 = (bf16[512,256]{1,0:T(8,128)(2,1)S(1)}, bf16[512,256]{1,0:T(8,128)(2,1)S(1)}, u32[]{:S(2)}, u32[]{:S(2)}) collective-permute-start(bf16[512,256]{1,0:T(8,128)(2,1)S(1)} %bitcast.139), channel_id=1, source_target_pairs={{0,8},{1,9},{2,10},{3,11},{4,12},{5,13},{6,14},{7,15},{8,0},{9,1},... | collective-permute-start | bytes 786440 | tf_op jit(solution)/shard_map/ppermute | solution.py:23
  114.9 11.5 %collective-permute-start.29 = (bf16[512,256]{1,0:T(8,128)(2,1)S(1)}, bf16[512,256]{1,0:T(8,128)(2,1)S(1)}, u32[]{:S(2)}, u32[]{:S(2)}) collective-permute-start(bf16[512,256]{1,0:T(8,128)(2,1)S(1)} %bitcast.136), channel_id=1, source_target_pairs={{0,6},{1,7},{2,0},{3,1},{4,2},{5,3},{6,4},{7,5},{8,14},{9,15},{10,... | collective-permute-start | bytes 786440 | tf_op jit(solution)/shard_map/ppermute | solution.py:23
  118.5 10.8 %collective-permute-start.24 = (bf16[512,256]{1,0:T(8,128)(2,1)S(1)}, bf16[512,256]{1,0:T(8,128)(2,1)S(1)}, u32[]{:S(2)}, u32[]{:S(2)}) collective-permute-start(bf16[512,256]{1,0:T(8,128)(2,1)S(1)} %bitcast.135), channel_id=1, source_target_pairs={{0,8},{1,9},{2,10},{3,11},{4,12},{5,13},{6,14},{7,15},{8,0},{9,1},... | collective-permute-start | bytes 786440 | tf_op jit(solution)/shard_map/ppermute | solution.py:23
  121.7 8.7 %collective-permute-start.26 = (bf16[512,256]{1,0:T(8,128)(2,1)S(1)}, bf16[512,256]{1,0:T(8,128)(2,1)S(1)}, u32[]{:S(2)}, u32[]{:S(2)}) collective-permute-start(bf16[512,256]{1,0:T(8,128)(2,1)S(1)} %bitcast.137), channel_id=1, source_target_pairs={{0,2},{1,3},{2,4},{3,5},{4,6},{5,7},{6,0},{7,1},{8,10},{9,11},{10,... | collective-permute-start | bytes 786440 | tf_op jit(solution)/shard_map/ppermute | solution.py:23
  124.6 7.5 %collective-permute-start.28 = (bf16[512,256]{1,0:T(8,128)(2,1)S(1)}, bf16[512,256]{1,0:T(8,128)(2,1)S(1)}, u32[]{:S(2)}, u32[]{:S(2)}) collective-permute-start(bf16[512,256]{1,0:T(8,128)(2,1)S(1)} %bitcast.133), channel_id=1, source_target_pairs={{0,6},{1,7},{2,0},{3,1},{4,2},{5,3},{6,4},{7,5},{8,14},{9,15},{10,... | collective-permute-start | bytes 786440 | tf_op jit(solution)/shard_map/ppermute | solution.py:23
  127.2 6.7 %collective-permute-start.30 = (bf16[512,256]{1,0:T(8,128)(2,1)S(1)}, bf16[512,256]{1,0:T(8,128)(2,1)S(1)}, u32[]{:S(2)}, u32[]{:S(2)}) collective-permute-start(bf16[512,256]{1,0:T(8,128)(2,1)S(1)} %bitcast.134), channel_id=1, source_target_pairs={{0,8},{1,9},{2,10},{3,11},{4,12},{5,13},{6,14},{7,15},{8,0},{9,1},... | collective-permute-start | bytes 786440 | tf_op jit(solution)/shard_map/ppermute | solution.py:23
  131.2 7.7 %collective-permute-start.27 = (bf16[512,256]{1,0:T(8,128)(2,1)S(1)}, bf16[512,256]{1,0:T(8,128)(2,1)S(1)}, u32[]{:S(2)}, u32[]{:S(2)}) collective-permute-start(bf16[512,256]{1,0:T(8,128)(2,1)S(1)} %bitcast.138), channel_id=1, source_target_pairs={{0,2},{1,3},{2,4},{3,5},{4,6},{5,7},{6,0},{7,1},{8,10},{9,11},{10,... | collective-permute-start | bytes 786440 | tf_op jit(solution)/shard_map/ppermute | solution.py:23
  131.4 7.5 %copy-start.12 = (s32[512,256]{1,0:T(8,128)S(1)}, s32[512,256]{1,0:T(8,128)}, u32[]{:S(2)}) copy-start(s32[512,256]{1,0:T(8,128)} %param.25) | copy-start | bytes 1572868
  (10 other events, 28.0 us)

commit v4 on v3

--- a/solution.py
+++ b/solution.py
@@ -84,24 +84,29 @@
                 part = t[128 * k : 128 * k + 128, pl.ds(at, width)].astype(F32).T
                 by_row[pl.ds(at * tiles + k, width, tiles), :] = part
 
-        def permute(c, _):
-            b0 = c * width
-
-            def body(n, _):
-                for k in range(32):
-                    row = n * 32 + k
-                    src = pl.multiple_of(idx[b0 + row] * tiles, tiles)
-                    dst = pl.multiple_of(row * tiles, tiles)
-                    picked[pl.ds(dst, tiles), :] = by_row[pl.ds(src, tiles), :]
+        def permute(weight, out, first):
+            def body(i, _):
+                cols = pl.ds(pl.multiple_of(i * 256, 256), 256)
+                out[0, :, cols] = dot(t[...], weight[:, cols]).astype(BF)
+                for c in range(4):
+                    b0 = pl.multiple_of((first + i * 4 + c) * width, width)
+                    base = c * width * tiles
+                    for row in range(width):
+                        src = pl.multiple_of(idx[b0 + row] * tiles, tiles)
+                        picked[base + row * tiles : base + (row + 1) * tiles, :] = by_row[
+                            pl.ds(src, tiles), :
+                        ]
+                    for k in range(tiles):
+                        part = picked[pl.ds(base + k, width, tiles), :].T
+                        tp[128 * k : 128 * k + 128, pl.ds(b0, width)] = part.astype(BF)
                 return 0
 
-            lax.fori_loop(0, width // 32, body, 0)
-            for k in range(tiles):
-                part = picked[pl.ds(k, width, tiles), :].T
-                tp[128 * k : 128 * k + 128, pl.ds(pl.multiple_of(b0, width), width)] = part.astype(BF)
-            return 0
-
-        lax.fori_loop(0, d // width, permute, 0)
+            lax.fori_loop(0, 2, body, 0)
+
+        weight_copies[1].wait()
+        permute(wv, v_out, 0)
+        weight_copies[2].wait()
+        permute(wg, g_out, 8)
         weight_copies[0].wait()
         r = lax.broadcasted_iota(jnp.int32, (rows, rows), 0)
         q = lax.broadcasted_iota(jnp.int32, (rows, rows), 1)
@@ -125,19 +130,18 @@
             decay = jnp.exp(cum[rows - 1 : rows] if b == 0 else cum[0:1])
             decay_o[b : b + 1] = decay
             decays += [decay, decay - decay.astype(BF).astype(F32)]
-        weight_copies[1].wait()
         row8 = lax.broadcasted_iota(jnp.int32, (8, inner), 0)
         for b, u in enumerate((t, tp)):
-            v = dot(u[...], wv[...])
-            v_out[b] = v.astype(BF)
-            message = pltpu.roll(v[rows - 8 :], 3, 0) if b == 0 else v[:8]
+            if b == 1:
+                v_out[1] = dot(tp[...], wv[...]).astype(BF)
+            edge = v_out[b, rows - 16 :] if b == 0 else v_out[b, :16]
+            edge = edge.astype(F32)
+            message = pltpu.roll(edge[8:], 3, 0) if b == 0 else edge[:8]
             for i, part in enumerate(decays):
                 wide = jnp.concatenate([part, jnp.zeros((1, inner - 128), F32)], axis=1)
                 message = jnp.where(row8 == 3 + i, wide, message)
             (down_o if b == 0 else up_o)[...] = message.astype(BF)
-        weight_copies[2].wait()
-        for b, u in enumerate((t, tp)):
-            g_out[b] = dot(u[...], wg[...]).astype(BF)
+        g_out[1] = dot(tp[...], wg[...]).astype(BF)
 
     shapes = [
         jax.ShapeDtypeStruct((2, rows, inner), BF),
@@ -164,7 +168,7 @@
                 pltpu.VMEM((rows, d), BF),
                 pltpu.VMEM((rows, d), BF),
                 pltpu.VMEM((d * tiles, 128), F32),
-                pltpu.VMEM((width * tiles, 128), F32),
+                pltpu.VMEM((4 * width * tiles, 128), F32),
                 pltpu.VMEM((d, inner), BF),
                 pltpu.VMEM((d, inner), BF),
                 pltpu.VMEM((d, ns + 128), BF),

time: 140 us -> 136 us (0.971)
  Pallas kernels: 59.9 us -> 55.8 us
    pallas_call x1, Pallas kernels: 29.9 us -> 26 us  [project(): pl.pallas_call(kernel, grid_spec=pltpu.PrefetchScalarGridSpec(num_scalar_...]
where the time goes in v4:
time: 136 us
  Pallas kernels  55.8 us (41%)
  starting transfers between devices  40.5 us (30%)
  waiting for transfers between devices  33.9 us (25%)
  local copies, waits for them, and re-layouts  3.09 us (2%)
  other arithmetic  1.95 us (1%)
    pallas_call x1, Pallas kernels, project(): pl.pallas_call(kernel, grid_spec=pltpu.PrefetchScalarGridSpec(num_scalar_...  26 us
    ppermute x14, starting transfers between devices, to_chip(): return lax.ppermute(a, 'chan', chip_route(dy, dx))  22.8 us
    ppermute x14, waiting for transfers between devices, to_chip(): return lax.ppermute(a, 'chan', chip_route(dy, dx))  21.7 us
    pallas_call x1, Pallas kernels, output_table(): pl.pallas_call(kernel, grid_spec=pltpu.PrefetchScalarGridSpec(num_scalar_...  11.6 us
    ppermute x3, waiting for transfers between devices, shards(): got.append(lax.ppermute(jnp.where(z + k < 4, msg_f, msg_b), 'seq', route))  7.34 us
    ppermute x3, starting transfers between devices, shards(): got.append(lax.ppermute(jnp.where(z + k < 4, msg_f, msg_b), 'seq', route))  7.22 us
    pallas_call x8, Pallas kernels, output_stage(): pl.pallas_call(kernel, grid_spec=pltpu.PrefetchScalarGridSpec(num_scalar_...  5.98 us
    pallas_call x1, Pallas kernels, within_shard(): pl.pallas_call(kernel, grid=(2, heads), in_specs=[head, by(rows, 256), by...  5.85 us
  transfers between devices with their start and end apart: 31, of which 15 were waited for; matrix products, arithmetic and copies ran while one was open for 1% of the time, Pallas kernels for 19%

profile of v4, /device:TPU:0, one launch (start us, length us, event | category | flops | bytes accessed | tf_op | source)
XLA Modules:
  0.0 135.8 jit_solution(14498228765008118232)
XLA Ops:
  0.0 1.6 %collective-permute-start.1 = (bf16[512,256]{1,0:T(8,128)(2,1)}, bf16[512,256]{1,0:T(8,128)(2,1)S(1)}, u32[]{:S(2)}, u32[]{:S(2)}) collective-permute-start(bf16[512,256]{1,0:T(8,128)(2,1)} %refs_0_.1), channel_id=1, source_target_pairs={{0,2},{1,3},{2,4},{3,5},{4,6},{5,7},{6,0},{7,1},{8,10},{9,11},{10,... | collective-permute-start | bytes 786440 | tf_op jit(solution)/shard_map/ppermute | solution.py:23
  1.6 1.7 %collective-permute-start.3 = (bf16[512,256]{1,0:T(8,128)(2,1)}, bf16[512,256]{1,0:T(8,128)(2,1)S(1)}, u32[]{:S(2)}, u32[]{:S(2)}) collective-permute-start(bf16[512,256]{1,0:T(8,128)(2,1)} %refs_0_.1), channel_id=1, source_target_pairs={{0,6},{1,7},{2,0},{3,1},{4,2},{5,3},{6,4},{7,5},{8,14},{9,15},{10,... | collective-permute-start | bytes 786440 | tf_op jit(solution)/shard_map/ppermute | solution.py:23
  3.2 1.7 %collective-permute-start.5 = (bf16[512,256]{1,0:T(8,128)(2,1)}, bf16[512,256]{1,0:T(8,128)(2,1)S(1)}, u32[]{:S(2)}, u32[]{:S(2)}) collective-permute-start(bf16[512,256]{1,0:T(8,128)(2,1)} %refs_0_.1), channel_id=1, source_target_pairs={{0,8},{1,9},{2,10},{3,11},{4,12},{5,13},{6,14},{7,15},{8,0},{9,1},... | collective-permute-start | bytes 786440 | tf_op jit(solution)/shard_map/ppermute | solution.py:23
  4.9 4.5 %collective-permute-done.1.refs_2_ = bf16[512,256]{1,0:T(8,128)(2,1)S(1)} collective-permute-done((bf16[512,256]{1,0:T(8,128)(2,1)}, bf16[512,256]{1,0:T(8,128)(2,1)S(1)}, u32[]{:S(2)}, u32[]{:S(2)}) %collective-permute-start.1) | collective-permute-done | bytes 262176 | tf_op jit(solution)/shard_map/ppermute | solution.py:23
  9.8 1.7 %collective-permute-start.7 = (bf16[512,256]{1,0:T(8,128)(2,1)S(1)}, bf16[512,256]{1,0:T(8,128)(2,1)S(1)}, u32[]{:S(2)}, u32[]{:S(2)}) collective-permute-start(bf16[512,256]{1,0:T(8,128)(2,1)S(1)} %collective-permute-done.1.refs_2_), channel_id=1, source_target_pairs={{0,8},{1,9},{2,10},{3,11},{4,12},{5,13},{6,14},{7,15},{8,0},{9,1},... | collective-permute-start | bytes 786440 | tf_op jit(solution)/shard_map/ppermute | solution.py:23
  12.2 2.5 %collective-permute-start.9 = (bf16[512,256]{1,0:T(8,128)(2,1)S(1)}, bf16[512,256]{1,0:T(8,128)(2,1)S(1)}, u32[]{:S(2)}, u32[]{:S(2)}) collective-permute-start(bf16[512,256]{1,0:T(8,128)(2,1)S(1)} %collective-permute-done.5.refs_6_), channel_id=1, source_target_pairs={{0,6},{1,7},{2,0},{3,1},{4,2},{5,3},{6,4},{7,5},{8,14},{9,15},{10,... | collective-permute-start | bytes 786440 | tf_op jit(solution)/shard_map/ppermute | solution.py:23
  14.6 3.0 %collective-permute-done.11.refs_12_ = bf16[512,256]{1,0:T(8,128)(2,1)S(1)} collective-permute-done((bf16[512,256]{1,0:T(8,128)(2,1)S(1)}, bf16[512,256]{1,0:T(8,128)(2,1)S(1)}, u32[]{:S(2)}, u32[]{:S(2)}) %collective-permute-start.11) | collective-permute-done | bytes 262176 | tf_op jit(solution)/shard_map/ppermute | solution.py:23
  17.6 1.9 %collective-permute-start.13 = (bf16[512,256]{1,0:T(8,128)(2,1)S(1)}, bf16[512,256]{1,0:T(8,128)(2,1)S(1)}, u32[]{:S(2)}, u32[]{:S(2)}) collective-permute-start(bf16[512,256]{1,0:T(8,128)(2,1)S(1)} %collective-permute-done.11.refs_12_), channel_id=1, source_target_pairs={{0,8},{1,9},{2,10},{3,11},{4,12},{5,13},{6,14},{7,15},{8,0},{9,1},... | collective-permute-start | bytes 786440 | tf_op jit(solution)/shard_map/ppermute | solution.py:23
  20.1 0.6 collective-permute-done.9.refs_10_
  20.7 3.5 %collective-permute-done.13.refs_14_ = bf16[512,256]{1,0:T(8,128)(2,1)S(1)} collective-permute-done((bf16[512,256]{1,0:T(8,128)(2,1)S(1)}, bf16[512,256]{1,0:T(8,128)(2,1)S(1)}, u32[]{:S(2)}, u32[]{:S(2)}) %collective-permute-start.13) | collective-permute-done | bytes 262176 | tf_op jit(solution)/shard_map/ppermute | solution.py:23
  24.2 0.7 stack.139.place_ref
  24.9 0.9 collective-permute-done.14.refs_15_
  26.0 26.0 %project.1 = (bf16[2,512,512]{2,1,0:T(8,128)(2,1)}, bf16[2,512,512]{2,1,0:T(8,128)(2,1)}, bf16[2,512,256]{2,1,0:T(8,128)(2,1)}, f32[2,512,128]{2,1,0:T(8,128)}, ...) custom-call(s32[16]{0:T(128)} %stack.139.place_ref, ...), custom_call_target="tpu_custom_call" | custom-call | flops 12884901888 | bytes 20971520 | tf_op jit(solution)/shard_map/project/pallas_call | solution.py:160
  52.0 5.2 %collective-permute-start.15 = (bf16[8,512]{1,0:T(8,128)(2,1)}, bf16[8,512]{1,0:T(8,128)(2,1)S(1)}, u32[]{:S(2)}, u32[]{:S(2)}) collective-permute-start(bf16[8,512]{1,0:T(8,128)(2,1)} %get-tuple-element.31), channel_id=1, source_target_pairs={{0,16},{16,32},{32,48},{48,64},{64,80},{80,96},{96,112},{1,17},{17... | collective-permute-start | bytes 24584 | tf_op jit(solution)/shard_map/ppermute | solution.py:516
  57.3 1.5 %collective-permute-start.16 = (bf16[8,512]{1,0:T(8,128)(2,1)}, bf16[8,512]{1,0:T(8,128)(2,1)S(1)}, u32[]{:S(2)}, u32[]{:S(2)}) collective-permute-start(bf16[8,512]{1,0:T(8,128)(2,1)} %get-tuple-element.32), channel_id=1, source_target_pairs={{16,0},{32,16},{48,32},{64,48},{80,64},{96,80},{112,96},{17,1},{33... | collective-permute-start | bytes 24584 | tf_op jit(solution)/shard_map/ppermute | solution.py:517
  58.8 2.2 %copy-done.4 = bf16[512,4096]{1,0:T(8,128)(2,1)S(1)} copy-done((bf16[512,4096]{1,0:T(8,128)(2,1)S(1)}, bf16[512,4096]{1,0:T(8,128)(2,1)}, u32[]{:S(2)}) %copy-start.4) | copy-done | bytes 4194328
  61.0 11.6 %output_table.1 = (bf16[2048,512]{1,0:T(8,128)(2,1)S(1)}, bf16[2048,512]{1,0:T(8,128)(2,1)S(1)}, bf16[2048,512]{1,0:T(8,128)(2,1)S(1)}, bf16[2048,512]{1,0:T(8,128)(2,1)S(1)}) custom-call(s32[4096]{0:T(1024)S(1)} %copy-done.5, s32[1]{0:T(128)} %bitcast.20.core_ref, bf16[512,4096]{1,0:T(8,128)(2,1)S(1)} %copy-done.4), custom_call_target="tpu_custom_call" | custom-call | flops 8000000000 | bytes 12582912 | tf_op jit(solution)/shard_map/output_table/pallas_call | solution.py:380
  72.9 2.9 %conv_states.1 = (bf16[2,512,512]{2,1,0:T(8,128)(2,1)S(1)}, f32[2,4,128,128]{3,2,1,0:T(8,128)S(1)}) custom-call(bf16[2,512,512]{2,1,0:T(8,128)(2,1)S(1)} %copy-done.8, bf16[8,512]{1,0:T(8,128)(2,1)S(1)} %collective-permute-done.15.below_ref, bf16[8,512]{1,0:T(8,128)(2,1)S(1)} %collective-permute-done.16.above_ref, f32[4,512]{1,0:T(4,128)S(1)} %copy-done.6, ...), custom_call_target="tpu_custom_call" | custom-call | flops 1000000000 | bytes 3145728 | tf_op jit(solution)/shard_map/conv_states/pallas_call | solution.py:216
  76.0 5.9 %collective-permute-start.19 = (bf16[528,128]{1,0:T(8,128)(2,1)S(1)}, bf16[528,128]{1,0:T(8,128)(2,1)S(1)}, u32[]{:S(2)}, u32[]{:S(2)}) collective-permute-start(bf16[528,128]{1,0:T(8,128)(2,1)S(1)} %get-tuple-element.60), channel_id=1, source_target_pairs={{0,96},{16,112},{32,0},{48,16},{64,32},{80,48},{96,64},{112,80},{1... | collective-permute-start | bytes 405512 | tf_op jit(solution)/shard_map/ppermute | solution.py:539
  81.9 1.3 collective-permute-start.17
  83.2 0.5 collective-permute-start.23
  83.7 4.0 %collective-permute-done.19 = bf16[528,128]{1,0:T(8,128)(2,1)S(1)} collective-permute-done((bf16[528,128]{1,0:T(8,128)(2,1)S(1)}, bf16[528,128]{1,0:T(8,128)(2,1)S(1)}, u32[]{:S(2)}, u32[]{:S(2)}) %collective-permute-start.19) | collective-permute-done | bytes 135200 | tf_op jit(solution)/shard_map/ppermute | solution.py:539
  87.7 2.2 %collective-permute-done.18 = bf16[528,128]{1,0:T(8,128)(2,1)S(1)} collective-permute-done((bf16[528,128]{1,0:T(8,128)(2,1)S(1)}, bf16[528,128]{1,0:T(8,128)(2,1)S(1)}, u32[]{:S(2)}, u32[]{:S(2)}) %collective-permute-start.18) | collective-permute-done | bytes 135200 | tf_op jit(solution)/shard_map/ppermute | solution.py:539
  89.9 1.2 collective-permute-done.17
  91.6 2.4 %collective-permute-start.20 = (bf16[2,4,128,128]{3,2,1,0:T(8,128)(2,1)S(1)}, bf16[2,4,128,128]{3,2,1,0:T(8,128)(2,1)S(1)}, u32[]{:S(2)}, u32[]{:S(2)}) collective-permute-start(bf16[2,4,128,128]{3,2,1,0:T(8,128)(2,1)S(1)} %pad_maximum_fusion), channel_id=1, source_target_pairs={{0,16},{16,0},{32,48},{48,32},{64,80},{80,64},{96,112},{112,96},{1... | collective-permute-start | bytes 786440 | tf_op jit(solution)/shard_map/ppermute | solution.py:564
  94.0 5.9 %within_shard.1.y_ref = f32[2,512,512]{2,1,0:T(8,128)S(1)} custom-call(bf16[2,512,512]{2,1,0:T(8,128)(2,1)S(1)} %get-tuple-element.43.x_ref, bf16[2,512,256]{2,1,0:T(8,128)(2,1)S(1)} %copy-done.1, f32[2,8,512]{2,1,0:T(8,128)S(1)} %copy-done.10, f32[2,8,512]{2,1,0:T(8,128)S(1)} %copy-done.11, f32[2,512,128]{2,1,0:T(8,128)S(1)} %copy-done.2, f32[1,4]{1,0:T(1,128)S(1)} %bitcast.141), custom_call_target="tpu_custom_call" | custom-call | flops 4000000000 | bytes 4194304 | tf_op jit(solution)/shard_map/within_shard/pallas_call | solution.py:284
  99.9 1.2 collective-permute-done.20
  101.6 3.5 %finish.1.a = bf16[512,1024]{1,0:T(8,128)(2,1)S(1)} custom-call(f32[2,512,512]{2,1,0:T(8,128)S(1)} %within_shard.1.y_ref, bf16[2,4,128,128]{3,2,1,0:T(8,128)(2,1)S(1)} %pad_maximum_fusion.1.s_ref, bf16[2,512,256]{2,1,0:T(8,128)(2,1)S(1)} %copy-done.1, f32[2,512,128]{2,1,0:T(8,128)S(1)} %copy-done.2, bf16[2,512,512]{2,1,0:T(8,128)(2,1)S(1)} %copy-done, ...), custom_call_target="tpu_custom_call" | custom-call | flops 1000000000 | bytes 5242880 | tf_op jit(solution)/shard_map/finish/pallas_call | solution.py:320
  105.2 2.6 %collective-permute-done.21.b = bf16[512,1024]{1,0:T(8,128)(2,1)S(1)} collective-permute-done((bf16[512,1024]{1,0:T(8,128)(2,1)S(1)}, bf16[512,1024]{1,0:T(8,128)(2,1)S(1)}, u32[]{:S(2)}, u32[]{:S(2)}) %collective-permute-start.21) | collective-permute-done | bytes 1048608 | tf_op jit(solution)/shard_map/ppermute | solution.py:27
  107.8 0.7 output_stage.10
  108.6 1.7 %collective-permute-start.25 = (bf16[512,256]{1,0:T(8,128)(2,1)S(1)}, bf16[512,256]{1,0:T(8,128)(2,1)S(1)}, u32[]{:S(2)}, u32[]{:S(2)}) collective-permute-start(bf16[512,256]{1,0:T(8,128)(2,1)S(1)} %bitcast.139), channel_id=1, source_target_pairs={{0,8},{1,9},{2,10},{3,11},{4,12},{5,13},{6,14},{7,15},{8,0},{9,1},... | collective-permute-start | bytes 786440 | tf_op jit(solution)/shard_map/ppermute | solution.py:23
  110.2 0.7 output_stage.14
  111.0 2.9 %collective-permute-start.29 = (bf16[512,256]{1,0:T(8,128)(2,1)S(1)}, bf16[512,256]{1,0:T(8,128)(2,1)S(1)}, u32[]{:S(2)}, u32[]{:S(2)}) collective-permute-start(bf16[512,256]{1,0:T(8,128)(2,1)S(1)} %bitcast.136), channel_id=1, source_target_pairs={{0,6},{1,7},{2,0},{3,1},{4,2},{5,3},{6,4},{7,5},{8,14},{9,15},{10,... | collective-permute-start | bytes 786440 | tf_op jit(solution)/shard_map/ppermute | solution.py:23
  113.9 0.7 output_stage.9
  114.6 0.5 collective-permute-start.24
  115.2 1.9 %collective-permute-done.25.rest_0_ = bf16[512,256]{1,0:T(8,128)(2,1)S(1)} collective-permute-done((bf16[512,256]{1,0:T(8,128)(2,1)S(1)}, bf16[512,256]{1,0:T(8,128)(2,1)S(1)}, u32[]{:S(2)}, u32[]{:S(2)}) %collective-permute-start.25) | collective-permute-done | bytes 262176 | tf_op jit(solution)/shard_map/ppermute | solution.py:23
  117.0 0.7 output_stage.11
  117.8 2.2 %collective-permute-start.26 = (bf16[512,256]{1,0:T(8,128)(2,1)S(1)}, bf16[512,256]{1,0:T(8,128)(2,1)S(1)}, u32[]{:S(2)}, u32[]{:S(2)}) collective-permute-start(bf16[512,256]{1,0:T(8,128)(2,1)S(1)} %bitcast.137), channel_id=1, source_target_pairs={{0,2},{1,3},{2,4},{3,5},{4,6},{5,7},{6,0},{7,1},{8,10},{9,11},{10,... | collective-permute-start | bytes 786440 | tf_op jit(solution)/shard_map/ppermute | solution.py:23
  120.0 0.8 output_stage.13
  120.8 1.8 %collective-permute-start.28 = (bf16[512,256]{1,0:T(8,128)(2,1)S(1)}, bf16[512,256]{1,0:T(8,128)(2,1)S(1)}, u32[]{:S(2)}, u32[]{:S(2)}) collective-permute-start(bf16[512,256]{1,0:T(8,128)(2,1)S(1)} %bitcast.133), channel_id=1, source_target_pairs={{0,6},{1,7},{2,0},{3,1},{4,2},{5,3},{6,4},{7,5},{8,14},{9,15},{10,... | collective-permute-start | bytes 786440 | tf_op jit(solution)/shard_map/ppermute | solution.py:23
  122.6 0.7 output_stage.15
  123.3 2.0 %collective-permute-start.30 = (bf16[512,256]{1,0:T(8,128)(2,1)S(1)}, bf16[512,256]{1,0:T(8,128)(2,1)S(1)}, u32[]{:S(2)}, u32[]{:S(2)}) collective-permute-start(bf16[512,256]{1,0:T(8,128)(2,1)S(1)} %bitcast.134), channel_id=1, source_target_pairs={{0,8},{1,9},{2,10},{3,11},{4,12},{5,13},{6,14},{7,15},{8,0},{9,1},... | collective-permute-start | bytes 786440 | tf_op jit(solution)/shard_map/ppermute | solution.py:23
  125.4 1.2 collective-permute-done.26.rest_1_
  126.6 0.7 output_stage.12
  127.6 0.7 output_stage.8
  128.3 1.6 %collective-permute-done.30 = bf16[512,256]{1,0:T(8,128)(2,1)S(1)} collective-permute-done((bf16[512,256]{1,0:T(8,128)(2,1)S(1)}, bf16[512,256]{1,0:T(8,128)(2,1)S(1)}, u32[]{:S(2)}, u32[]{:S(2)}) %collective-permute-start.30) | collective-permute-done | bytes 262176 | tf_op jit(solution)/shard_map/ppermute | solution.py:23
  129.9 5.0 %collective-permute-done.27 = bf16[512,256]{1,0:T(8,128)(2,1)S(1)} collective-permute-done((bf16[512,256]{1,0:T(8,128)(2,1)S(1)}, bf16[512,256]{1,0:T(8,128)(2,1)S(1)}, u32[]{:S(2)}, u32[]{:S(2)}) %collective-permute-start.27) | collective-permute-done | bytes 262176 | tf_op jit(solution)/shard_map/ppermute | solution.py:23
  135.0 0.9 fusion.4
  (116 shorter events, 3.4 us)
Async XLA Ops:
  0.0 9.4 %collective-permute-start.1 = (bf16[512,256]{1,0:T(8,128)(2,1)}, bf16[512,256]{1,0:T(8,128)(2,1)S(1)}, u32[]{:S(2)}, u32[]{:S(2)}) collective-permute-start(bf16[512,256]{1,0:T(8,128)(2,1)} %refs_0_.1), channel_id=1, source_target_pairs={{0,2},{1,3},{2,4},{3,5},{4,6},{5,7},{6,0},{7,1},{8,10},{9,11},{10,... | collective-permute-start | bytes 786440 | tf_op jit(solution)/shard_map/ppermute | solution.py:23
  1.6 8.3 %collective-permute-start.3 = (bf16[512,256]{1,0:T(8,128)(2,1)}, bf16[512,256]{1,0:T(8,128)(2,1)S(1)}, u32[]{:S(2)}, u32[]{:S(2)}) collective-permute-start(bf16[512,256]{1,0:T(8,128)(2,1)} %refs_0_.1), channel_id=1, source_target_pairs={{0,6},{1,7},{2,0},{3,1},{4,2},{5,3},{6,4},{7,5},{8,14},{9,15},{10,... | collective-permute-start | bytes 786440 | tf_op jit(solution)/shard_map/ppermute | solution.py:23
  3.2 8.3 %collective-permute-start = (bf16[512,256]{1,0:T(8,128)(2,1)}, bf16[512,256]{1,0:T(8,128)(2,1)S(1)}, u32[]{:S(2)}, u32[]{:S(2)}) collective-permute-start(bf16[512,256]{1,0:T(8,128)(2,1)} %refs_0_.1), channel_id=1, source_target_pairs={{0,1},{1,0},{2,3},{3,2},{4,5},{5,4},{6,7},{7,6},{8,9},{9,8},{10,11... | collective-permute-start | bytes 786440 | tf_op jit(solution)/shard_map/ppermute | solution.py:27
  3.2 8.9 %collective-permute-start.5 = (bf16[512,256]{1,0:T(8,128)(2,1)}, bf16[512,256]{1,0:T(8,128)(2,1)S(1)}, u32[]{:S(2)}, u32[]{:S(2)}) collective-permute-start(bf16[512,256]{1,0:T(8,128)(2,1)} %refs_0_.1), channel_id=1, source_target_pairs={{0,8},{1,9},{2,10},{3,11},{4,12},{5,13},{6,14},{7,15},{8,0},{9,1},... | collective-permute-start | bytes 786440 | tf_op jit(solution)/shard_map/ppermute | solution.py:23
  9.4 16.5 %copy-start.14 = (bf16[512,256]{1,0:T(8,128)(2,1)}, bf16[512,256]{1,0:T(8,128)(2,1)S(1)}, u32[]{:S(2)}) copy-start(bf16[512,256]{1,0:T(8,128)(2,1)S(1)} %collective-permute-done.1.refs_2_) | copy-start | bytes 786436
  9.4 8.3 %collective-permute-start.11 = (bf16[512,256]{1,0:T(8,128)(2,1)S(1)}, bf16[512,256]{1,0:T(8,128)(2,1)S(1)}, u32[]{:S(2)}, u32[]{:S(2)}) collective-permute-start(bf16[512,256]{1,0:T(8,128)(2,1)S(1)} %collective-permute-done.1.refs_2_), channel_id=1, source_target_pairs={{0,2},{1,3},{2,4},{3,5},{4,6},{5,7},{6,0},{7,1},{8,10},{9,11},{10,... | collective-permute-start | bytes 786440 | tf_op jit(solution)/shard_map/ppermute | solution.py:23
  9.8 16.0 %copy-start.15 = (bf16[512,256]{1,0:T(8,128)(2,1)}, bf16[512,256]{1,0:T(8,128)(2,1)S(1)}, u32[]{:S(2)}) copy-start(bf16[512,256]{1,0:T(8,128)(2,1)S(1)} %collective-permute-done.3.refs_4_) | copy-start | bytes 786436
  9.8 9.7 %collective-permute-start.4 = (bf16[512,256]{1,0:T(8,128)(2,1)S(1)}, bf16[512,256]{1,0:T(8,128)(2,1)S(1)}, u32[]{:S(2)}, u32[]{:S(2)}) collective-permute-start(bf16[512,256]{1,0:T(8,128)(2,1)S(1)} %collective-permute-done.3.refs_4_), channel_id=1, source_target_pairs={{0,1},{1,0},{2,3},{3,2},{4,5},{5,4},{6,7},{7,6},{8,9},{9,8},{10,11... | collective-permute-start | bytes 786440 | tf_op jit(solution)/shard_map/ppermute | solution.py:27
  9.8 9.7 %collective-permute-start.7 = (bf16[512,256]{1,0:T(8,128)(2,1)S(1)}, bf16[512,256]{1,0:T(8,128)(2,1)S(1)}, u32[]{:S(2)}, u32[]{:S(2)}) collective-permute-start(bf16[512,256]{1,0:T(8,128)(2,1)S(1)} %collective-permute-done.1.refs_2_), channel_id=1, source_target_pairs={{0,8},{1,9},{2,10},{3,11},{4,12},{5,13},{6,14},{7,15},{8,0},{9,1},... | collective-permute-start | bytes 786440 | tf_op jit(solution)/shard_map/ppermute | solution.py:23
  11.5 14.4 %copy-start.16 = (bf16[512,256]{1,0:T(8,128)(2,1)}, bf16[512,256]{1,0:T(8,128)(2,1)S(1)}, u32[]{:S(2)}) copy-start(bf16[512,256]{1,0:T(8,128)(2,1)S(1)} %collective-permute-done.refs_1_) | copy-start | bytes 786436
  11.5 8.5 %collective-permute-start.2 = (bf16[512,256]{1,0:T(8,128)(2,1)S(1)}, bf16[512,256]{1,0:T(8,128)(2,1)S(1)}, u32[]{:S(2)}, u32[]{:S(2)}) collective-permute-start(bf16[512,256]{1,0:T(8,128)(2,1)S(1)} %collective-permute-done.1.refs_2_), channel_id=1, source_target_pairs={{0,1},{1,0},{2,3},{3,2},{4,5},{5,4},{6,7},{7,6},{8,9},{9,8},{10,11... | collective-permute-start | bytes 786440 | tf_op jit(solution)/shard_map/ppermute | solution.py:27
  12.2 13.7 %copy-start.17 = (bf16[512,256]{1,0:T(8,128)(2,1)}, bf16[512,256]{1,0:T(8,128)(2,1)S(1)}, u32[]{:S(2)}) copy-start(bf16[512,256]{1,0:T(8,128)(2,1)S(1)} %collective-permute-done.5.refs_6_) | copy-start | bytes 786436
  12.2 8.5 %collective-permute-start.9 = (bf16[512,256]{1,0:T(8,128)(2,1)S(1)}, bf16[512,256]{1,0:T(8,128)(2,1)S(1)}, u32[]{:S(2)}, u32[]{:S(2)}) collective-permute-start(bf16[512,256]{1,0:T(8,128)(2,1)S(1)} %collective-permute-done.5.refs_6_), channel_id=1, source_target_pairs={{0,6},{1,7},{2,0},{3,1},{4,2},{5,3},{6,4},{7,5},{8,14},{9,15},{10,... | collective-permute-start | bytes 786440 | tf_op jit(solution)/shard_map/ppermute | solution.py:23
  17.6 8.3 %copy-start.18 = (bf16[512,256]{1,0:T(8,128)(2,1)}, bf16[512,256]{1,0:T(8,128)(2,1)S(1)}, u32[]{:S(2)}) copy-start(bf16[512,256]{1,0:T(8,128)(2,1)S(1)} %collective-permute-done.11.refs_12_) | copy-start | bytes 786436
  17.6 6.6 %collective-permute-start.13 = (bf16[512,256]{1,0:T(8,128)(2,1)S(1)}, bf16[512,256]{1,0:T(8,128)(2,1)S(1)}, u32[]{:S(2)}, u32[]{:S(2)}) collective-permute-start(bf16[512,256]{1,0:T(8,128)(2,1)S(1)} %collective-permute-done.11.refs_12_), channel_id=1, source_target_pairs={{0,8},{1,9},{2,10},{3,11},{4,12},{5,13},{6,14},{7,15},{8,0},{9,1},... | collective-permute-start | bytes 786440 | tf_op jit(solution)/shard_map/ppermute | solution.py:23
  19.5 6.4 %copy-start.19 = (bf16[512,256]{1,0:T(8,128)(2,1)}, bf16[512,256]{1,0:T(8,128)(2,1)S(1)}, u32[]{:S(2)}) copy-start(bf16[512,256]{1,0:T(8,128)(2,1)S(1)} %collective-permute-done.4.refs_5_) | copy-start | bytes 786436
  19.5 5.4 %collective-permute-start.6 = (bf16[512,256]{1,0:T(8,128)(2,1)S(1)}, bf16[512,256]{1,0:T(8,128)(2,1)S(1)}, u32[]{:S(2)}, u32[]{:S(2)}) collective-permute-start(bf16[512,256]{1,0:T(8,128)(2,1)S(1)} %collective-permute-done.5.refs_6_), channel_id=1, source_target_pairs={{0,1},{1,0},{2,3},{3,2},{4,5},{5,4},{6,7},{7,6},{8,9},{9,8},{10,11... | collective-permute-start | bytes 786440 | tf_op jit(solution)/shard_map/ppermute | solution.py:27
  19.5 5.3 %collective-permute-start.12 = (bf16[512,256]{1,0:T(8,128)(2,1)S(1)}, bf16[512,256]{1,0:T(8,128)(2,1)S(1)}, u32[]{:S(2)}, u32[]{:S(2)}) collective-permute-start(bf16[512,256]{1,0:T(8,128)(2,1)S(1)} %collective-permute-done.11.refs_12_), channel_id=1, source_target_pairs={{0,1},{1,0},{2,3},{3,2},{4,5},{5,4},{6,7},{7,6},{8,9},{9,8},{10,11... | collective-permute-start | bytes 786440 | tf_op jit(solution)/shard_map/ppermute | solution.py:27
  20.0 4.9 %collective-permute-start.8 = (bf16[512,256]{1,0:T(8,128)(2,1)S(1)}, bf16[512,256]{1,0:T(8,128)(2,1)S(1)}, u32[]{:S(2)}, u32[]{:S(2)}) collective-permute-start(bf16[512,256]{1,0:T(8,128)(2,1)S(1)} %collective-permute-done.7.refs_8_), channel_id=1, source_target_pairs={{0,1},{1,0},{2,3},{3,2},{4,5},{5,4},{6,7},{7,6},{8,9},{9,8},{10,11... | collective-permute-start | bytes 786440 | tf_op jit(solution)/shard_map/ppermute | solution.py:27
  20.7 4.2 %collective-permute-start.10 = (bf16[512,256]{1,0:T(8,128)(2,1)S(1)}, bf16[512,256]{1,0:T(8,128)(2,1)}, u32[]{:S(2)}, u32[]{:S(2)}) collective-permute-start(bf16[512,256]{1,0:T(8,128)(2,1)S(1)} %collective-permute-done.9.refs_10_), channel_id=1, source_target_pairs={{0,1},{1,0},{2,3},{3,2},{4,5},{5,4},{6,7},{7,6},{8,9},{9,8},{10,11... | collective-permute-start | bytes 786440 | tf_op jit(solution)/shard_map/ppermute | solution.py:27
  24.2 1.7 %collective-permute-start.14 = (bf16[512,256]{1,0:T(8,128)(2,1)S(1)}, bf16[512,256]{1,0:T(8,128)(2,1)}, u32[]{:S(2)}, u32[]{:S(2)}) collective-permute-start(bf16[512,256]{1,0:T(8,128)(2,1)S(1)} %collective-permute-done.13.refs_14_), channel_id=1, source_target_pairs={{0,1},{1,0},{2,3},{3,2},{4,5},{5,4},{6,7},{7,6},{8,9},{9,8},{10,11... | collective-permute-start | bytes 786440 | tf_op jit(solution)/shard_map/ppermute | solution.py:27
  26.0 32.8 %copy-start.5 = (s32[4096]{0:T(1024)S(1)}, s32[4096]{0:T(1024)}, u32[]{:S(2)}) copy-start(s32[4096]{0:T(1024)} %idx.2) | copy-start | bytes 49156
  52.0 20.6 %collective-permute-start.15 = (bf16[8,512]{1,0:T(8,128)(2,1)}, bf16[8,512]{1,0:T(8,128)(2,1)S(1)}, u32[]{:S(2)}, u32[]{:S(2)}) collective-permute-start(bf16[8,512]{1,0:T(8,128)(2,1)} %get-tuple-element.31), channel_id=1, source_target_pairs={{0,16},{16,32},{32,48},{48,64},{64,80},{80,96},{96,112},{1,17},{17... | collective-permute-start | bytes 24584 | tf_op jit(solution)/shard_map/ppermute | solution.py:516
  57.3 15.3 %collective-permute-start.16 = (bf16[8,512]{1,0:T(8,128)(2,1)}, bf16[8,512]{1,0:T(8,128)(2,1)S(1)}, u32[]{:S(2)}, u32[]{:S(2)}) collective-permute-start(bf16[8,512]{1,0:T(8,128)(2,1)} %get-tuple-element.32), channel_id=1, source_target_pairs={{16,0},{32,16},{48,32},{64,48},{80,64},{96,80},{112,96},{17,1},{33... | collective-permute-start | bytes 24584 | tf_op jit(solution)/shard_map/ppermute | solution.py:517
  61.0 11.6 %copy-start.13 = (f32[2,128]{1,0:T(2,128)S(1)}, f32[2,128]{1,0:T(2,128)}, u32[]{:S(2)}) copy-start(f32[2,128]{1,0:T(2,128)} %get-tuple-element.47) | copy-start | bytes 3076
  61.0 11.8 %copy-start.1 = (bf16[2,512,256]{2,1,0:T(8,128)(2,1)S(1)}, bf16[2,512,256]{2,1,0:T(8,128)(2,1)}, u32[]{:S(2)}) copy-start(bf16[2,512,256]{2,1,0:T(8,128)(2,1)} %get-tuple-element.40.bc_ref) | copy-start | bytes 1572868
  61.0 11.8 %copy-start.2 = (f32[2,512,128]{2,1,0:T(8,128)S(1)}, f32[2,512,128]{2,1,0:T(8,128)}, u32[]{:S(2)}) copy-start(f32[2,512,128]{2,1,0:T(8,128)} %get-tuple-element.42.cum_ref) | copy-start | bytes 1572868
  61.0 11.8 %copy-start.6 = (f32[4,512]{1,0:T(4,128)S(1)}, f32[4,512]{1,0:T(4,128)}, u32[]{:S(2)}) copy-start(f32[4,512]{1,0:T(4,128)} %taps_ref.1) | copy-start | bytes 24580
  61.0 11.8 %copy-start.8 = (bf16[2,512,512]{2,1,0:T(8,128)(2,1)S(1)}, bf16[2,512,512]{2,1,0:T(8,128)(2,1)}, u32[]{:S(2)}) copy-start(bf16[2,512,512]{2,1,0:T(8,128)(2,1)} %get-tuple-element.30.v_ref) | copy-start | bytes 3145732
  61.0 11.8 %copy-start.9 = (f32[2,512,128]{2,1,0:T(8,128)S(1)}, f32[2,512,128]{2,1,0:T(8,128)}, u32[]{:S(2)}) copy-start(f32[2,512,128]{2,1,0:T(8,128)} %get-tuple-element.41.step_ref) | copy-start | bytes 1572868
  75.8 18.2 %copy-start.7 = (f32[4]{0:T(128)S(1)}, f32[4]{0:T(128)}, u32[]{:S(2)}) copy-start(f32[4]{0:T(128)} %param.20) | copy-start | bytes 52
  75.8 18.2 %copy-start.10 = (f32[2,8,512]{2,1,0:T(8,128)S(1)}, f32[2,8,512]{2,1,0:T(8,128)}, u32[]{:S(2)}) copy-start(f32[2,8,512]{2,1,0:T(8,128)} %get-tuple-element.44.st_ref) | copy-start | bytes 98308
  75.8 18.2 %copy-start.11 = (f32[2,8,512]{2,1,0:T(8,128)S(1)}, f32[2,8,512]{2,1,0:T(8,128)}, u32[]{:S(2)}) copy-start(f32[2,8,512]{2,1,0:T(8,128)} %get-tuple-element.45.ct_ref) | copy-start | bytes 98308
  76.0 11.7 %collective-permute-start.19 = (bf16[528,128]{1,0:T(8,128)(2,1)S(1)}, bf16[528,128]{1,0:T(8,128)(2,1)S(1)}, u32[]{:S(2)}, u32[]{:S(2)}) collective-permute-start(bf16[528,128]{1,0:T(8,128)(2,1)S(1)} %get-tuple-element.60), channel_id=1, source_target_pairs={{0,96},{16,112},{32,0},{48,16},{64,32},{80,48},{96,64},{112,80},{1... | collective-permute-start | bytes 405512 | tf_op jit(solution)/shard_map/ppermute | solution.py:539
  81.9 8.0 %collective-permute-start.18 = (bf16[528,128]{1,0:T(8,128)(2,1)S(1)}, bf16[528,128]{1,0:T(8,128)(2,1)S(1)}, u32[]{:S(2)}, u32[]{:S(2)}) collective-permute-start(bf16[528,128]{1,0:T(8,128)(2,1)S(1)} %get-tuple-element.61), channel_id=1, source_target_pairs={{0,64},{16,80},{32,96},{48,112},{64,0},{80,16},{96,32},{112,48},{1... | collective-permute-start | bytes 405512 | tf_op jit(solution)/shard_map/ppermute | solution.py:539
  81.9 9.2 %collective-permute-start.17 = (bf16[528,128]{1,0:T(8,128)(2,1)S(1)}, bf16[528,128]{1,0:T(8,128)(2,1)S(1)}, u32[]{:S(2)}, u32[]{:S(2)}) collective-permute-start(bf16[528,128]{1,0:T(8,128)(2,1)S(1)} %get-tuple-element.62), channel_id=1, source_target_pairs={{0,32},{16,48},{32,64},{48,80},{64,96},{80,112},{96,0},{112,16},{1... | collective-permute-start | bytes 405512 | tf_op jit(solution)/shard_map/ppermute | solution.py:539
  83.2 24.6 %collective-permute-start.22 = (bf16[2048,512]{1,0:T(8,128)(2,1)S(1)}, bf16[2048,512]{1,0:T(8,128)(2,1)S(1)}, u32[]{:S(2)}, u32[]{:S(2)}) collective-permute-start(bf16[2048,512]{1,0:T(8,128)(2,1)S(1)} %get-tuple-element.51), channel_id=1, source_target_pairs={{0,1},{1,0},{2,3},{3,2},{4,5},{5,4},{6,7},{7,6},{8,9},{9,8},{10,11... | collective-permute-start | bytes 6291464 | tf_op jit(solution)/shard_map/ppermute | solution.py:27
  83.2 24.6 %collective-permute-start.23 = (bf16[2048,512]{1,0:T(8,128)(2,1)S(1)}, bf16[2048,512]{1,0:T(8,128)(2,1)S(1)}, u32[]{:S(2)}, u32[]{:S(2)}) collective-permute-start(bf16[2048,512]{1,0:T(8,128)(2,1)S(1)} %get-tuple-element.52), channel_id=1, source_target_pairs={{0,1},{1,0},{2,3},{3,2},{4,5},{5,4},{6,7},{7,6},{8,9},{9,8},{10,11... | collective-permute-start | bytes 6291464 | tf_op jit(solution)/shard_map/ppermute | solution.py:27
  91.6 9.5 %collective-permute-start.20 = (bf16[2,4,128,128]{3,2,1,0:T(8,128)(2,1)S(1)}, bf16[2,4,128,128]{3,2,1,0:T(8,128)(2,1)S(1)}, u32[]{:S(2)}, u32[]{:S(2)}) collective-permute-start(bf16[2,4,128,128]{3,2,1,0:T(8,128)(2,1)S(1)} %pad_maximum_fusion), channel_id=1, source_target_pairs={{0,16},{16,0},{32,48},{48,32},{64,80},{80,64},{96,112},{112,96},{1... | collective-permute-start | bytes 786440 | tf_op jit(solution)/shard_map/ppermute | solution.py:564
  105.1 2.7 %collective-permute-start.21 = (bf16[512,1024]{1,0:T(8,128)(2,1)S(1)}, bf16[512,1024]{1,0:T(8,128)(2,1)S(1)}, u32[]{:S(2)}, u32[]{:S(2)}) collective-permute-start(bf16[512,1024]{1,0:T(8,128)(2,1)S(1)} %finish.1.a), channel_id=1, source_target_pairs={{0,1},{1,0},{2,3},{3,2},{4,5},{5,4},{6,7},{7,6},{8,9},{9,8},{10,11... | collective-permute-start | bytes 3145736 | tf_op jit(solution)/shard_map/ppermute | solution.py:27
  108.6 8.5 %collective-permute-start.25 = (bf16[512,256]{1,0:T(8,128)(2,1)S(1)}, bf16[512,256]{1,0:T(8,128)(2,1)S(1)}, u32[]{:S(2)}, u32[]{:S(2)}) collective-permute-start(bf16[512,256]{1,0:T(8,128)(2,1)S(1)} %bitcast.139), channel_id=1, source_target_pairs={{0,8},{1,9},{2,10},{3,11},{4,12},{5,13},{6,14},{7,15},{8,0},{9,1},... | collective-permute-start | bytes 786440 | tf_op jit(solution)/shard_map/ppermute | solution.py:23
  111.0 11.6 %collective-permute-start.29 = (bf16[512,256]{1,0:T(8,128)(2,1)S(1)}, bf16[512,256]{1,0:T(8,128)(2,1)S(1)}, u32[]{:S(2)}, u32[]{:S(2)}) collective-permute-start(bf16[512,256]{1,0:T(8,128)(2,1)S(1)} %bitcast.136), channel_id=1, source_target_pairs={{0,6},{1,7},{2,0},{3,1},{4,2},{5,3},{6,4},{7,5},{8,14},{9,15},{10,... | collective-permute-start | bytes 786440 | tf_op jit(solution)/shard_map/ppermute | solution.py:23
  114.6 10.7 %collective-permute-start.24 = (bf16[512,256]{1,0:T(8,128)(2,1)S(1)}, bf16[512,256]{1,0:T(8,128)(2,1)S(1)}, u32[]{:S(2)}, u32[]{:S(2)}) collective-permute-start(bf16[512,256]{1,0:T(8,128)(2,1)S(1)} %bitcast.135), channel_id=1, source_target_pairs={{0,8},{1,9},{2,10},{3,11},{4,12},{5,13},{6,14},{7,15},{8,0},{9,1},... | collective-permute-start | bytes 786440 | tf_op jit(solution)/shard_map/ppermute | solution.py:23
  117.8 8.8 %collective-permute-start.26 = (bf16[512,256]{1,0:T(8,128)(2,1)S(1)}, bf16[512,256]{1,0:T(8,128)(2,1)S(1)}, u32[]{:S(2)}, u32[]{:S(2)}) collective-permute-start(bf16[512,256]{1,0:T(8,128)(2,1)S(1)} %bitcast.137), channel_id=1, source_target_pairs={{0,2},{1,3},{2,4},{3,5},{4,6},{5,7},{6,0},{7,1},{8,10},{9,11},{10,... | collective-permute-start | bytes 786440 | tf_op jit(solution)/shard_map/ppermute | solution.py:23
  120.8 7.6 %collective-permute-start.28 = (bf16[512,256]{1,0:T(8,128)(2,1)S(1)}, bf16[512,256]{1,0:T(8,128)(2,1)S(1)}, u32[]{:S(2)}, u32[]{:S(2)}) collective-permute-start(bf16[512,256]{1,0:T(8,128)(2,1)S(1)} %bitcast.133), channel_id=1, source_target_pairs={{0,6},{1,7},{2,0},{3,1},{4,2},{5,3},{6,4},{7,5},{8,14},{9,15},{10,... | collective-permute-start | bytes 786440 | tf_op jit(solution)/shard_map/ppermute | solution.py:23
  123.3 6.6 %collective-permute-start.30 = (bf16[512,256]{1,0:T(8,128)(2,1)S(1)}, bf16[512,256]{1,0:T(8,128)(2,1)S(1)}, u32[]{:S(2)}, u32[]{:S(2)}) collective-permute-start(bf16[512,256]{1,0:T(8,128)(2,1)S(1)} %bitcast.134), channel_id=1, source_target_pairs={{0,8},{1,9},{2,10},{3,11},{4,12},{5,13},{6,14},{7,15},{8,0},{9,1},... | collective-permute-start | bytes 786440 | tf_op jit(solution)/shard_map/ppermute | solution.py:23
  127.3 7.7 %collective-permute-start.27 = (bf16[512,256]{1,0:T(8,128)(2,1)S(1)}, bf16[512,256]{1,0:T(8,128)(2,1)S(1)}, u32[]{:S(2)}, u32[]{:S(2)}) collective-permute-start(bf16[512,256]{1,0:T(8,128)(2,1)S(1)} %bitcast.138), channel_id=1, source_target_pairs={{0,2},{1,3},{2,4},{3,5},{4,6},{5,7},{6,0},{7,1},{8,10},{9,11},{10,... | collective-permute-start | bytes 786440 | tf_op jit(solution)/shard_map/ppermute | solution.py:23
  127.5 7.4 %copy-start.12 = (s32[512,256]{1,0:T(8,128)S(1)}, s32[512,256]{1,0:T(8,128)}, u32[]{:S(2)}) copy-start(s32[512,256]{1,0:T(8,128)} %param.25) | copy-start | bytes 1572868
  (10 other events, 28.0 us)
